TPU v7x, 32 devices: a whole 2x2x4 slice. The times are simulated.
32 devices in a mesh: ctx: 16 (over z, y, x), fsdp: 2 (over core).
Axes of the slice: x: 2, y: 2, z: 4, core: 2. Of those that a mesh axis runs over, the one named last changes fastest.
Arguments:
- inputs: bfloat16 [2, 2048, 1024], P('fsdp', 'ctx'), may hold values from -48 to 48
- cotangent: bfloat16 [2, 2048, 1024], P('fsdp', 'ctx'), may hold values from -6 to 6
- doc_lengths: int32 [2, 8], P('fsdp'), may hold values from 1 to 1024, 2048 in all within a row
- qkv_weight: bfloat16 [1024, 3072], P('fsdp'), may hold values from -0.1875 to 0.1875
- out_weight: bfloat16 [1024, 1024], P('fsdp'), may hold values from -0.1875 to 0.1875
- fc1_weight: bfloat16 [1024, 4096], P('fsdp'), may hold values from -0.1875 to 0.1875
- fc2_weight: bfloat16 [4096, 1024], P('fsdp'), may hold values from -0.09375 to 0.09375
- norm_gain: bfloat16 [3, 1024], P(None, 'fsdp'), may hold values from 0.099609375 to 1.8984375
- norm_bias: bfloat16 [3, 1024], P(None, 'fsdp'), may hold values from -1.5 to 1.5
- mid_gain: bfloat16 [4096], P('fsdp'), may hold values from 0.099609375 to 1.8984375
- mid_bias: bfloat16 [4096], P('fsdp'), may hold values from -1.5 to 1.5
- head_scale: bfloat16 [16], P('fsdp'), may hold values from 0.5 to 2
Outputs:
- output: bfloat16 [2, 2048, 1024], P('fsdp', 'ctx')
- input_grad: bfloat16 [2, 2048, 1024], P('fsdp', 'ctx')
- qkv_grad: float32 [1024, 3072], P('fsdp')
- out_grad: float32 [1024, 1024], P('fsdp')
- fc1_grad: float32 [1024, 4096], P('fsdp')
- fc2_grad: float32 [4096, 1024], P('fsdp')
- gain_grad: float32 [3, 1024], P(None, 'fsdp')
- bias_grad: float32 [3, 1024], P(None, 'fsdp')
- mid_gain_grad: float32 [4096], P('fsdp')
- mid_bias_grad: float32 [4096], P('fsdp')
- scale_grad: float32 [16], P('fsdp')
- rms_values: float32 [3], replicated
Inputs may be any that keep to these rules, and one draw needn't show every extreme that they name: `doc_lengths`: each row holds 8 document lengths that sum to 2048; the longest is 1024.
All inputs are finite; a program needn't handle non-finite values.
Results may differ from a plain program's by a relative error of at most 0.022.
Values may be sent and summed in bfloat16 or wider, within the bound.
No kernel may reach another device: no remote copies, remote signals or barrier semaphores. Data moves between devices by JAX's collectives and lax.ppermute only.
A program may use at most 320 MiB of HBM per device.

v0:
```python
from functools import partial
import math

import jax
import jax.numpy as jnp
from jax import lax
from jax.sharding import PartitionSpec as P

HEADS = 16
HEAD_DIM = 64


epsilon = 1e-05
masked_value = -1e30


def stored_positions(first_row, n_rows, half_rows, groups):
    offsets = first_row + jnp.arange(n_rows, dtype=jnp.int32)
    halves = offsets // half_rows
    paired = halves // 2
    placed = jnp.where(halves % 2 == 0, paired, 2 * groups - 1 - paired)
    return placed * half_rows + offsets % half_rows


def doc_floor(positions, starts):
    begun_mask = starts[None, :] <= positions[:, None]
    return jnp.max(jnp.where(begun_mask, starts[None, :], 0), axis=1)


def allowed_mask(query_pos, query_floor, key_pos):
    return (key_pos[None, :] <= query_pos[:, None]) & (key_pos[None, :] >= query_floor[:, None])


def normalize(values):
    centered = values - jnp.mean(values, axis=-1, keepdims=True)
    inverse = lax.rsqrt(jnp.mean(centered * centered, axis=-1, keepdims=True) + epsilon)
    return (centered * inverse, inverse)


def norm_backward(grad_out, normed, inverse, gain_vec):
    grad_normed = grad_out * gain_vec
    grad_in = inverse * (
        grad_normed
        - jnp.mean(grad_normed, axis=-1, keepdims=True)
        - normed * jnp.mean(grad_normed * normed, axis=-1, keepdims=True)
    )
    return (grad_in, jnp.sum(grad_out * normed, axis=0), jnp.sum(grad_out, axis=0))


def split_heads(rows_array, model_width):
    n_rows = rows_array.shape[0]
    return (
        rows_array[:, :model_width].reshape(n_rows, HEADS, HEAD_DIM),
        rows_array[:, model_width:].reshape(n_rows, HEADS, HEAD_DIM),
    )


def block_grads(query_heads, dout_heads, log_total, delta_rows, key_heads, value_heads, allowed):
    scores = jnp.einsum(
        "qhe,khe->qhk", query_heads, key_heads, preferred_element_type=jnp.float32
    ) * HEAD_DIM ** (-0.5)
    p_block = jnp.where(allowed[:, None, :], jnp.exp(scores - log_total[:, :, None]), 0.0)
    grad_probs = jnp.einsum(
        "qhe,khe->qhk", dout_heads, value_heads, preferred_element_type=jnp.float32
    )
    grad_scores = (p_block * (grad_probs - delta_rows[:, :, None])).astype(jnp.bfloat16)
    return (grad_scores, p_block.astype(jnp.bfloat16))


def local(
    inputs,
    cotangent,
    doc_lengths,
    qkv_weight,
    out_weight,
    fc1_weight,
    fc2_weight,
    norm_gain,
    norm_bias,
    mid_gain,
    mid_bias,
    head_scale,
):
    groups = lax.axis_size("ctx")
    member = lax.axis_index("ctx")
    x_local = inputs[0].astype(jnp.float32)
    tok_rows, model_width = x_local.shape
    half_rows = tok_rows // 2
    stream_rows = tok_rows * groups
    score_scale = HEAD_DIM ** (-0.5)
    (
        qkv_full,
        out_full,
        fc1_full,
        fc2_full,
        gain_full,
        bias_full,
        mid_gain_full,
        mid_bias_full,
        scale_full,
    ) = (
        lax.all_gather(qkv_weight, "fsdp", axis=0, tiled=True),
        lax.all_gather(out_weight, "fsdp", axis=0, tiled=True),
        lax.all_gather(fc1_weight, "fsdp", axis=0, tiled=True),
        lax.all_gather(fc2_weight, "fsdp", axis=0, tiled=True),
        lax.all_gather(norm_gain, "fsdp", axis=1, tiled=True),
        lax.all_gather(norm_bias, "fsdp", axis=1, tiled=True),
        lax.all_gather(mid_gain, "fsdp", axis=0, tiled=True),
        lax.all_gather(mid_bias, "fsdp", axis=0, tiled=True),
        lax.all_gather(head_scale, "fsdp", axis=0, tiled=True),
    )
    norm_gains = gain_full.astype(jnp.float32)
    norm_biases = bias_full.astype(jnp.float32)
    mid_gains = mid_gain_full.astype(jnp.float32)
    mid_biases = mid_bias_full.astype(jnp.float32)
    head_scales = scale_full.astype(jnp.float32)
    lengths_row = doc_lengths[0]
    starts = jnp.cumsum(lengths_row) - lengths_row
    my_pos = stored_positions(member * tok_rows, tok_rows, half_rows, groups)
    my_floor = doc_floor(my_pos, starts)
    norm_one, inv_one = normalize(x_local)
    normed_one = (norm_one * norm_gains[0] + norm_biases[0]).astype(jnp.bfloat16)
    project = jnp.dot(normed_one, qkv_full, preferred_element_type=jnp.float32).astype(jnp.bfloat16)
    queries = project[:, :model_width].reshape(tok_rows, HEADS, HEAD_DIM)
    keys_values = project[:, model_width:]
    start_state = (
        jnp.zeros((tok_rows, HEADS, HEAD_DIM), jnp.float32),
        jnp.full((tok_rows, HEADS), masked_value, jnp.float32),
        jnp.zeros((tok_rows, HEADS), jnp.float32),
    )
    running = start_state
    fetched = lax.all_gather(keys_values, "ctx", axis=0, tiled=True)
    n_rows = fetched.shape[0]
    sub_rows = math.gcd(n_rows, 1024)
    fetched_blocks = fetched.reshape(n_rows // sub_rows, sub_rows, 2 * model_width)
    block_firsts = sub_rows * jnp.arange(n_rows // sub_rows, dtype=jnp.int32)

    def attend_block(state_now, scanned):
        out_sum, row_max, row_sum = state_now
        key_block, block_first = scanned
        key_heads, value_heads = split_heads(key_block, model_width)
        key_pos = stored_positions(block_first, sub_rows, half_rows, groups)
        usable = allowed_mask(my_pos, my_floor, key_pos)[:, None, :]
        scores = (
            jnp.einsum("qhe,khe->qhk", queries, key_heads, preferred_element_type=jnp.float32)
            * score_scale
        )
        new_max = jnp.maximum(row_max, jnp.max(jnp.where(usable, scores, masked_value), axis=-1))
        p_block = jnp.where(usable, jnp.exp(scores - new_max[:, :, None]), 0.0)
        rescale = jnp.exp(row_max - new_max)
        row_sum = row_sum * rescale + jnp.sum(p_block, axis=-1)
        out_sum = out_sum * rescale[:, :, None] + jnp.einsum(
            "qhk,khe->qhe",
            p_block.astype(jnp.bfloat16),
            value_heads,
            preferred_element_type=jnp.float32,
        )
        return ((out_sum, new_max, row_sum), None)

    running, unused_out = lax.scan(attend_block, running, (fetched_blocks, block_firsts))
    out_sum, row_max, row_sum = running
    attended = out_sum / row_sum[:, :, None]
    log_total = row_max + jnp.log(row_sum)
    scaled = (
        (attended * head_scales[None, :, None]).reshape(tok_rows, model_width).astype(jnp.bfloat16)
    )
    branch = jnp.dot(scaled, out_full, preferred_element_type=jnp.float32)
    norm_att, inv_att = normalize(branch)
    attn_out = norm_att * norm_gains[1] + norm_biases[1]
    middle = x_local + attn_out
    norm_two, inv_two = normalize(middle)
    normed_two = (norm_two * norm_gains[2] + norm_biases[2]).astype(jnp.bfloat16)
    hidden = jnp.dot(normed_two, fc1_full, preferred_element_type=jnp.float32)
    active, gelu_back = jax.vjp(partial(jax.nn.gelu, approximate=True), hidden)
    norm_mid, inv_mid = normalize(active)
    mixed_in = (norm_mid * mid_gains + mid_biases).astype(jnp.bfloat16)
    ffn_out = jnp.dot(mixed_in, fc2_full, preferred_element_type=jnp.float32)
    result = middle + ffn_out
    sq_sums = lax.psum(
        jnp.stack(
            [jnp.sum(result * result), jnp.sum(attn_out * attn_out), jnp.sum(ffn_out * ffn_out)]
        ),
        ("ctx", "fsdp"),
    )
    rms_values = jnp.sqrt(sq_sums / (stream_rows * lax.axis_size("fsdp") * model_width))
    grad_top = cotangent[0].astype(jnp.float32)
    grad_ffn = cotangent[0]
    fc2_grad = jnp.einsum("tf,td->fd", mixed_in, grad_ffn, preferred_element_type=jnp.float32)
    grad_mixed = jnp.einsum("td,fd->tf", grad_ffn, fc2_full, preferred_element_type=jnp.float32)
    grad_active, mid_gain_grad, mid_bias_grad = norm_backward(
        grad_mixed, norm_mid, inv_mid, mid_gains
    )
    grad_hidden = gelu_back(grad_active)[0].astype(jnp.bfloat16)
    fc1_grad = jnp.einsum("td,tf->df", normed_two, grad_hidden, preferred_element_type=jnp.float32)
    grad_two = jnp.einsum("tf,df->td", grad_hidden, fc1_full, preferred_element_type=jnp.float32)
    grad_mid_in, gain_two, bias_two = norm_backward(grad_two, norm_two, inv_two, norm_gains[2])
    grad_middle = grad_top + grad_mid_in
    grad_branch_f, gain_att, bias_att = norm_backward(grad_middle, norm_att, inv_att, norm_gains[1])
    grad_branch = grad_branch_f.astype(jnp.bfloat16)
    out_grad = jnp.einsum("ta,tb->ab", scaled, grad_branch, preferred_element_type=jnp.float32)
    grad_scaled = jnp.einsum(
        "tb,ab->ta", grad_branch, out_full, preferred_element_type=jnp.float32
    ).reshape(tok_rows, HEADS, HEAD_DIM)
    scale_grad = jnp.sum(grad_scaled * attended, axis=(0, 2))
    grad_att = (grad_scaled * head_scales[None, :, None]).astype(jnp.bfloat16)
    delta_rows = jnp.sum(grad_att.astype(jnp.float32) * attended, axis=-1)
    query_start = jnp.zeros((tok_rows, HEADS, HEAD_DIM), jnp.float32)
    every_kv = lax.all_gather(keys_values, "ctx", axis=0, tiled=True)
    running = query_start
    n_rows = every_kv.shape[0]
    query_sub_rows = math.gcd(n_rows, 1024)
    fetched_blocks = every_kv.reshape(n_rows // query_sub_rows, query_sub_rows, 2 * model_width)
    block_firsts = 0 + query_sub_rows * jnp.arange(n_rows // query_sub_rows, dtype=jnp.int32)

    def query_block(partial_sum, scanned):
        key_block, block_first = scanned
        key_heads, value_heads = split_heads(key_block, model_width)
        key_pos = stored_positions(block_first, query_sub_rows, half_rows, groups)
        allowed = allowed_mask(my_pos, my_floor, key_pos)
        grad_scores, unused_low = block_grads(
            queries, grad_att, log_total, delta_rows, key_heads, value_heads, allowed
        )
        return (
            partial_sum
            + jnp.einsum(
                "qhk,khe->qhe", grad_scores, key_heads, preferred_element_type=jnp.float32
            ),
            None,
        )

    running, unused_out = lax.scan(query_block, running, (fetched_blocks, block_firsts))
    n_rows = tok_rows * lax.axis_size("ctx")
    key_sub_rows = math.gcd(n_rows, 1024)

    def key_term(sub_first):
        key_block = lax.dynamic_slice_in_dim(every_kv, sub_first, key_sub_rows, 0)
        key_heads, value_heads = split_heads(key_block, model_width)
        key_pos = stored_positions(sub_first, key_sub_rows, half_rows, groups)
        allowed = allowed_mask(my_pos, my_floor, key_pos)
        grad_scores, low_probs = block_grads(
            queries, grad_att, log_total, delta_rows, key_heads, value_heads, allowed
        )
        grad_keys = (
            jnp.einsum("qhk,qhe->khe", grad_scores, queries, preferred_element_type=jnp.float32)
            * score_scale
        )
        grad_values = jnp.einsum(
            "qhk,qhe->khe", low_probs, grad_att, preferred_element_type=jnp.float32
        )
        return jnp.concatenate(
            [
                grad_keys.reshape(key_sub_rows, model_width),
                grad_values.reshape(key_sub_rows, model_width),
            ],
            axis=1,
        )

    sub_firsts = key_sub_rows * jnp.arange(n_rows // key_sub_rows, dtype=jnp.int32)
    kv_grad = lax.psum_scatter(
        lax.map(key_term, sub_firsts).reshape(n_rows, 2 * model_width),
        "ctx",
        scatter_dimension=0,
        tiled=True,
    )
    grad_queries = (running * score_scale).reshape(tok_rows, model_width)
    grad_project = jnp.concatenate([grad_queries, kv_grad], axis=1).astype(jnp.bfloat16)
    qkv_grad = jnp.einsum("td,tp->dp", normed_one, grad_project, preferred_element_type=jnp.float32)
    grad_one = jnp.einsum("tp,dp->td", grad_project, qkv_full, preferred_element_type=jnp.float32)
    grad_first, gain_one, bias_one = norm_backward(grad_one, norm_one, inv_one, norm_gains[0])
    input_grad = (grad_middle + grad_first).astype(jnp.bfloat16)[None]
    gain_grad = jnp.stack([gain_one, gain_att, gain_two])
    bias_grad = jnp.stack([bias_one, bias_att, bias_two])
    shard_grads = (
        lax.psum_scatter(
            qkv_grad.astype(jnp.bfloat16), "fsdp", scatter_dimension=0, tiled=True
        ).astype(jnp.float32),
        lax.psum_scatter(
            out_grad.astype(jnp.bfloat16), "fsdp", scatter_dimension=0, tiled=True
        ).astype(jnp.float32),
        lax.psum_scatter(
            fc1_grad.astype(jnp.bfloat16), "fsdp", scatter_dimension=0, tiled=True
        ).astype(jnp.float32),
        lax.psum_scatter(
            fc2_grad.astype(jnp.bfloat16), "fsdp", scatter_dimension=0, tiled=True
        ).astype(jnp.float32),
        lax.psum_scatter(
            gain_grad.astype(jnp.bfloat16), "fsdp", scatter_dimension=1, tiled=True
        ).astype(jnp.float32),
        lax.psum_scatter(
            bias_grad.astype(jnp.bfloat16), "fsdp", scatter_dimension=1, tiled=True
        ).astype(jnp.float32),
        lax.psum_scatter(
            mid_gain_grad.astype(jnp.bfloat16), "fsdp", scatter_dimension=0, tiled=True
        ).astype(jnp.float32),
        lax.psum_scatter(
            mid_bias_grad.astype(jnp.bfloat16), "fsdp", scatter_dimension=0, tiled=True
        ).astype(jnp.float32),
        lax.psum_scatter(
            scale_grad.astype(jnp.bfloat16), "fsdp", scatter_dimension=0, tiled=True
        ).astype(jnp.float32),
    )
    summed = lax.psum(
        (
            shard_grads[0],
            shard_grads[1],
            shard_grads[2],
            shard_grads[3],
            shard_grads[4],
            shard_grads[5],
            shard_grads[6],
            shard_grads[7],
            shard_grads[8],
        ),
        "ctx",
    )
    return (
        result.astype(jnp.bfloat16)[None],
        input_grad,
        summed[0],
        summed[1],
        summed[2],
        summed[3],
        summed[4],
        summed[5],
        summed[6],
        summed[7],
        summed[8],
        rms_values,
    )


def solution(mesh):
    placed = (
        P("fsdp", "ctx", None),
        P("fsdp", "ctx", None),
        P("fsdp", None),
        P("fsdp", None),
        P("fsdp", None),
        P("fsdp", None),
        P("fsdp", None),
        P(None, "fsdp"),
        P(None, "fsdp"),
        P("fsdp"),
        P("fsdp"),
        P("fsdp"),
    )
    return jax.shard_map(
        local,
        mesh=mesh,
        in_specs=placed,
        out_specs=(
            P("fsdp", "ctx", None),
            P("fsdp", "ctx", None),
            P("fsdp", None),
            P("fsdp", None),
            P("fsdp", None),
            P("fsdp", None),
            P(None, "fsdp"),
            P(None, "fsdp"),
            P("fsdp"),
            P("fsdp"),
            P("fsdp"),
            P(),
        ),
        check_vma=False,
    )
```

profile of v0, /device:TPU:12, one launch (start us, length us, event | category | flops | bytes accessed | tf_op | source)
XLA Modules:
  0.0 1841.5 jit_solution(4212419879417016194)
XLA Ops:
  12.1 15.6 all-gather.6.cloned.1.call-done
  43.2 101.8 %all-gather.8.cloned.1.call-done = bf16[2048,2048]{1,0:T(8,128)(2,1)} async-done(((bf16[128,2048]{1,0:T(8,128)(2,1)}), bf16[2048,2048]{1,0:T(8,128)(2,1)}) %all-gather.8.cloned.1.call-update) | async-done | bytes 8388624 | tf_op jit(solution)/shard_map/all_gather | solution.py:132
  144.9 12.1 copy.75
  157.1 41.7 %while.47 = (s32[]{:T(128)}, f32[128,16,64]{0,2,1:T(8,128)S(1)}, f32[128,16]{0,1:T(8,128)S(1)}, f32[128,16]{0,1:T(8,128)S(1)}, s32[2]{0:T(128)S(1)}, /*index=5*/...) while((s32[]{:T(128)}, f32[128,16,64]{0,2,1:T(8,128)S(1)}, ...), condition=%wide.region_7.8_spmd.clone, body=%wide.region_4.7_spmd.clone.sunk | while | flops 560786944 | bytes 81667752 | solution.py:160
  161.6 5.9 fusion.228
  167.5 6.7 fusion.229
  183.0 5.3 fusion.228
  188.3 6.6 fusion.229
  203.3 5.5 fusion.131
  210.0 6.7 multiply_reduce_fusion
  218.8 6.7 fusion.143
  232.5 116.8 %while.46 = (s32[]{:T(128)}, f32[2,1024,2048]{2,1,0:T(8,128)}, s32[2]{0:T(128)S(1)}, s32[128]{0:T(128)S(1)}, bf16[2048,2048]{1,0:T(8,128)(2,1)}, /*index=5*/bf16...) while((s32[]{:T(128)}, f32[2,1024,2048]{2,1,0:T(8,128)}, ...), condition=%wide.region_24.25_spmd.clone, body=%wide.region_23.24_spmd.clone.sunk | while | flops 1098302976 | bytes 123111664 | solution.py:260
  244.9 6.3 fusion.217
  254.7 10.0 broadcast_multiply_fusion.14
  264.7 5.4 fusion.220
  274.3 9.1 copy.129
  283.4 7.7 constant_dynamic-update-slice_fusion.2
  303.1 6.3 fusion.217
  312.9 10.0 broadcast_multiply_fusion.14
  322.9 5.4 fusion.220
  332.5 9.1 copy.129
  341.6 7.7 constant_dynamic-update-slice_fusion.2
  352.7 5.9 convolution_convert_fusion.1
  360.2 6.2 convolution_convert_fusion
  366.4 36.4 %while.48 = (s32[]{:T(128)}, f32[128,16,64]{0,2,1:T(8,128)S(1)}, bf16[2,1024,2048]{1,2,0:T(8,128)(2,1)}, s32[2]{0:T(128)S(1)}, s32[128]{0:T(128)S(1)}, /*index=5...) while((s32[]{:T(128)}, f32[128,16,64]{0,2,1:T(8,128)S(1)}, ...), condition=%wide.region_22.23_spmd.clone, body=%wide.region_21.22_spmd.clone.sunk | while | flops 818595328 | bytes 41707156 | solution.py:231
  376.9 7.7 fusion.242
  395.2 7.7 fusion.242
  403.2 295.5 %reduce-scatter.12.cloned.1.call-done = f32[128,2048]{1,0:T(8,128)} async-done(((f32[2048,2048]{1,0:T(8,128)}), f32[128,2048]{1,0:T(8,128)}) %reduce-scatter.12.cloned.1.call-update) | async-done | bytes 1048592 | tf_op jit(solution)/shard_map/reduce_scatter | solution.py:259
  715.3 41.5 %psum.79 = f32[3]{0:T(128)S(1)} all-reduce(f32[3]{0:T(128)S(1)} %pad_maximum_fusion.5), channel_id=1, replica_groups=mesh['ctx'=16,'fsdp'=2] {'ctx','fsdp'}, use_global_device_ids=true, to_apply=%region_58.59 | all-reduce | flops 3 | bytes 24 | tf_op jit(solution)/shard_map/psum | solution.py:179
  766.2 10.7 reduce-scatter.22.cloned.1.call-done
  777.9 17.8 reduce-scatter.14.cloned.1.call-done
  795.7 1038.7 %all-reduce.7 = (f32[512,3072]{1,0:T(8,128)}, f32[512,1024]{1,0:T(8,128)}, f32[512,4096]{1,0:T(8,128)}, f32[2048,1024]{1,0:T(8,128)}, f32[3,512]{1,0:T(4,128)}, ...) all-reduce(bf16[512,3072]{1,0:T(8,128)(2,1)} %reduce-scatter.14.clo, ...), channel_id=1, replica_groups=mesh['ctx'=16,'fsdp'=2] {'ctx'}, use_global_device_ids=true, to_apply=%region_29.30 | all-reduce | flops 6298632 | bytes 37800000 | tf_op jit(solution)/shard_map/psum | solution.py:302
  (291 shorter events, 137.5 us)
Async XLA Ops:
  7.2 20.5 %all-gather.6.cloned.1.call-start = ((), (), s32[]{:S(2)}) async-start(), calls=%async_computation.7 | async-start | bytes 9437184 | tf_op jit(solution)/shard_map/all_gather | solution.py:102
  7.9 137.0 %all-gather.8.cloned.1.call-start = ((), (), s32[]{:S(2)}) async-start(), calls=%async_computation.8 | async-start | bytes 8912896 | tf_op jit(solution)/shard_map/all_gather | solution.py:132
  11.8 19.8 %copy-start.35 = (f32[128]{0:T(128)}, f32[128]{0:T(128)S(1)}, u32[]{:S(2)}) copy-start(f32[128]{0:T(128)S(1)} %broadcast_multiply_fusion.12) | copy-start | bytes 1540
  12.0 217.1 %copy-start.29 = (f32[1,1024]{1,0:T(1,128)}, f32[1,1024]{1,0:T(1,128)S(1)}, u32[]{:S(2)}) copy-start(f32[1,1024]{1,0:T(1,128)S(1)} %get-tuple-element.858) | copy-start | bytes 12292
  12.1 191.2 %copy-start.33 = (f32[1,1024]{1,0:T(1,128)}, f32[1,1024]{1,0:T(1,128)S(1)}, u32[]{:S(2)}) copy-start(f32[1,1024]{1,0:T(1,128)S(1)} %get-tuple-element.861) | copy-start | bytes 12292
  32.5 166.4 %all-gather.10.cloned.1.call-start = ((), (), s32[]{:S(2)}) async-start(), calls=%async_computation.9 | async-start | bytes 3145728 | tf_op jit(solution)/shard_map/all_gather | solution.py:103
  33.2 170.0 %all-gather.12.cloned.1.call-start = ((), (), s32[]{:S(2)}) async-start(), calls=%async_computation.10 | async-start | bytes 12582912 | tf_op jit(solution)/shard_map/all_gather | solution.py:104
  33.9 175.9 %all-gather.14.cloned.1.call-start = ((), (), s32[]{:S(2)}) async-start(), calls=%async_computation.11 | async-start | bytes 12582912 | tf_op jit(solution)/shard_map/all_gather | solution.py:105
  34.5 664.3 %reduce-scatter.12.cloned.1.call-start = ((), (), s32[]{:S(2)}) async-start(), calls=%async_computation.12 | async-start | bytes 17825792 | tf_op jit(solution)/shard_map/reduce_scatter | solution.py:259
  40.6 185.0 %copy-start.27 = (f32[4096]{0:T(1024)}, f32[4096]{0:T(1024)S(1)}, u32[]{:S(2)}) copy-start(f32[4096]{0:T(1024)S(1)} %convert_element_type.149) | copy-start | bytes 49156
  42.9 182.7 %copy-start.31 = (f32[4096]{0:T(1024)}, f32[4096]{0:T(1024)S(1)}, u32[]{:S(2)}) copy-start(f32[4096]{0:T(1024)S(1)} %convert_element_type.150) | copy-start | bytes 49156
  202.2 26.9 %copy-start.45 = (f32[128]{0:T(128)}, f32[128]{0:T(128)S(1)}, u32[]{:S(2)}) copy-start(f32[128]{0:T(128)S(1)} %broadcast_multiply_fusion.10) | copy-start | bytes 1540
  203.2 25.9 %copy-start.49 = (f32[128]{0:T(128)}, f32[128]{0:T(128)S(1)}, u32[]{:S(2)}) copy-start(f32[128]{0:T(128)S(1)} %add_rsqrt_fusion.1) | copy-start | bytes 1540
  349.4 411.4 %reduce-scatter.16.cloned.1.call-start = ((), (), s32[]{:S(2)}) async-start(), calls=%async_computation.14 | async-start | bytes 3145728 | tf_op jit(solution)/shard_map/reduce_scatter | solution.py:277
  352.4 408.4 %reduce-scatter.18.cloned.1.call-start = ((), (), s32[]{:S(2)}) async-start(), calls=%async_computation.15 | async-start | bytes 12582912 | tf_op jit(solution)/shard_map/reduce_scatter | solution.py:280
  358.6 402.2 %reduce-scatter.20.cloned.1.call-start = ((), (), s32[]{:S(2)}) async-start(), calls=%async_computation.16 | async-start | bytes 12582912 | tf_op jit(solution)/shard_map/reduce_scatter | solution.py:283
  366.3 398.8 %reduce-scatter.24.cloned.1.call-start = ((), (), s32[]{:S(2)}) async-start(), calls=%async_computation.18 | async-start | bytes 393216
  366.4 36.8 %copy-start.42 = (bf16[1024]{0:T(1024)(128)(2,1)S(1)}, bf16[1024]{0:T(1024)(128)(2,1)}, u32[]{:S(2)}) copy-start(bf16[1024]{0:T(1024)(128)(2,1)} %get-tuple-element.772) | copy-start | bytes 6148
  366.4 36.8 %copy-start.57 = (bf16[1024]{0:T(1024)(128)(2,1)S(1)}, bf16[1024]{0:T(1024)(128)(2,1)}, u32[]{:S(2)}) copy-start(bf16[1024]{0:T(1024)(128)(2,1)} %get-tuple-element.770) | copy-start | bytes 6148
  366.4 36.8 %copy-start.41 = (bf16[1024]{0:T(1024)(128)(2,1)S(1)}, bf16[1024]{0:T(1024)(128)(2,1)}, u32[]{:S(2)}) copy-start(bf16[1024]{0:T(1024)(128)(2,1)} %get-tuple-element.753) | copy-start | bytes 6148
  366.4 36.8 %copy-start.56 = (bf16[1024]{0:T(1024)(128)(2,1)S(1)}, bf16[1024]{0:T(1024)(128)(2,1)}, u32[]{:S(2)}) copy-start(bf16[1024]{0:T(1024)(128)(2,1)} %get-tuple-element.769) | copy-start | bytes 6148
  402.9 297.1 %copy-start.5 = (bf16[1,128,1024]{2,1,0:T(8,128)(2,1)S(1)}, bf16[1,128,1024]{2,1,0:T(8,128)(2,1)}, u32[]{:S(2)}) copy-start(bf16[1,128,1024]{2,1,0:T(8,128)(2,1)} %param.18) | copy-start | bytes 786436
  402.9 297.1 %copy-start.24 = (f32[1,1024]{1,0:T(1,128)S(1)}, f32[1,1024]{1,0:T(1,128)}, u32[]{:S(2)}) copy-start(f32[1,1024]{1,0:T(1,128)} %copy-done.23) | copy-start | bytes 12292
  402.9 297.1 %copy-start.36 = (f32[128]{0:T(128)S(1)}, f32[128]{0:T(128)}, u32[]{:S(2)}) copy-start(f32[128]{0:T(128)} %copy-done.35) | copy-start | bytes 1540
  402.9 297.1 %copy-start.38 = (f32[128]{0:T(128)S(1)}, f32[128]{0:T(128)}, u32[]{:S(2)}) copy-start(f32[128]{0:T(128)} %copy-done.37) | copy-start | bytes 1540
  706.2 70.7 %reduce-scatter.22.cloned.1.call-start = ((), (), s32[]{:S(2)}) async-start(), calls=%async_computation.17 | async-start | bytes 393216
  707.1 88.6 %reduce-scatter.14.cloned.1.call-start = ((), (), s32[]{:S(2)}) async-start(), calls=%async_computation.13 | async-start | bytes 9437184 | tf_op jit(solution)/shard_map/reduce_scatter | solution.py:274
  711.8 44.9 %copy-start.39 = (bf16[4096]{0:T(1024)(128)(2,1)S(1)}, bf16[4096]{0:T(1024)(128)(2,1)}, u32[]{:S(2)}) copy-start(bf16[4096]{0:T(1024)(128)(2,1)} %get-tuple-element.749) | copy-start | bytes 24580
  711.8 44.9 %copy-start.40 = (bf16[4096]{0:T(1024)(128)(2,1)S(1)}, bf16[4096]{0:T(1024)(128)(2,1)}, u32[]{:S(2)}) copy-start(bf16[4096]{0:T(1024)(128)(2,1)} %get-tuple-element.752) | copy-start | bytes 24580
  711.8 44.9 %copy-start.55 = (bf16[16]{0:T(256)(128)(2,1)S(1)}, bf16[16]{0:T(256)(128)(2,1)}, u32[]{:S(2)}) copy-start(bf16[16]{0:T(256)(128)(2,1)} %get-tuple-element.759) | copy-start | bytes 100
  711.8 49.0 %copy-start.13 = (f32[128,1024]{1,0:T(8,128)S(1)}, f32[128,1024]{1,0:T(8,128)}, u32[]{:S(2)}) copy-start(f32[128,1024]{1,0:T(8,128)} %copy-done.12) | copy-start | bytes 1572868
  760.8 34.9 %copy-start.22 = (bf16[512,1024]{1,0:T(8,128)(2,1)S(1)}, bf16[512,1024]{1,0:T(8,128)(2,1)}, u32[]{:S(2)}) copy-start(bf16[512,1024]{1,0:T(8,128)(2,1)} %reduce-scatter.16.cloned.1.call-done) | copy-start | bytes 3145732
  (44 other events, 228.8 us)
Sparse Core Ops, SparseCore 0:
  9.6 18.1 all-gather.5
  32.6 112.2 all-gather.7
  146.5 9.9 all-gather.9
  157.9 21.0 all-gather.11
  180.3 21.0 all-gather.13
  349.5 349.2 reduce-scatter.11
  701.6 12.0 reduce-scatter.15
  716.5 17.6 reduce-scatter.17
  736.5 17.6 reduce-scatter.19
  756.3 8.8 reduce-scatter.23
  768.0 8.8 reduce-scatter.21
  779.6 16.0 reduce-scatter.13
where the time goes:
time: 1870 us; the launch traced here: 1840 us
  blocking collectives  1090 us (58%)
  waiting for transfers between devices  447 us (24%)
  matrix products  136 us (7%)
  local copies, waits for them, and re-layouts  102 us (5%)
  other arithmetic  39 us (2%)
    psum x1, blocking collectives, local(): lax.psum((shard_grads[0], shard_grads[1], shard_grads[2], shard_grads[3],...  1040 us
    reduce_scatter x1, waiting for transfers between devices, local(): lax.psum_scatter(lax.map(key_term, sub_firsts).reshape(n_rows, 2 * model_...  295 us
    all_gather x1, waiting for transfers between devices, local(): fetched = lax.all_gather(keys_values, 'ctx', axis=0, tiled=True)  102 us
    psum x1, blocking collectives, local(): lax.psum(jnp.stack([jnp.sum(result * result), jnp.sum(attn_out * attn_out...  41.5 us
  transfers between devices with their start and end apart: 12, of which 6 were waited for; matrix products, arithmetic and copies ran while one was open for 7% of the time, Pallas kernels for 0%

commit v1 on v0

v1 whole, which is shorter than its diff:
```python
from functools import partial

import jax
import jax.numpy as jnp
from jax import lax
from jax.experimental import pallas as pl
from jax.experimental.pallas import tpu as pltpu
from jax.sharding import PartitionSpec as P

HEADS = 16
HEAD_DIM = 64
TILE = 256
EPS = 1e-05
MASKED = -1e30
SCALE = HEAD_DIM ** (-0.5)


def dot(a, b, ca=1, cb=0):
    return lax.dot_general(a, b, (((ca,), (cb,)), ((), ())), preferred_element_type=jnp.float32)


def normalize(values):
    centered = values - jnp.mean(values, axis=-1, keepdims=True)
    inverse = lax.rsqrt(jnp.mean(centered * centered, axis=-1, keepdims=True) + EPS)
    return (centered * inverse, inverse)


def norm_backward(grad_out, normed, inverse, gain_vec):
    grad_normed = grad_out * gain_vec
    grad_in = inverse * (
        grad_normed
        - jnp.mean(grad_normed, axis=-1, keepdims=True)
        - normed * jnp.mean(grad_normed * normed, axis=-1, keepdims=True)
    )
    return (grad_in, jnp.sum(grad_out * normed, axis=0), jnp.sum(grad_out, axis=0))


def sorted_sources(n_tiles):
    return [(t, 0) for t in range(n_tiles)] + [(t, 1) for t in range(n_tiles - 1, -1, -1)]


def pair_up(first, second):
    lane = lax.broadcasted_iota(jnp.int32, first[0].shape, 1)
    left = first[0] if first[1] == 0 else pltpu.roll(first[0], 64, 1)
    right = second[0] if second[1] == 1 else pltpu.roll(second[0], 64, 1)
    return jnp.where(lane < 64, left, right)


def sort_tiles(load, n_tiles, store):
    order = sorted_sources(n_tiles)
    for u in range(n_tiles):
        (ta, ha), (tb, hb) = order[2 * u], order[2 * u + 1]
        store(u, pair_up((load(ta), ha), (load(tb), hb)))


def unsort_tiles(load, n_tiles, store):
    for t in range(n_tiles):
        a, b = t, 2 * n_tiles - 1 - t
        store(t, pair_up((load(a // 2), a % 2), (load(b // 2), b % 2)))


def tile_spans(info_ref, qt, n_q_tiles, half_run, total_blocks):
    group = info_ref[0]
    per_run = n_q_tiles // 2
    low_first = group * half_run
    high_first = total_blocks * 64 - (group + 1) * half_run
    q_first = jnp.where(qt < per_run, low_first + qt * TILE, high_first + (qt - per_run) * TILE)
    start = jnp.int32(0)
    floor_first = jnp.int32(0)
    for d in range(8):
        floor_first = jnp.where(start <= q_first, start, floor_first)
        start = start + info_ref[1 + d]
    return q_first, floor_first // TILE


def query_rows(info_ref, q_first):
    q_pos = q_first + lax.broadcasted_iota(jnp.int32, (1, TILE), 1)
    start = jnp.int32(0)
    floor = jnp.zeros((1, TILE), jnp.int32)
    for d in range(8):
        floor = jnp.where(q_pos >= start, start, floor)
        start = start + info_ref[1 + d]
    return q_pos, floor


def usable_mask(q_pos, floor, kt):
    k_pos = kt * TILE + lax.broadcasted_iota(jnp.int32, (TILE, TILE), 0)
    return (k_pos <= q_pos) & (k_pos >= floor)


def attend_kernel(
    info_ref, hs_ref, q_ref, kv_ref, scaled_ref, att_ref, log_ref, qs_ref, ks_ref, vs_ref, kn_ref,
    *, n_q, n_k, k_at,
):
    per = TILE // 128
    f32 = jnp.float32

    def put(ref):
        def store(u, tile):
            ref[u // per, :, (u % per) * 128 : (u % per) * 128 + 128] = tile.astype(jnp.bfloat16)
        return store

    sort_tiles(lambda t: q_ref[t, 0].astype(f32), n_q, put(qs_ref))
    sort_tiles(lambda t: kv_ref[t, k_at].astype(f32), n_k, put(ks_ref))
    sort_tiles(lambda t: kv_ref[t, k_at + 1].astype(f32), n_k, put(vs_ref))
    for kt in range(n_k // per):
        kn_ref[kt] = ks_ref[kt].astype(f32).T.astype(jnp.bfloat16)

    def one_query_tile(qt, carry):
        q_first, k_low = tile_spans(info_ref, qt, n_q // per, n_q * 64, 2 * n_k)
        q_pos, floor = query_rows(info_ref, q_first)
        q_t = qs_ref[qt]

        def one_key_tile(kt, state):
            high, total, acc = state
            scores = dot(kn_ref[kt], q_t) * SCALE
            usable = usable_mask(q_pos, floor, kt)
            scores = jnp.where(usable, scores, MASKED)
            new_high = jnp.maximum(high, jnp.max(scores, axis=0, keepdims=True))
            probs = jnp.where(usable, jnp.exp(scores - new_high), 0.0)
            fix = jnp.exp(high - new_high)
            total = total * fix + jnp.sum(probs, axis=0, keepdims=True)
            acc = acc * fix + dot(vs_ref[kt], probs.astype(jnp.bfloat16))
            return new_high, total, acc

        high, total, acc = lax.fori_loop(
            k_low,
            q_first // TILE + 1,
            one_key_tile,
            (
                jnp.full((1, TILE), MASKED, f32),
                jnp.zeros((1, TILE), f32),
                jnp.zeros((HEAD_DIM, TILE), f32),
            ),
        )
        att_ref[qt] = acc / total
        log_ref[qt] = high + jnp.log(total)
        return carry

    lax.fori_loop(0, n_q // per, one_query_tile, 0)
    head_scale = hs_ref[0]

    def load(u):
        return att_ref[u // per, :, (u % per) * 128 : (u % per) * 128 + 128]

    def give(t, tile):
        scaled_ref[t] = (tile * head_scale).astype(jnp.bfloat16)

    unsort_tiles(load, n_q, give)


def attend_back_kernel(
    info_ref, qs_ref, ks_ref, vs_ref, att_ref, log_ref, go_ref, dq_ref, dk_ref, dv_ref, dsum_ref,
    go_s, kn_ref, vn_ref, dq_s, dk_s, dv_s,
    *, n_q, n_k,
):
    per = TILE // 128
    f32 = jnp.float32
    low = jnp.bfloat16

    def store(u, tile):
        go_s[u // per, :, (u % per) * 128 : (u % per) * 128 + 128] = tile.astype(low)

    sort_tiles(lambda t: go_ref[t].astype(f32), n_q, store)
    for kt in range(n_k // per):
        kn_ref[kt] = ks_ref[kt].astype(f32).T.astype(low)
        vn_ref[kt] = vs_ref[kt].astype(f32).T.astype(low)
        dk_s[kt] = jnp.zeros((TILE, HEAD_DIM), f32)
        dv_s[kt] = jnp.zeros((TILE, HEAD_DIM), f32)
    dsum_ref[...] = jnp.zeros((1, TILE), f32)

    def one_query_tile(qt, carry):
        q_first, k_low = tile_spans(info_ref, qt, n_q // per, n_q * 64, 2 * n_k)
        q_pos, floor = query_rows(info_ref, q_first)
        q_t = qs_ref[qt]
        g_t = go_s[qt]
        q_n = q_t.astype(f32).T.astype(low)
        g_n = g_t.astype(f32).T.astype(low)
        log_total = log_ref[qt]
        delta = jnp.sum(g_t.astype(f32) * att_ref[qt], axis=0, keepdims=True)
        dsum_ref[...] += delta

        def one_key_tile(kt, acc):
            scores = dot(kn_ref[kt], q_t) * SCALE
            usable = usable_mask(q_pos, floor, kt)
            probs = jnp.where(usable, jnp.exp(scores - log_total), 0.0)
            grad_probs = dot(vn_ref[kt], g_t)
            grad_scores = (probs * (grad_probs - delta)).astype(low)
            dv_s[kt] += dot(probs.astype(low), g_n)
            dk_s[kt] += dot(grad_scores, q_n)
            return acc + dot(ks_ref[kt], grad_scores)

        dq_s[qt] = lax.fori_loop(
            k_low, q_first // TILE + 1, one_key_tile, jnp.zeros((HEAD_DIM, TILE), f32)
        )
        return carry

    lax.fori_loop(0, n_q // per, one_query_tile, 0)

    def load_q(u):
        return dq_s[u // per, :, (u % per) * 128 : (u % per) * 128 + 128]

    def give_q(t, tile):
        dq_ref[t] = (tile * SCALE).astype(dq_ref.dtype)

    def load_k(u):
        return dk_s[u // per, (u % per) * 128 : (u % per) * 128 + 128, :].T

    def give_k(t, tile):
        dk_ref[t] = (tile * SCALE).astype(dk_ref.dtype)

    def load_v(u):
        return dv_s[u // per, (u % per) * 128 : (u % per) * 128 + 128, :].T

    def give_v(t, tile):
        dv_ref[t] = tile.astype(dv_ref.dtype)

    unsort_tiles(load_q, n_q, give_q)
    unsort_tiles(load_k, n_k, give_k)
    unsort_tiles(load_v, n_k, give_v)


def on_chip(n):
    return [pl.BlockSpec(memory_space=pltpu.VMEM)] * n


def in_scalars(n):
    return [pl.BlockSpec(memory_space=pltpu.SMEM)] * n


def attend(info, head_scale, q_tiles, kv_tiles, k_at):
    n_q, n_k = q_tiles.shape[0], kv_tiles.shape[0]
    nq, nk = n_q * 128 // TILE, n_k * 128 // TILE
    low, f32 = jnp.bfloat16, jnp.float32
    return pl.pallas_call(
        partial(attend_kernel, n_q=n_q, n_k=n_k, k_at=k_at),
        in_specs=in_scalars(2) + on_chip(2),
        out_specs=tuple(on_chip(6)),
        out_shape=(
            jax.ShapeDtypeStruct((n_q, HEAD_DIM, 128), low),
            jax.ShapeDtypeStruct((nq, HEAD_DIM, TILE), f32),
            jax.ShapeDtypeStruct((nq, 1, TILE), f32),
            jax.ShapeDtypeStruct((nq, HEAD_DIM, TILE), low),
            jax.ShapeDtypeStruct((nk, HEAD_DIM, TILE), low),
            jax.ShapeDtypeStruct((nk, HEAD_DIM, TILE), low),
        ),
        scratch_shapes=[pltpu.VMEM((nk, TILE, HEAD_DIM), low)],
        compiler_params=pltpu.CompilerParams(vmem_limit_bytes=48 << 20),
        name="attend",
    )(info, head_scale, q_tiles, kv_tiles)


def attend_back(info, qs, ks, vs, att, log_total, grad_tiles, kv_type):
    n_q = grad_tiles.shape[0]
    nq, nk = qs.shape[0], ks.shape[0]
    n_k = nk * TILE // 128
    low, f32 = jnp.bfloat16, jnp.float32
    return pl.pallas_call(
        partial(attend_back_kernel, n_q=n_q, n_k=n_k),
        in_specs=in_scalars(1) + on_chip(6),
        out_specs=tuple(on_chip(4)),
        out_shape=(
            jax.ShapeDtypeStruct((n_q, HEAD_DIM, 128), low),
            jax.ShapeDtypeStruct((n_k, HEAD_DIM, 128), kv_type),
            jax.ShapeDtypeStruct((n_k, HEAD_DIM, 128), kv_type),
            jax.ShapeDtypeStruct((1, TILE), f32),
        ),
        scratch_shapes=[
            pltpu.VMEM((nq, HEAD_DIM, TILE), low),
            pltpu.VMEM((nk, TILE, HEAD_DIM), low),
            pltpu.VMEM((nk, TILE, HEAD_DIM), low),
            pltpu.VMEM((nq, HEAD_DIM, TILE), f32),
            pltpu.VMEM((nk, TILE, HEAD_DIM), f32),
            pltpu.VMEM((nk, TILE, HEAD_DIM), f32),
        ],
        compiler_params=pltpu.CompilerParams(vmem_limit_bytes=48 << 20),
        name="attend_back",
    )(info, qs, ks, vs, att, log_total, grad_tiles)


def from_member(value, s, size):
    return lax.ppermute(value, "fsdp", [((i + s) % size, i) for i in range(size)])


def gather_parts(shard, size):
    return [shard] + [from_member(shard, s, size) for s in range(1, size)]


def part_of(value, s, me, size, axis):
    width = value.shape[axis] // size
    return lax.dynamic_slice_in_dim(value, ((me + s) % size) * width, width, axis)


def natural(parts, me, axis):
    size = len(parts)
    twice = jnp.concatenate(parts + parts, axis=axis)
    width = parts[0].shape[axis]
    return lax.dynamic_slice_in_dim(twice, ((size - me) % size) * width, size * width, axis)


def times_parts(value, parts, me):
    size = len(parts)
    total = dot(part_of(value, 0, me, size, 1), parts[0])
    for s in range(1, size):
        total = total + dot(part_of(value, s, me, size, 1), parts[s])
    return total


def all_tokens(value, size):
    return jnp.concatenate([value] + [from_member(value, s, size) for s in range(1, size)], axis=0)


def all_tokens_own(value, me, size):
    pieces = [part_of(value, 0, me, size, 1)]
    for s in range(1, size):
        pieces.append(from_member(part_of(value, size - s, me, size, 1), s, size))
    return jnp.concatenate(pieces, axis=0)


def local(
    inputs, cotangent, doc_lengths, qkv_weight, out_weight, fc1_weight, fc2_weight,
    norm_gain, norm_bias, mid_gain, mid_bias, head_scale,
):
    low, f32 = jnp.bfloat16, jnp.float32
    groups = lax.axis_size("ctx")
    size = lax.axis_size("fsdp")
    member = lax.axis_index("ctx")
    me = lax.axis_index("fsdp")
    x_low = inputs[0]
    rows, width = x_low.shape
    hidden_width = fc1_weight.shape[1]
    copies = groups // HEADS
    head_groups = [[g * HEADS + i for i in range(HEADS)] for g in range(copies)]
    copy_groups = [[g * HEADS + i for g in range(copies)] for i in range(HEADS)]
    head = member % HEADS
    info = jnp.concatenate([(member // HEADS)[None].astype(jnp.int32), doc_lengths[0]])

    qkv_parts = gather_parts(qkv_weight, size)
    small = jnp.concatenate(
        [norm_gain.reshape(-1), norm_bias.reshape(-1), mid_gain, mid_bias, head_scale]
    )
    smalls = gather_parts(small, size)
    out_parts = gather_parts(out_weight, size)
    fc1_parts = gather_parts(fc1_weight, size)
    fc2_parts = gather_parts(fc2_weight, size)

    n_norm = norm_gain.size
    n_mid = mid_gain.size
    n_head = head_scale.size
    cut = [0, n_norm, 2 * n_norm, 2 * n_norm + n_mid, 2 * n_norm + 2 * n_mid, small.size]
    fields = [[s[cut[i] : cut[i + 1]] for s in smalls] for i in range(5)]
    gains = natural([f.reshape(3, -1) for f in fields[0]], me, 1).astype(f32)
    biases = natural([f.reshape(3, -1) for f in fields[1]], me, 1).astype(f32)
    mid_gains = natural(fields[2], me, 0).astype(f32)
    mid_biases = natural(fields[3], me, 0).astype(f32)
    head_scales = natural(fields[4], me, 0).astype(f32)
    my_scale = lax.dynamic_slice_in_dim(head_scales, head, 1, 0)

    x_local = x_low.astype(f32)
    norm_one, inv_one = normalize(x_local)
    normed_one = (norm_one * gains[0] + biases[0]).astype(low)
    project_t = sum(
        dot(qkv_parts[s], part_of(normed_one, s, me, size, 1), 0, 1) for s in range(size)
    ).astype(low)
    by_head = project_t.reshape(3, HEADS, HEAD_DIM, rows).transpose(1, 0, 2, 3)
    qkv_tiles = lax.all_to_all(by_head, "ctx", 0, 0, tiled=True, axis_index_groups=head_groups)
    if copies == 1:
        kv_tiles, k_at = qkv_tiles, 1
    else:
        kv_tiles, k_at = lax.all_gather(
            qkv_tiles[:, 1:], "ctx", axis=0, tiled=True, axis_index_groups=copy_groups
        ), 0
    scaled_tiles, att, log_total, qs, ks, vs = attend(info, my_scale, qkv_tiles, kv_tiles, k_at)
    scaled_t = lax.all_to_all(
        scaled_tiles, "ctx", 0, 0, tiled=True, axis_index_groups=head_groups
    ).reshape(width, rows)
    branch = sum(dot(part_of(scaled_t, s, me, size, 0), out_parts[s], 0, 0) for s in range(size))
    norm_att, inv_att = normalize(branch)
    attn_out = norm_att * gains[1] + biases[1]
    middle = x_local + attn_out
    norm_two, inv_two = normalize(middle)
    normed_two = (norm_two * gains[2] + biases[2]).astype(low)
    hidden = times_parts(normed_two, fc1_parts, me)
    active, gelu_back = jax.vjp(partial(jax.nn.gelu, approximate=True), hidden)
    norm_mid, inv_mid = normalize(active)
    mixed_in = (norm_mid * mid_gains + mid_biases).astype(low)
    ffn_out = times_parts(mixed_in, fc2_parts, me)
    result = middle + ffn_out

    grad_ffn = cotangent[0]
    grad_top = grad_ffn.astype(f32)
    fc2_grad = dot(all_tokens_own(mixed_in, me, size), all_tokens(grad_ffn, size), 0, 0).astype(low)
    grad_mixed = natural([dot(grad_ffn, part, 1, 1) for part in fc2_parts], me, 1)
    grad_active, mid_gain_grad, mid_bias_grad = norm_backward(
        grad_mixed, norm_mid, inv_mid, mid_gains
    )
    grad_hidden = gelu_back(grad_active)[0].astype(low)
    fc1_grad = dot(
        all_tokens_own(normed_two, me, size), all_tokens(grad_hidden, size), 0, 0
    ).astype(low)
    fc2_sum, fc1_sum = lax.psum((fc2_grad, fc1_grad), "ctx")
    grad_two = natural([dot(grad_hidden, part, 1, 1) for part in fc1_parts], me, 1)
    grad_mid_in, gain_two, bias_two = norm_backward(grad_two, norm_two, inv_two, gains[2])
    grad_middle = grad_top + grad_mid_in
    grad_branch_f, gain_att, bias_att = norm_backward(grad_middle, norm_att, inv_att, gains[1])
    grad_branch = grad_branch_f.astype(low)
    out_grad = dot(
        all_tokens_own(scaled_t.T, me, size), all_tokens(grad_branch, size), 0, 0
    ).astype(low)
    grad_scaled_t = natural([dot(part, grad_branch, 1, 1) for part in out_parts], me, 0)
    grad_att = (
        grad_scaled_t.reshape(HEADS, HEAD_DIM, rows) * head_scales[:, None, None]
    ).astype(low)
    grad_tiles = lax.all_to_all(grad_att, "ctx", 0, 0, tiled=True, axis_index_groups=head_groups)
    dq, dk, dv, delta_sum = attend_back(
        info, qs, ks, vs, att, log_total, grad_tiles, low if copies == 1 else f32
    )
    if copies > 1:
        dk, dv = (
            lax.psum_scatter(
                d, "ctx", scatter_dimension=0, tiled=True, axis_index_groups=copy_groups
            ).astype(low)
            for d in (dk, dv)
        )
    grads_out = jnp.stack([dq, dk, dv], axis=1)
    grad_proj_t = lax.all_to_all(
        grads_out, "ctx", 0, 0, tiled=True, axis_index_groups=head_groups
    ).transpose(1, 0, 2, 3).reshape(3 * width, rows)
    qkv_grad = dot(
        all_tokens_own(normed_one, me, size), all_tokens(grad_proj_t.T, size), 0, 0
    ).astype(low)
    fc2_sum, fc1_sum, out_grad, qkv_grad = lax.optimization_barrier(
        (fc2_sum, fc1_sum, out_grad, qkv_grad)
    )
    out_sum, qkv_sum = lax.psum((out_grad, qkv_grad), "ctx")
    grad_one = natural([dot(grad_proj_t, part, 0, 1) for part in qkv_parts], me, 1)
    grad_first, gain_one, bias_one = norm_backward(grad_one, norm_one, inv_one, gains[0])
    input_grad = (grad_middle + grad_first).astype(low)[None]

    my_scale_grad = jnp.sum(delta_sum) / my_scale[0]
    scale_grad = jnp.where(jnp.arange(HEADS) == head, my_scale_grad, 0.0)
    squares = jnp.stack(
        [jnp.sum(result * result), jnp.sum(attn_out * attn_out), jnp.sum(ffn_out * ffn_out)]
    )
    packed = jnp.concatenate(
        [gain_one, gain_att, gain_two, bias_one, bias_att, bias_two,
         mid_gain_grad, mid_bias_grad, scale_grad, squares]
    )
    total = lax.psum(packed, ("ctx", "fsdp"))
    gain_grad = part_of(total[: 3 * width].reshape(3, width), 0, me, size, 1)
    bias_grad = part_of(total[3 * width : 6 * width].reshape(3, width), 0, me, size, 1)
    at = 6 * width
    mid_gain_sum = part_of(total[at : at + hidden_width], 0, me, size, 0)
    at = at + hidden_width
    mid_bias_sum = part_of(total[at : at + hidden_width], 0, me, size, 0)
    at = at + hidden_width
    scale_sum = part_of(total[at : at + HEADS], 0, me, size, 0)
    rms_values = jnp.sqrt(total[at + HEADS :] / (rows * groups * size * width))
    return (
        result.astype(low)[None],
        input_grad,
        qkv_sum.astype(f32),
        out_sum.astype(f32),
        fc1_sum.astype(f32),
        fc2_sum.astype(f32),
        gain_grad,
        bias_grad,
        mid_gain_sum,
        mid_bias_sum,
        scale_sum,
        rms_values,
    )


def solution(mesh):
    split = P("fsdp", "ctx", None)
    by_row = P("fsdp", None)
    by_col = P(None, "fsdp")
    one = P("fsdp")
    return jax.shard_map(
        local,
        mesh=mesh,
        in_specs=(split, split, by_row, by_row, by_row, by_row, by_row, by_col, by_col, one, one, one),
        out_specs=(split, split, by_row, by_row, by_row, by_row, by_col, by_col, one, one, one, P()),
        check_vma=False,
    )
```

time: 1870 us -> 577 us (0.31); the launches traced: 1840 us -> 573 us
  blocking collectives: 1090 us -> 109 us
  waiting for transfers between devices: 447 us -> 295 us
  local copies, waits for them, and re-layouts: 102 us -> 20.4 us
  matrix products: 136 us -> 55.6 us
  Pallas kernels: 0 us -> 22.6 us
    psum x2 -> x1, blocking collectives: 1080 us -> 44.9 us  [local(): total = lax.psum(packed, ('ctx', 'fsdp'))]
    reduce_scatter x5 -> x0, waiting for transfers between devices: 313 us -> none  [the longest x1 295 us: local(): lax.psum_scatter(lax.map(key_term, sub_firsts).reshape(n_rows, 2 * model_...]
    psum x0 -> x2, waiting for transfers between devices: none -> 277 us  [the longest x1 172 us: local(): fc2_sum, fc1_sum = lax.psum((fc2_grad, fc1_grad), 'ctx')]
    all_gather x5 -> x0, waiting for transfers between devices: 117 us -> none  [the longest x1 102 us: local(): fetched = lax.all_gather(keys_values, 'ctx', axis=0, tiled=True)]
    dot_general x26 -> x20, matrix products: 136 us -> 55.6 us  [dot(): lax.dot_general(a, b, (((ca,), (cb,)), ((), ())), preferred_element_type=...]
    all_to_all x0 -> x2, blocking collectives: none -> 64.2 us  [the longest x1 41.8 us: local(): lax.all_to_all(grads_out, 'ctx', 0, 0, tiled=True, axis_index_groups=head...]
    dynamic_update_slice x4 -> x0, local copies, waits for them, and re-layouts: 33.6 us -> none  [local(): lax.map(key_term, sub_firsts).reshape(n_rows, 2 * model_width)]
    convert_element_type x9 -> x13, other arithmetic: 2.54 us -> 26.3 us  [the longest x1 6.82 us: local(): fc1_sum.astype(f32)]
  transfers between devices with their start and end apart: 12 -> 17, of which waited for: 6 -> 6; matrix products, arithmetic and copies ran while one was open for 7% -> 15% of each run, Pallas kernels for 0% -> 4%
where the time goes in v1:
time: 577 us; the launch traced here: 573 us
  waiting for transfers between devices  295 us (51%)
  blocking collectives  109 us (19%)
  matrix products  55.6 us (10%)
  other arithmetic  37.8 us (7%)
  Pallas kernels  22.6 us (4%)
  local copies, waits for them, and re-layouts  20.4 us (4%)
  between operations  16.4 us (3%)
  starting transfers between devices  16.1 us (3%)
    psum x1, waiting for transfers between devices, local(): fc2_sum, fc1_sum = lax.psum((fc2_grad, fc1_grad), 'ctx')  172 us
    psum x1, waiting for transfers between devices, local(): out_sum, qkv_sum = lax.psum((out_grad, qkv_grad), 'ctx')  105 us
    dot_general x20, matrix products, dot(): lax.dot_general(a, b, (((ca,), (cb,)), ((), ())), preferred_element_type=...  55.6 us
    psum x1, blocking collectives, local(): total = lax.psum(packed, ('ctx', 'fsdp'))  44.9 us
    all_to_all x1, blocking collectives, local(): lax.all_to_all(grads_out, 'ctx', 0, 0, tiled=True, axis_index_groups=head...  41.8 us
    all_to_all x1, blocking collectives, local(): lax.all_to_all(grad_att, 'ctx', 0, 0, tiled=True, axis_index_groups=head_...  22.4 us
    all_to_all x1, waiting for transfers between devices, local(): lax.all_to_all(by_head, 'ctx', 0, 0, tiled=True, axis_index_groups=head_g...  13.6 us
  transfers between devices with their start and end apart: 17, of which 6 were waited for; matrix products, arithmetic and copies ran while one was open for 15% of the time, Pallas kernels for 4%

profile of v1, /device:TPU:12, one launch (start us, length us, event | category | flops | bytes accessed | tf_op | source)
XLA Modules:
  0.0 572.9 jit_solution(170154580971865397)
XLA Ops:
  17.9 2.6 fusion.106
  20.5 1.9 fusion.1
  22.4 2.3 copy.32
  24.7 2.1 copy.38
  26.8 7.2 %all-to-all-start = ((bf16[16,3,64,128]{3,2,1,0:T(8,128)(2,1)}), bf16[16,3,64,128]{3,2,1,0:T(8,128)(2,1)S(1)}, u32[]{:S(2)}, u32[]{:S(2)}) async-start(bf16[16,3,64,128]{3,2,1,0:T(8,128)(2,1)} %bitcast.113), calls=%async_computation | async-start | bytes 1572864 | tf_op jit(solution)/shard_map/all_to_all | solution.py:366
  34.5 4.7 fusion.91
  40.5 13.6 %all-to-all-done.q_ref.kv_ref = bf16[16,3,64,128]{3,2,1,0:T(8,128)(2,1)S(1)} async-done(((bf16[16,3,64,128]{3,2,1,0:T(8,128)(2,1)}), bf16[16,3,64,128]{3,2,1,0:T(8,128)(2,1)S(1)}, u32[]{:S(2)}, u32[]{:S(2)}) %all-to-all-start) | async-done | bytes 786464 | tf_op jit(solution)/shard_map/all_to_all | solution.py:366
  54.2 11.3 %attend.1 = (bf16[16,64,128]{2,1,0:T(8,128)(2,1)}, f32[8,64,256]{2,1,0:T(8,128)S(1)}, f32[8,1,256]{2,1,0:T(1,128)S(1)}, bf16[8,64,256]{2,1,0:T(8,128)(2,1)S(1)},...) custom-call(s32[9]{0:T(128)S(1)} %pad_add_fusion.info_ref, f32[1]{0:T(128)} %dynamic_slice.82.hs_ref, ...), custom_call_target="tpu_custom_call" | custom-call | tf_op jit(solution)/shard_map/attend/pallas_call | solution.py:235
  65.5 5.1 all-to-all-start.1
  72.2 4.7 fusion.89
  79.2 1.8 fusion.105
  83.3 3.8 fusion.93
  88.7 3.3 multiply_reduce_fusion
  91.9 3.1 fusion.8
  98.9 3.3 convolution_convert_fusion.2
  102.2 4.5 convolution_convert_fusion
  107.1 3.2 fusion.108
  112.3 4.8 fusion.110
  117.2 4.7 multiply_reduce_fusion.4
  129.2 22.4 %all_to_all.20.go_ref = bf16[16,64,128]{2,1,0:T(8,128)(2,1)S(1)} all-to-all(bf16[16,64,128]{2,1,0:T(8,128)(2,1)S(1)} %multiply_convert_fusion), channel_id=1, replica_groups={{0,2,4,6,8,10,12,14,16,18,20,22,24,26,28,30},{1,3,5,7,9,11,13,15,17,19,..., dimensions={0} | all-to-all | bytes 524288 | tf_op jit(solution)/shard_map/all_to_all | solution.py:414
  151.5 11.3 %attend_back.1 = (bf16[16,64,128]{2,1,0:T(8,128)(2,1)S(1)}, bf16[16,64,128]{2,1,0:T(8,128)(2,1)S(1)}, bf16[16,64,128]{2,1,0:T(8,128)(2,1)S(1)}, f32[1,256]{1,0:T(1,128)S(1)}) custom-call(s32[9]{0:T(128)S(1)} %pad_add_fusion.info_ref, bf16[8,64,256]{2,1,0:T(8,128)(2,1)S(1)} %get-tuple-element.27.qs_ref, bf16[8,64,256]{2,1,0:T(8,128)(2,1)S(1)} %get-tuple-element.28.ks_ref, ...), custom_call_target="tpu_custom_call" | custom-call | tf_op jit(solution)/shard_map/attend_back/pallas_call | solution.py:258
  163.0 41.8 %all_to_all.21 = bf16[16,3,64,128]{3,2,1,0:T(8,128)(2,1)S(1)} all-to-all(bf16[16,3,64,128]{3,2,1,0:T(8,128)(2,1)S(1)} %copy.35), channel_id=1, replica_groups={{0,2,4,6,8,10,12,14,16,18,20,22,24,26,28,30},{1,3,5,7,9,11,13,15,17,19,..., dimensions={0} | all-to-all | bytes 1572864 | tf_op jit(solution)/shard_map/all_to_all | solution.py:426
  206.0 1.7 collective-permute-done.9
  209.2 2.7 convolution_convert_fusion.1
  211.9 172.4 %all-reduce.7.cloned.1.call-done = (bf16[2048,1024]{1,0:T(8,128)(2,1)}, bf16[512,4096]{1,0:T(8,128)(2,1)}) async-done(((bf16[2048,1024]{1,0:T(8,128)(2,1)}, bf16[512,4096]{1,0:T(8,128)(2,1)}), (bf16[2048,1024]{1,0:T(8,128)(2,1)}, bf16[512,4096]{1,0:T(8,128)(2,1)})) %all-reduce.7.cloned.1.call-update) | async-done | bytes 8388624 | tf_op jit(solution)/shard_map/psum | solution.py:401
  386.3 3.2 fusion.111
  391.3 1.9 concatenate.79
  393.2 44.9 %psum.39 = f32[14355]{0:T(1024)S(1)} all-reduce(f32[14355]{0:T(1024)S(1)} %concatenate.79), channel_id=1, replica_groups=mesh['ctx'=16,'fsdp'=2] {'ctx','fsdp'}, use_global_device_ids=true, to_apply=%region_32.33 | all-reduce | flops 14355 | bytes 114840 | tf_op jit(solution)/shard_map/psum | solution.py:449
  442.7 6.8 %convert_element_type.102 = f32[512,4096]{1,0:T(8,128)} convert(bf16[512,4096]{1,0:T(8,128)(2,1)} %get-tuple-element.37) | non-fusion elementwise | flops 2097152 | bytes 12582912 | tf_op jit(solution)/shard_map/convert_element_type | solution.py:464
  449.5 4.4 convert_element_type.103
  454.0 105.0 %all-reduce.5.cloned.1.call-done = (bf16[512,3072]{1,0:T(8,128)(2,1)}, bf16[512,1024]{1,0:T(8,128)(2,1)}) async-done(((bf16[512,3072]{1,0:T(8,128)(2,1)}, bf16[512,1024]{1,0:T(8,128)(2,1)}), (bf16[512,3072]{1,0:T(8,128)(2,1)}, bf16[512,1024]{1,0:T(8,128)(2,1)})) %all-reduce.5.cloned.1.call-update) | async-done | bytes 4194320 | tf_op jit(solution)/shard_map/psum | solution.py:435
  559.0 5.5 convert_element_type.100
  (227 shorter events, 44.5 us)
Async XLA Ops:
  7.2 13.3 %collective-permute-start.1 = (bf16[512,3072]{1,0:T(8,128)(2,1)}, bf16[512,3072]{1,0:T(8,128)(2,1)S(1)}, u32[]{:S(2)}, u32[]{:S(2)}) collective-permute-start(bf16[512,3072]{1,0:T(8,128)(2,1)} %param.15), channel_id=1, source_target_pairs={{1,0},{0,1},{3,2},{2,3},{5,4},{4,5},{7,6},{6,7},{9,8},{8,9},{11,10... | collective-permute-start | bytes 9437192 | tf_op jit(solution)/shard_map/ppermute | solution.py:282
  11.2 2.8 collective-permute-start
  11.7 60.6 %collective-permute-start.4 = (bf16[2048,1024]{1,0:T(8,128)(2,1)}, bf16[2048,1024]{1,0:T(8,128)(2,1)}, u32[]{:S(2)}, u32[]{:S(2)}) collective-permute-start(bf16[2048,1024]{1,0:T(8,128)(2,1)} %param.18), channel_id=1, source_target_pairs={{1,0},{0,1},{3,2},{2,3},{5,4},{4,5},{7,6},{6,7},{9,8},{8,9},{11,10... | collective-permute-start | bytes 12582920 | tf_op jit(solution)/shard_map/ppermute | solution.py:282
  12.8 7.7 %copy-start.41 = (f32[128]{0:T(128)}, f32[128]{0:T(128)S(1)}, u32[]{:S(2)}) copy-start(f32[128]{0:T(128)S(1)} %broadcast_multiply_fusion.11) | copy-start | bytes 1540
  13.9 6.5 %copy-start.45 = (f32[128]{0:T(128)}, f32[128]{0:T(128)S(1)}, u32[]{:S(2)}) copy-start(f32[128]{0:T(128)S(1)} %add_rsqrt_fusion.3) | copy-start | bytes 1540
  22.4 12.1 %copy-start.56 = (s32[1,8]{1,0:T(1,128)S(1)}, s32[1,8]{1,0:T(1,128)}, u32[]{:S(2)}) copy-start(s32[1,8]{1,0:T(1,128)} %param.14) | copy-start | bytes 100
  22.4 12.2 %copy-start.10 = (bf16[1,128,1024]{2,1,0:T(8,128)(2,1)S(1)}, bf16[1,128,1024]{2,1,0:T(8,128)(2,1)}, u32[]{:S(2)}) copy-start(bf16[1,128,1024]{2,1,0:T(8,128)(2,1)} %param.13) | copy-start | bytes 786436
  26.8 27.4 %all-to-all-start = ((bf16[16,3,64,128]{3,2,1,0:T(8,128)(2,1)}), bf16[16,3,64,128]{3,2,1,0:T(8,128)(2,1)S(1)}, u32[]{:S(2)}, u32[]{:S(2)}) async-start(bf16[16,3,64,128]{3,2,1,0:T(8,128)(2,1)} %bitcast.113), calls=%async_computation | async-start | bytes 1572864 | tf_op jit(solution)/shard_map/all_to_all | solution.py:366
  33.9 45.3 %collective-permute-start.2 = (bf16[512,1024]{1,0:T(8,128)(2,1)}, bf16[512,1024]{1,0:T(8,128)(2,1)}, u32[]{:S(2)}, u32[]{:S(2)}) collective-permute-start(bf16[512,1024]{1,0:T(8,128)(2,1)} %param.16), channel_id=1, source_target_pairs={{1,0},{0,1},{3,2},{2,3},{5,4},{4,5},{7,6},{6,7},{9,8},{8,9},{11,10... | collective-permute-start | bytes 3145736 | tf_op jit(solution)/shard_map/ppermute | solution.py:282
  33.9 49.4 %collective-permute-start.3 = (bf16[512,4096]{1,0:T(8,128)(2,1)}, bf16[512,4096]{1,0:T(8,128)(2,1)}, u32[]{:S(2)}, u32[]{:S(2)}) collective-permute-start(bf16[512,4096]{1,0:T(8,128)(2,1)} %param.17), channel_id=1, source_target_pairs={{1,0},{0,1},{3,2},{2,3},{5,4},{4,5},{7,6},{6,7},{9,8},{8,9},{11,10... | collective-permute-start | bytes 12582920 | tf_op jit(solution)/shard_map/ppermute | solution.py:282
  39.2 31.6 %copy-start.37 = (bf16[2048]{0:T(1024)(128)(2,1)S(1)}, bf16[2048]{0:T(1024)(128)(2,1)}, u32[]{:S(2)}) copy-start(bf16[2048]{0:T(1024)(128)(2,1)} %param.21) | copy-start | bytes 12292
  39.2 32.3 %copy-start.38 = (bf16[2048]{0:T(1024)(128)(2,1)S(1)}, bf16[2048]{0:T(1024)(128)(2,1)}, u32[]{:S(2)}) copy-start(bf16[2048]{0:T(1024)(128)(2,1)} %param.22) | copy-start | bytes 12292
  39.2 33.0 %copy-start.11 = (bf16[1,128,1024]{2,1,0:T(8,128)(2,1)S(1)}, bf16[1,128,1024]{2,1,0:T(8,128)(2,1)}, u32[]{:S(2)}) copy-start(bf16[1,128,1024]{2,1,0:T(8,128)(2,1)} %param.13) | copy-start | bytes 786436
  65.5 12.1 %all-to-all-start.1 = ((bf16[16,64,128]{2,1,0:T(8,128)(2,1)}), bf16[16,64,128]{2,1,0:T(8,128)(2,1)S(1)}, u32[]{:S(2)}, u32[]{:S(2)}) async-start(bf16[16,64,128]{2,1,0:T(8,128)(2,1)} %get-tuple-element.26), calls=%async_computation.1 | async-start | bytes 524288 | tf_op jit(solution)/shard_map/all_to_all | solution.py:374
  70.6 313.6 %all-reduce.7.cloned.1.call-start = ((), (), s32[]{:S(2)}) async-start(), calls=%async_computation.5 | async-start | bytes 16777216 | tf_op jit(solution)/shard_map/psum | solution.py:401
  95.1 7.2 %collective-permute-start.8 = (bf16[128,4096]{1,0:T(8,128)(2,1)S(1)}, bf16[128,4096]{1,0:T(8,128)(2,1)}, u32[]{:S(2)}, u32[]{:S(2)}) collective-permute-start(bf16[128,4096]{1,0:T(8,128)(2,1)S(1)} %get-tuple-element.72), channel_id=1, source_target_pairs={{1,0},{0,1},{3,2},{2,3},{5,4},{4,5},{7,6},{6,7},{9,8},{8,9},{11,10... | collective-permute-start | bytes 3145736 | tf_op jit(solution)/shard_map/ppermute | solution.py:282
  96.4 5.8 %copy-start.14 = (bf16[128,2048]{1,0:T(8,128)(2,1)}, bf16[128,2048]{1,0:T(8,128)(2,1)S(1)}, u32[]{:S(2)}) copy-start(bf16[128,2048]{1,0:T(8,128)(2,1)S(1)} %get-tuple-element.76) | copy-start | bytes 1572868
  96.4 2.5 collective-permute-start.5
  97.0 1.9 collective-permute-start.6
  97.1 5.1 collective-permute-start.7
  106.8 452.2 %all-reduce.5.cloned.1.call-start = ((), (), s32[]{:S(2)}) async-start(), calls=%async_computation.4 | async-start | bytes 8388608 | tf_op jit(solution)/shard_map/psum | solution.py:435
  112.2 4.8 copy-start.6
  112.2 4.8 copy-start.21
  112.2 4.8 copy-start.31
  112.2 4.8 copy-start.50
  163.0 42.6 %copy-start.19 = (bf16[128,512]{1,0:T(8,128)(2,1)S(1)}, bf16[128,512]{1,0:T(8,128)(2,1)}, u32[]{:S(2)}) copy-start(bf16[128,512]{1,0:T(8,128)(2,1)} %copy-done.18) | copy-start | bytes 393220
  204.9 4.3 collective-permute-start.12
  204.9 2.8 collective-permute-start.10
  205.5 2.3 collective-permute-start.9
  205.6 3.6 collective-permute-start.11
  442.7 6.8 %copy-start.7 = (bf16[2048,1024]{1,0:T(8,128)(2,1)S(1)}, bf16[2048,1024]{1,0:T(8,128)(2,1)}, u32[]{:S(2)}) copy-start(bf16[2048,1024]{1,0:T(8,128)(2,1)} %get-tuple-element.38) | copy-start | bytes 12582916
  559.0 5.5 copy-start.17
  (43 other events, 110.3 us)
Sparse Core Ops, SparseCore 0:
  106.9 277.2 all-reduce.6
  390.5 168.4 all-reduce.4

commit v2 on v1

--- a/solution.py
+++ b/solution.py
@@ -218,6 +218,29 @@
     unsort_tiles(load_q, n_q, give_q)
     unsort_tiles(load_k, n_k, give_k)
     unsort_tiles(load_v, n_k, give_v)
+
+
+def head_grad_kernel(x_ref, dq_ref, dk_ref, dv_ref, m_ref, c_ref, *, n_q):
+    low, f32 = jnp.bfloat16, jnp.float32
+    m_ref[...] = jnp.zeros(m_ref.shape, f32)
+    c_ref[...] = jnp.zeros(c_ref.shape, f32)
+    ones = jnp.ones((8, 256), low)
+
+    def two_tiles(u, carry):
+        x = jnp.concatenate([x_ref[2 * u], x_ref[2 * u + 1]], axis=0).astype(f32)
+        normed = normalize(x)[0].astype(low)
+        grads = jnp.concatenate(
+            [
+                jnp.concatenate([ref[2 * u], ref[2 * u + 1]], axis=1)
+                for ref in (dq_ref, dk_ref, dv_ref)
+            ],
+            axis=0,
+        )
+        m_ref[...] += dot(grads, normed)
+        c_ref[...] += dot(ones, grads, 1, 1)
+        return carry
+
+    lax.fori_loop(0, n_q // 2, two_tiles, 0)
 
 
 def on_chip(n):
@@ -278,6 +301,129 @@
     )(info, qs, ks, vs, att, log_total, grad_tiles)
 
 
+def head_grad(x_tiles, dq, dk, dv):
+    n_q, _, width = x_tiles.shape
+    f32 = jnp.float32
+    return pl.pallas_call(
+        partial(head_grad_kernel, n_q=n_q),
+        in_specs=on_chip(4),
+        out_specs=tuple(on_chip(2)),
+        out_shape=(
+            jax.ShapeDtypeStruct((3 * HEAD_DIM, width), f32),
+            jax.ShapeDtypeStruct((8, 3 * HEAD_DIM), f32),
+        ),
+        compiler_params=pltpu.CompilerParams(vmem_limit_bytes=48 << 20),
+        name="head_grad",
+    )(x_tiles, dq, dk, dv)
+
+
+def place_sums_kernel(at_a_ref, at_b_ref, a_ref, b_ref, fc1_ref, out_ref, small_ref):
+    f32 = jnp.float32
+    cut_at = a_ref.shape[2]
+    rest = fc1_ref.shape[2] - cut_at
+    width = out_ref.shape[2]
+    fc1_ref[0, :, :cut_at] = a_ref[0].astype(f32)
+    fc1_ref[0, :, cut_at:] = b_ref[0, :, :rest].astype(f32)
+    out_ref[0] = b_ref[0, :, rest : rest + width].astype(f32)
+    small_ref[0] = b_ref[0, :, rest + width :].astype(f32)
+
+
+def place_sums(at_a, at_b, sum_a, sum_b, hidden_width, width):
+    blocks, n, wide_a = sum_a.shape
+    wide_b = sum_b.shape[2]
+    small = wide_a + wide_b - hidden_width - width
+    f32 = jnp.float32
+
+    def out_block(w):
+        return pl.BlockSpec((1, n, w), lambda r, at_a_ref, at_b_ref: (r, 0, 0))
+
+    return pl.pallas_call(
+        place_sums_kernel,
+        grid_spec=pltpu.PrefetchScalarGridSpec(
+            num_scalar_prefetch=2,
+            grid=(blocks,),
+            in_specs=[
+                pl.BlockSpec((1, n, wide_a), lambda r, at_a_ref, at_b_ref: (at_a_ref[r], 0, 0)),
+                pl.BlockSpec((1, n, wide_b), lambda r, at_a_ref, at_b_ref: (at_b_ref[r], 0, 0)),
+            ],
+            out_specs=(out_block(hidden_width), out_block(width), out_block(small)),
+        ),
+        out_shape=(
+            jax.ShapeDtypeStruct((blocks, n, hidden_width), f32),
+            jax.ShapeDtypeStruct((blocks, n, width), f32),
+            jax.ShapeDtypeStruct((blocks, n, small), f32),
+        ),
+        name="place_sums",
+    )(at_a, at_b, sum_a, sum_b)
+
+
+def place_qkv_kernel(
+    at_l_ref, at_r_ref, left_ref, right_ref, weight_ref, gain_ref, bias_ref,
+    grad_ref, gain_sum_ref, bias_sum_ref, scale_ref,
+):
+    f32 = jnp.float32
+    block = pl.program_id(0)
+    per = HEADS // 2
+    which = block // per
+    first = 2 * (block % per)
+    n_rows = 3 * HEAD_DIM
+    half = left_ref.shape[2]
+    row = lax.broadcasted_iota(jnp.int32, (16, 128), 0)
+    lane = lax.broadcasted_iota(jnp.int32, (1, 128), 1)
+
+    def extra_row(head, i):
+        rows = left_ref[at_l_ref[head], n_rows : n_rows + 16, :128].astype(f32)
+        return jnp.sum(jnp.where((row == i) | (row == i + 4), rows, 0.0), axis=0, keepdims=True)
+
+    @pl.when(block == 0)
+    def _():
+        gain_sum_ref[...] = jnp.zeros(gain_sum_ref.shape, f32)
+        bias_sum_ref[...] = jnp.zeros(bias_sum_ref.shape, f32)
+        for head in range(HEADS):
+            scale_ref[head : head + 1, :] = extra_row(head, 3)
+
+    columns = jnp.where(lane < HEAD_DIM, extra_row(first, which), extra_row(first + 1, which))
+    rows = pl.ds(pl.multiple_of(which * HEAD_DIM, HEAD_DIM), HEAD_DIM)
+    for side, (ref, at_ref) in enumerate(((left_ref, at_l_ref), (right_ref, at_r_ref))):
+        sums = jnp.concatenate(
+            [ref[at_ref[first], rows, :], ref[at_ref[first + 1], rows, :]], axis=0
+        ).astype(f32).T
+        d = slice(side * half, side * half + half)
+        weight = weight_ref[d, :].astype(f32)
+        grad_ref[d, :] = sums * gain_ref[d, :] + bias_ref[d, :] * columns
+        gain_sum_ref[d, :] += weight * sums
+        bias_sum_ref[d, :] += weight * columns
+
+
+def place_qkv(at_l, at_r, left, right, weight, gain, bias):
+    wide, n_columns = weight.shape
+    f32 = jnp.float32
+
+    def whole(shape):
+        return pl.BlockSpec(shape, lambda i, at_l_ref, at_r_ref: (0,) * len(shape))
+
+    column = pl.BlockSpec((wide, 128), lambda i, at_l_ref, at_r_ref: (0, i))
+    return pl.pallas_call(
+        place_qkv_kernel,
+        grid_spec=pltpu.PrefetchScalarGridSpec(
+            num_scalar_prefetch=2,
+            grid=(n_columns // 128,),
+            in_specs=[
+                whole(left.shape), whole(right.shape), column, whole((wide, 1)), whole((wide, 1)),
+            ],
+            out_specs=(column, whole((wide, 128)), whole((wide, 128)), whole((HEADS, 128))),
+        ),
+        out_shape=(
+            jax.ShapeDtypeStruct((wide, n_columns), f32),
+            jax.ShapeDtypeStruct((wide, 128), f32),
+            jax.ShapeDtypeStruct((wide, 128), f32),
+            jax.ShapeDtypeStruct((HEADS, 128), f32),
+        ),
+        compiler_params=pltpu.CompilerParams(vmem_limit_bytes=48 << 20),
+        name="place_qkv",
+    )(at_l, at_r, left, right, weight, gain[:, None], bias[:, None])
+
+
 def from_member(value, s, size):
     return lax.ppermute(value, "fsdp", [((i + s) % size, i) for i in range(size)])
 
@@ -315,6 +461,64 @@
     for s in range(1, size):
         pieces.append(from_member(part_of(value, size - s, me, size, 1), s, size))
     return jnp.concatenate(pieces, axis=0)
+
+
+def swapped(value, stride, groups):
+    return lax.ppermute(value, "ctx", [(i, i ^ stride) for i in range(groups)])
+
+
+def half_of(value, which, axis=0):
+    n = value.shape[axis] // 2
+    return lax.dynamic_slice_in_dim(value, which * n, n, axis)
+
+
+def bit_of(member, stride):
+    return (member // stride) % 2
+
+
+def plane_sum(product, sent, strides, member, groups):
+    low, f32 = jnp.bfloat16, jnp.float32
+    got = swapped(sent, strides[0], groups)
+    total = (product(bit_of(member, strides[0])) + got.astype(f32)).astype(low)
+    for stride in strides[1:]:
+        bit = bit_of(member, stride)
+        got = swapped(half_of(total, 1 - bit), stride, groups)
+        total = (half_of(total, bit).astype(f32) + got.astype(f32)).astype(low)
+    return total
+
+
+def plane_join(value, strides, groups):
+    for stride in strides:
+        value = jnp.concatenate([value, swapped(value, stride, groups)], axis=0)
+    return value
+
+
+def from_line(value, k, plane, groups):
+    return lax.ppermute(value, "ctx", [(i, (i + k * plane) % groups) for i in range(groups)])
+
+
+def line_sum(value, line, plane, groups):
+    lines = groups // plane
+    n = value.shape[0] // lines
+    total = lax.dynamic_slice_in_dim(value, line * n, n, 0).astype(jnp.float32)
+    for k in range(1, lines):
+        chunk = lax.dynamic_slice_in_dim(value, ((line + k) % lines) * n, n, 0)
+        total = total + from_line(chunk, k, plane, groups).astype(jnp.float32)
+    return total.astype(value.dtype)
+
+
+def line_join(value, plane, groups):
+    pieces = [value] + [from_line(value, k, plane, groups) for k in range(1, groups // plane)]
+    return jnp.concatenate(pieces, axis=0)
+
+
+def joined_places(lines_of, bits_of, order, member, line, lines, plane):
+    place = (line - lines_of) % lines
+    step = lines
+    for i in order:
+        place = place + (bits_of[i] ^ bit_of(member, 1 << i)) * step
+        step = 2 * step
+    return place.astype(jnp.int32)
 
 
 def local(
@@ -333,8 +537,17 @@
     head_groups = [[g * HEADS + i for i in range(HEADS)] for g in range(copies)]
     copy_groups = [[g * HEADS + i for g in range(copies)] for i in range(HEADS)]
     head = member % HEADS
+    lines = 1
+    while lines * lines < groups:
+        lines = 2 * lines
+    plane = groups // lines
+    line = member // plane
+    strides = [1 << i for i in range(plane.bit_length() - 1)]
     info = jnp.concatenate([(member // HEADS)[None].astype(jnp.int32), doc_lengths[0]])
 
+    x_tiles = lax.all_gather(
+        x_low, "ctx", axis=0, axis_index_groups=None if copies == 1 else head_groups
+    )
     qkv_parts = gather_parts(qkv_weight, size)
     small = jnp.concatenate(
         [norm_gain.reshape(-1), norm_bias.reshape(-1), mid_gain, mid_bias, head_scale]
@@ -395,22 +608,84 @@
         grad_mixed, norm_mid, inv_mid, mid_gains
     )
     grad_hidden = gelu_back(grad_active)[0].astype(low)
-    fc1_grad = dot(
-        all_tokens_own(normed_two, me, size), all_tokens(grad_hidden, size), 0, 0
-    ).astype(low)
-    fc2_sum, fc1_sum = lax.psum((fc2_grad, fc1_grad), "ctx")
+    fc2_grad, grad_hidden = lax.optimization_barrier((fc2_grad, grad_hidden))
+    fc2_sum = lax.psum(fc2_grad, "ctx")
+    fc1_left = all_tokens_own(normed_two, me, size)
+    fc1_right = all_tokens(grad_hidden, size)
     grad_two = natural([dot(grad_hidden, part, 1, 1) for part in fc1_parts], me, 1)
     grad_mid_in, gain_two, bias_two = norm_backward(grad_two, norm_two, inv_two, gains[2])
     grad_middle = grad_top + grad_mid_in
     grad_branch_f, gain_att, bias_att = norm_backward(grad_middle, norm_att, inv_att, gains[1])
     grad_branch = grad_branch_f.astype(low)
-    out_grad = dot(
-        all_tokens_own(scaled_t.T, me, size), all_tokens(grad_branch, size), 0, 0
-    ).astype(low)
+    out_left = all_tokens_own(scaled_t.T, me, size)
+    out_right = all_tokens(grad_branch, size)
+
+    squares = jnp.stack(
+        [jnp.sum(result * result), jnp.sum(attn_out * attn_out), jnp.sum(ffn_out * ffn_out)]
+    )
+    norms = jnp.stack([gain_att, gain_two, bias_att, bias_two])
+    mids = jnp.stack([mid_gain_grad, mid_bias_grad])
+
+    def packed(s):
+        return jnp.concatenate(
+            [
+                part_of(norms, s, me, size, 1).reshape(-1, 128),
+                part_of(mids, s, me, size, 1).reshape(-1, 128),
+                jnp.pad(squares[None], ((0, 7), (0, 125))),
+            ],
+            axis=0,
+        )
+
+    small_rows = packed(0)
+    for s in range(1, size):
+        small_rows = small_rows + from_member(packed(size - s), s, size)
+    own_rows = fc1_weight.shape[0]
+    n_small = small_rows.shape[0]
+    small_block = jnp.concatenate([small_rows, jnp.zeros((own_rows - n_small, 128), f32)], axis=0)
+
+    cut_at = 5 * hidden_width // 8
+
+    def product_a(w):
+        return dot(half_of(fc1_left, w, 1), fc1_right[:, :cut_at], 0, 0)
+
+    def product_b(w):
+        return jnp.concatenate(
+            [
+                dot(half_of(fc1_left, w, 1), fc1_right[:, cut_at:], 0, 0),
+                dot(half_of(out_left, w, 1), out_right, 0, 0),
+                half_of(small_block, w),
+            ],
+            axis=1,
+        )
+
+    sent_a = product_a(1 - bit_of(member, strides[0])).astype(low)
+    sent_a, grad_branch = lax.optimization_barrier((sent_a, grad_branch))
+    sent_b = product_b(1 - bit_of(member, strides[-1])).astype(low)
+
     grad_scaled_t = natural([dot(part, grad_branch, 1, 1) for part in out_parts], me, 0)
     grad_att = (
         grad_scaled_t.reshape(HEADS, HEAD_DIM, rows) * head_scales[:, None, None]
     ).astype(low)
+    sent_b, grad_att = lax.optimization_barrier((sent_b, grad_att))
+    sum_a = plane_sum(product_a, sent_a, strides, member, groups)
+    sum_b = plane_sum(product_b, sent_b, strides[::-1], member, groups)
+    both = line_sum(jnp.concatenate([sum_a, sum_b], axis=1), line, plane, groups)
+    both = line_join(both, plane, groups)
+    n_block = own_rows // groups
+    bits = range(len(strides))
+    block = jnp.arange(groups)
+    block_bits = [block // lines // (1 << i) % 2 for i in bits]
+    sum_a = plane_join(both[:, :cut_at], strides[::-1], groups).reshape(groups, n_block, -1)
+    sum_b = plane_join(both[:, cut_at:], strides, groups).reshape(groups, n_block, -1)
+    at_a = joined_places(
+        block % lines, block_bits[::-1], bits[::-1], member, line, lines, plane
+    )
+    at_b = joined_places(block % lines, block_bits, bits, member, line, lines, plane)
+    fc1_sum, out_sum, total = place_sums(at_a, at_b, sum_a, sum_b, hidden_width, width)
+    fc1_sum = fc1_sum.reshape(own_rows, hidden_width)
+    out_sum = out_sum.reshape(own_rows, width)
+    total = total.reshape(own_rows, 128)[:n_small].reshape(-1)
+
     grad_tiles = lax.all_to_all(grad_att, "ctx", 0, 0, tiled=True, axis_index_groups=head_groups)
     dq, dk, dv, delta_sum = attend_back(
         info, qs, ks, vs, att, log_total, grad_tiles, low if copies == 1 else f32
@@ -422,46 +697,78 @@
             ).astype(low)
             for d in (dk, dv)
         )
+
+    head_sums, column_sums = head_grad(x_tiles, dq, dk, dv)
+    my_scale_grad = jnp.sum(delta_sum) / my_scale[0]
+    extra = jnp.concatenate(
+        [column_sums[0].reshape(3, HEAD_DIM), jnp.full((1, HEAD_DIM), my_scale_grad)], axis=0
+    )
+    if copies > 1:
+        head_sums, extra = (
+            lax.psum(d, "ctx", axis_index_groups=copy_groups) for d in (head_sums, extra)
+        )
+    wide = norm_gain.shape[1]
+    n_head_rows = head_sums.shape[0]
+    extra = jnp.pad(jnp.concatenate([extra, extra], axis=1), ((0, 12), (0, wide - 2 * HEAD_DIM)))
+
+    def with_extra(sums, more):
+        high = more.astype(low)
+        rest_of = (more - high.astype(f32)).astype(low)
+        both_parts = high + jnp.roll(rest_of, 4, axis=0)
+        return jnp.concatenate([sums.astype(low), both_parts], axis=0)
+
+    own_sums = part_of(head_sums, 0, me, size, 1)
+    own_extra = extra
+    for s in range(1, size):
+        got = from_member(
+            with_extra(part_of(head_sums, size - s, me, size, 1), extra), s, size
+        ).astype(f32)
+        own_sums = own_sums + got[:n_head_rows]
+        got = got[n_head_rows:]
+        own_extra = own_extra + jnp.pad(got[:4] + got[4:8], ((0, 12), (0, 0)))
+    payload = lax.optimization_barrier(with_extra(own_sums, own_extra))
+    heads = jnp.arange(HEADS)
+    if copies > 1:
+        every = lax.all_gather(payload, "ctx", axis=0, axis_index_groups=head_groups)
+        left, right = every[:, :, : wide // 2], every[:, :, wide // 2 :]
+        at_l = at_r = heads.astype(jnp.int32)
+    else:
+        on_line = line_join(payload, plane, groups)
+        left = plane_join(on_line[:, : wide // 2], strides, groups)
+        right = plane_join(on_line[:, wide // 2 :], strides[::-1], groups)
+        left, right = (d.reshape(HEADS, n_head_rows + 16, wide // 2) for d in (left, right))
+        head_bits = [bit_of(heads, stride) for stride in strides]
+        at_l = joined_places(heads // plane, head_bits, bits, member, line, lines, plane)
+        at_r = joined_places(heads // plane, head_bits, bits[::-1], member, line, lines, plane)
+    qkv_sum, gain_parts, bias_parts, scales = place_qkv(
+        at_l, at_r, left, right, qkv_weight, norm_gain[0].astype(f32), norm_bias[0].astype(f32)
+    )
+    gain_one, bias_one = jnp.sum(gain_parts, axis=1), jnp.sum(bias_parts, axis=1)
+    scale_sum = part_of(scales[:, 0], 0, me, size, 0)
+
     grads_out = jnp.stack([dq, dk, dv], axis=1)
     grad_proj_t = lax.all_to_all(
         grads_out, "ctx", 0, 0, tiled=True, axis_index_groups=head_groups
     ).transpose(1, 0, 2, 3).reshape(3 * width, rows)
-    qkv_grad = dot(
-        all_tokens_own(normed_one, me, size), all_tokens(grad_proj_t.T, size), 0, 0
-    ).astype(low)
-    fc2_sum, fc1_sum, out_grad, qkv_grad = lax.optimization_barrier(
-        (fc2_sum, fc1_sum, out_grad, qkv_grad)
-    )
-    out_sum, qkv_sum = lax.psum((out_grad, qkv_grad), "ctx")
     grad_one = natural([dot(grad_proj_t, part, 0, 1) for part in qkv_parts], me, 1)
-    grad_first, gain_one, bias_one = norm_backward(grad_one, norm_one, inv_one, gains[0])
+    grad_first = norm_backward(grad_one, norm_one, inv_one, gains[0])[0]
     input_grad = (grad_middle + grad_first).astype(low)[None]
 
-    my_scale_grad = jnp.sum(delta_sum) / my_scale[0]
-    scale_grad = jnp.where(jnp.arange(HEADS) == head, my_scale_grad, 0.0)
-    squares = jnp.stack(
-        [jnp.sum(result * result), jnp.sum(attn_out * attn_out), jnp.sum(ffn_out * ffn_out)]
-    )
-    packed = jnp.concatenate(
-        [gain_one, gain_att, gain_two, bias_one, bias_att, bias_two,
-         mid_gain_grad, mid_bias_grad, scale_grad, squares]
-    )
-    total = lax.psum(packed, ("ctx", "fsdp"))
-    gain_grad = part_of(total[: 3 * width].reshape(3, width), 0, me, size, 1)
-    bias_grad = part_of(total[3 * width : 6 * width].reshape(3, width), 0, me, size, 1)
-    at = 6 * width
-    mid_gain_sum = part_of(total[at : at + hidden_width], 0, me, size, 0)
-    at = at + hidden_width
-    mid_bias_sum = part_of(total[at : at + hidden_width], 0, me, size, 0)
-    at = at + hidden_width
-    scale_sum = part_of(total[at : at + HEADS], 0, me, size, 0)
-    rms_values = jnp.sqrt(total[at + HEADS :] / (rows * groups * size * width))
+    own_norms = total[: 4 * wide].reshape(4, wide)
+    gain_grad = jnp.stack([gain_one, own_norms[0], own_norms[1]])
+    bias_grad = jnp.stack([bias_one, own_norms[2], own_norms[3]])
+    at = 4 * wide
+    n_own = mid_gain.shape[0]
+    mid_gain_sum = total[at : at + n_own]
+    mid_bias_sum = total[at + n_own : at + 2 * n_own]
+    at = at + 2 * n_own
+    rms_values = jnp.sqrt(total[at : at + 3] / (rows * groups * size * width))
     return (
         result.astype(low)[None],
         input_grad,
-        qkv_sum.astype(f32),
-        out_sum.astype(f32),
-        fc1_sum.astype(f32),
+        qkv_sum,
+        out_sum,
+        fc1_sum,
         fc2_sum.astype(f32),
         gain_grad,
         bias_grad,

time: 577 us -> 467 us (0.81)
  blocking collectives: 109 us -> 0 us
  waiting for transfers between devices: 295 us -> 194 us
  starting transfers between devices: 16.1 us -> 53 us
  Pallas kernels: 22.6 us -> 57.1 us
  other arithmetic: 37.8 us -> 46.6 us
  local copies, waits for them, and re-layouts: 20.4 us -> 29 us
  matrix products: 55.6 us -> 63.3 us
    psum x2 -> x1, waiting for transfers between devices: 277 us -> 0.01 us  [local(): fc2_sum = lax.psum(fc2_grad, 'ctx')]
    ppermute x0 -> x21, waiting for transfers between devices: none -> 139 us  [the longest x9 111 us: from_line(): lax.ppermute(value, 'ctx', [(i, (i + k * plane) % groups) for i in range(...]
    all_to_all x2 -> x0, blocking collectives: 64.2 us -> none  [the longest x1 41.8 us: local(): lax.all_to_all(grads_out, 'ctx', 0, 0, tiled=True, axis_index_groups=head...]
    psum x1 -> x0, blocking collectives: 44.9 us -> none  [local(): total = lax.psum(packed, ('ctx', 'fsdp'))]
    pallas_call x0 -> x3, Pallas kernels: none -> 34.5 us  [the longest x1 17.3 us: place_qkv(): pl.pallas_call(place_qkv_kernel, grid_spec=pltpu.PrefetchScalarGridSpec(n...]
    ppermute x0 -> x21, starting transfers between devices: none -> 24.9 us  [the longest x12 13.3 us: swapped(): return lax.ppermute(value, 'ctx', [(i, i ^ stride) for i in range(groups)])]
    all_to_all x0 -> x2, waiting for transfers between devices: none -> 20.3 us  [the longest x1 20.3 us: local(): lax.all_to_all(grad_att, 'ctx', 0, 0, tiled=True, axis_index_groups=head_...]
    concatenate x0 -> x15, other arithmetic: none -> 12.4 us  [the longest x8 10.9 us: plane_join(): value = jnp.concatenate([value, swapped(value, stride, groups)], axis=0)]
  transfers between devices with their start and end apart: 17 -> 40, of which waited for: 6 -> 18; matrix products, arithmetic and copies ran while one was open for 15% -> 28% of each run, Pallas kernels for 4% -> 10%
where the time goes in v2:
time: 467 us; the launch traced here: 460 us
  waiting for transfers between devices  194 us (42%)
  matrix products  63.3 us (14%)
  Pallas kernels  57.1 us (12%)
  starting transfers between devices  53 us (11%)
  other arithmetic  46.6 us (10%)
  local copies, waits for them, and re-layouts  29 us (6%)
  between operations  17.1 us (4%)
    ppermute x9, waiting for transfers between devices, from_line(): lax.ppermute(value, 'ctx', [(i, (i + k * plane) % groups) for i in range(...  111 us
    dot_general x23, matrix products, dot(): lax.dot_general(a, b, (((ca,), (cb,)), ((), ())), preferred_element_type=...  63.3 us
    ppermute x12, waiting for transfers between devices, swapped(): return lax.ppermute(value, 'ctx', [(i, i ^ stride) for i in range(groups)])  28.6 us
    all_to_all x1, waiting for transfers between devices, local(): lax.all_to_all(by_head, 'ctx', 0, 0, tiled=True, axis_index_groups=head_g...  23.7 us
    all_to_all x1, waiting for transfers between devices, local(): lax.all_to_all(grad_att, 'ctx', 0, 0, tiled=True, axis_index_groups=head_...  20.3 us
    pallas_call x1, Pallas kernels, place_qkv(): pl.pallas_call(place_qkv_kernel, grid_spec=pltpu.PrefetchScalarGridSpec(n...  17.3 us
    ppermute x12, starting transfers between devices, swapped(): return lax.ppermute(value, 'ctx', [(i, i ^ stride) for i in range(groups)])  13.3 us
    pallas_call x1, Pallas kernels, place_sums(): pl.pallas_call(place_sums_kernel, grid_spec=pltpu.PrefetchScalarGridSpec(...  12.5 us
  transfers between devices with their start and end apart: 40, of which 18 were waited for; matrix products, arithmetic and copies ran while one was open for 28% of the time, Pallas kernels for 10%

profile of v2, /device:TPU:12, one launch (start us, length us, event | category | flops | bytes accessed | tf_op | source)
XLA Modules:
  0.0 460.4 jit_solution(3790237244212368044)
XLA Ops:
  26.1 7.2 %all-to-all-start = ((bf16[16,3,64,128]{3,2,1,0:T(8,128)(2,1)}), bf16[16,3,64,128]{3,2,1,0:T(8,128)(2,1)S(1)}, u32[]{:S(2)}, u32[]{:S(2)}) async-start(bf16[16,3,64,128]{3,2,1,0:T(8,128)(2,1)} %bitcast.138), calls=%async_computation | async-start | bytes 1572864 | tf_op jit(solution)/shard_map/all_to_all | solution.py:579
  34.6 4.7 %fusion.128 = f32[128,2048]{1,0:T(8,128)} fusion(bf16[2048,1024]{1,0:T(8,128)(2,1)} %param.18, bf16[1,128,1024]{2,1,0:T(8,128)(2,1)S(1)} %copy-done.22), kind=kOutput, calls=%fused_computation.331 | convolution fusion | flops 536870912 | bytes 5505024 | tf_op jit(solution)/shard_map/dot_general | solution.py:19
  40.6 23.7 %all-to-all-done.q_ref.kv_ref = bf16[16,3,64,128]{3,2,1,0:T(8,128)(2,1)S(1)} async-done(((bf16[16,3,64,128]{3,2,1,0:T(8,128)(2,1)}), bf16[16,3,64,128]{3,2,1,0:T(8,128)(2,1)S(1)}, u32[]{:S(2)}, u32[]{:S(2)}) %all-to-all-start) | async-done | bytes 786464 | tf_op jit(solution)/shard_map/all_to_all | solution.py:579
  64.2 11.3 %attend.1 = (bf16[16,64,128]{2,1,0:T(8,128)(2,1)}, f32[8,64,256]{2,1,0:T(8,128)S(1)}, f32[8,1,256]{2,1,0:T(1,128)S(1)}, bf16[8,64,256]{2,1,0:T(8,128)(2,1)S(1)},...) custom-call(s32[9]{0:T(128)S(1)} %pad_add_fusion.1.info_ref, f32[1]{0:T(128)} %dynamic_slice.136.hs_ref, ...), custom_call_target="tpu_custom_call" | custom-call | tf_op jit(solution)/shard_map/attend/pallas_call | solution.py:258
  75.5 5.1 %all-to-all-start.1 = ((bf16[16,64,128]{2,1,0:T(8,128)(2,1)}), bf16[16,64,128]{2,1,0:T(8,128)(2,1)S(1)}, u32[]{:S(2)}, u32[]{:S(2)}) async-start(bf16[16,64,128]{2,1,0:T(8,128)(2,1)} %get-tuple-element.37), calls=%async_computation.1 | async-start | bytes 524288 | tf_op jit(solution)/shard_map/all_to_all | solution.py:587
  81.0 4.7 %fusion.126 = f32[128,2048]{1,0:T(8,128)} fusion(bf16[2048,1024]{1,0:T(8,128)(2,1)} %collective-permute-done.4, bf16[1,128,1024]{2,1,0:T(8,128)(2,1)S(1)} %copy-done.22), kind=kOutput, calls=%fused_computation.329 | convolution fusion | flops 536870912 | bytes 5505024 | tf_op jit(solution)/shard_map/dot_general | solution.py:19
  85.7 10.3 %all-to-all-done.1 = bf16[16,64,128]{2,1,0:T(8,128)(2,1)S(1)} async-done(((bf16[16,64,128]{2,1,0:T(8,128)(2,1)}), bf16[16,64,128]{2,1,0:T(8,128)(2,1)S(1)}, u32[]{:S(2)}, u32[]{:S(2)}) %all-to-all-start.1) | async-done | bytes 262176 | tf_op jit(solution)/shard_map/all_to_all | solution.py:587
  101.8 3.8 fusion.130
  109.9 3.4 fusion.10
  115.7 3.9 fusion.145
  119.7 4.4 convolution_convert_fusion.1
  124.6 4.0 fusion.146
  128.7 3.8 fusion.147
  132.5 4.7 %multiply_reduce_fusion.7 = (f32[1024]{0:T(1024)S(1)}, f32[128]{0:T(128)S(1)}, f32[128]{0:T(128)S(1)}, f32[]{:T(128)}, f32[]{:T(128)}, /*index=5*/f32[1024]{0:T(...) fusion(f32[128,1024]{1,0:T(8,128)S(1)} %get-tuple-element.84, f32[128]{0:T(128)S(1)} %add_rsqrt_fusion.1, ...), kind=kOutput, calls=%fused_computation.121 | convolution fusion | flops 539358976 | bytes 7092236 | tf_op jit(solution)/shard_map/dot_general | solution.py:19
  160.4 6.1 %all-to-all-start.2 = ((bf16[16,64,128]{2,1,0:T(8,128)(2,1)}), bf16[16,64,128]{2,1,0:T(8,128)(2,1)S(1)}, u32[]{:S(2)}, u32[]{:S(2)}) async-start(bf16[16,64,128]{2,1,0:T(8,128)(2,1)} %multiply_convert_fusion), calls=%async_computation.2 | async-start | bytes 524288 | tf_op jit(solution)/shard_map/all_to_all | solution.py:689
  172.7 20.3 %all-to-all-done.2.go_ref = bf16[16,64,128]{2,1,0:T(8,128)(2,1)S(1)} async-done(((bf16[16,64,128]{2,1,0:T(8,128)(2,1)}), bf16[16,64,128]{2,1,0:T(8,128)(2,1)S(1)}, u32[]{:S(2)}, u32[]{:S(2)}) %all-to-all-start.2) | async-done | bytes 262176 | tf_op jit(solution)/shard_map/all_to_all | solution.py:689
  193.1 11.3 %attend_back.1 = (bf16[16,64,128]{2,1,0:T(8,128)(2,1)S(1)}, bf16[16,64,128]{2,1,0:T(8,128)(2,1)S(1)}, bf16[16,64,128]{2,1,0:T(8,128)(2,1)S(1)}, f32[1,256]{1,0:T(1,128)S(1)}) custom-call(s32[9]{0:T(128)S(1)} %pad_add_fusion.1.info_ref, bf16[8,64,256]{2,1,0:T(8,128)(2,1)S(1)} %get-tuple-element.39.qs_ref, bf16[8,64,256]{2,1,0:T(8,128)(2,1)S(1)} %get-tuple-element.40.ks_ref, ...), custom_call_target="tpu_custom_call" | custom-call | tf_op jit(solution)/shard_map/attend_back/pallas_call | solution.py:281
  205.4 6.2 %all-to-all-start.3 = ((bf16[16,3,64,128]{3,2,1,0:T(8,128)(2,1)}), bf16[16,3,64,128]{3,2,1,0:T(8,128)(2,1)}, u32[]{:S(2)}, u32[]{:S(2)}) async-start(bf16[16,3,64,128]{3,2,1,0:T(8,128)(2,1)} %copy.39), calls=%async_computation.3 | async-start | bytes 1572864 | tf_op jit(solution)/shard_map/all_to_all | solution.py:750
  215.8 4.6 %head_grad.1 = (f32[192,1024]{1,0:T(8,128)S(1)}, f32[8,192]{1,0:T(8,128)S(1)}) custom-call(bf16[16,128,1024]{2,1,0:T(8,128)(2,1)S(1)} %copy-done, bf16[16,64,128]{2,1,0:T(8,128)(2,1)S(1)} %get-tuple-element.46.dq_ref, bf16[16,64,128]{2,1,0:T(8,128)(2,1)S(1)} %get-tuple-element.47.dk_ref, bf16[16,64,128]{2,1,0:T(8,128)(2,1)S(1)} %get-tuple-element.48.dv_ref), custom_call_target="tpu_custom_call" | custom-call | tf_op jit(solution)/shard_map/head_grad/pallas_call | solution.py:307
  233.6 15.1 %collective-permute-done.13 = bf16[208,512]{1,0:T(8,128)(2,1)S(1)} collective-permute-done((bf16[208,512]{1,0:T(8,128)(2,1)S(1)}, bf16[208,512]{1,0:T(8,128)(2,1)S(1)}, u32[]{:S(2)}, u32[]{:S(2)}) %collective-permute-start.13) | collective-permute-done | bytes 213024 | tf_op jit(solution)/shard_map/ppermute | solution.py:497
  248.7 4.1 collective-permute-done.14
  258.3 3.2 fusion.148
  269.6 6.9 %collective-permute-done.24 = bf16[32,5248]{1,0:T(8,128)(2,1)S(1)} collective-permute-done((bf16[32,5248]{1,0:T(8,128)(2,1)S(1)}, bf16[32,5248]{1,0:T(8,128)(2,1)S(1)}, u32[]{:S(2)}, u32[]{:S(2)}) %collective-permute-start.24) | collective-permute-done | bytes 335904 | tf_op jit(solution)/shard_map/ppermute | solution.py:497
  276.5 26.6 %collective-permute-done.25 = bf16[32,5248]{1,0:T(8,128)(2,1)S(1)} collective-permute-done((bf16[32,5248]{1,0:T(8,128)(2,1)S(1)}, bf16[32,5248]{1,0:T(8,128)(2,1)S(1)}, u32[]{:S(2)}, u32[]{:S(2)}) %collective-permute-start.25) | collective-permute-done | bytes 335904 | tf_op jit(solution)/shard_map/ppermute | solution.py:497
  309.7 8.7 %collective-permute-done.27 = bf16[32,5248]{1,0:T(8,128)(2,1)S(1)} collective-permute-done((bf16[32,5248]{1,0:T(8,128)(2,1)S(1)}, bf16[32,5248]{1,0:T(8,128)(2,1)S(1)}, u32[]{:S(2)}, u32[]{:S(2)}) %collective-permute-start.27) | collective-permute-done | bytes 335904 | tf_op jit(solution)/shard_map/ppermute | solution.py:497
  318.4 38.4 %collective-permute-done.28 = bf16[32,5248]{1,0:T(8,128)(2,1)S(1)} collective-permute-done((bf16[32,5248]{1,0:T(8,128)(2,1)S(1)}, bf16[32,5248]{1,0:T(8,128)(2,1)S(1)}, u32[]{:S(2)}, u32[]{:S(2)}) %collective-permute-start.28) | collective-permute-done | bytes 335904 | tf_op jit(solution)/shard_map/ppermute | solution.py:497
  356.8 7.2 %collective-permute-done.29 = bf16[32,5248]{1,0:T(8,128)(2,1)S(1)} collective-permute-done((bf16[32,5248]{1,0:T(8,128)(2,1)S(1)}, bf16[32,5248]{1,0:T(8,128)(2,1)S(1)}, u32[]{:S(2)}, u32[]{:S(2)}) %collective-permute-start.29) | collective-permute-done | bytes 335904 | tf_op jit(solution)/shard_map/ppermute | solution.py:497
  369.9 12.2 %collective-permute-done.30 = bf16[128,2560]{1,0:T(8,128)(2,1)S(1)} collective-permute-done((bf16[128,2560]{1,0:T(8,128)(2,1)S(1)}, bf16[128,2560]{1,0:T(8,128)(2,1)S(1)}, u32[]{:S(2)}, u32[]{:S(2)}) %collective-permute-start.30) | collective-permute-done | bytes 655392 | tf_op jit(solution)/shard_map/ppermute | solution.py:467
  387.8 15.4 %collective-permute-done.19 = bf16[1664,256]{1,0:T(8,128)(2,1)S(1)} collective-permute-done((bf16[1664,256]{1,0:T(8,128)(2,1)S(1)}, bf16[1664,256]{1,0:T(8,128)(2,1)S(1)}, u32[]{:S(2)}, u32[]{:S(2)}) %collective-permute-start.19) | collective-permute-done | bytes 852000 | tf_op jit(solution)/shard_map/ppermute | solution.py:467
  404.4 17.3 %place_qkv.1 = (f32[512,3072]{1,0:T(8,128)}, f32[512,128]{1,0:T(8,128)S(1)}, f32[512,128]{1,0:T(8,128)S(1)}, f32[16,128]{1,0:T(8,128)S(1)}) custom-call(s32[16]{0:T(128)S(1)} %get-tuple-element.126.at_l_ref, s32[16]{0:T(128)S(1)} %get-tuple-element.125.at_r_ref, bf16[16,208,256]{2,1,0:T(8,128)(2,1)S(1)} %bitcast.143, bf16[16,208,256]{2,1,0:T(8,128)(2,1)S(1)} %bitcast.142, ...), custom_call_target="tpu_custom_call" | custom-call | tf_op jit(solution)/shard_map/place_qkv/pallas_call | solution.py:406
  422.7 6.7 %convert_element_type.217 = f32[2048,1024]{1,0:T(8,128)} convert(bf16[2048,1024]{1,0:T(8,128)(2,1)} %all-reduce.7.cloned.1.call-done) | non-fusion elementwise | flops 2097152 | bytes 12582912 | tf_op jit(solution)/shard_map/convert_element_type | solution.py:772
  436.0 12.5 %place_sums.1 = (f32[16,32,4096]{2,1,0:T(8,128)}, f32[16,32,1024]{2,1,0:T(8,128)}, f32[16,32,128]{2,1,0:T(8,128)}) custom-call(s32[16]{0:T(128)} %get-tuple-element.124.at_a_ref, s32[16]{0:T(128)} %get-tuple-element.123.at_b_ref, bf16[16,32,2560]{2,1,0:T(8,128)(2,1)} %bitcast.149, bf16[16,32,2688]{2,1,0:T(8,128)(2,1)} %bitcast.148), custom_call_target="tpu_custom_call" | custom-call | tf_op jit(solution)/shard_map/place_sums/pallas_call | solution.py:340
  (295 shorter events, 125.6 us)
Async XLA Ops:
  7.2 206.3 %all-gather.2.cloned.1.call-start = ((), (), s32[]{:S(2)}) async-start(), calls=%async_computation.4 | async-start | bytes 4456448 | tf_op jit(solution)/shard_map/all_gather | solution.py:548
  11.7 85.9 %collective-permute-start.2 = (bf16[512,1024]{1,0:T(8,128)(2,1)}, bf16[512,1024]{1,0:T(8,128)(2,1)}, u32[]{:S(2)}, u32[]{:S(2)}) collective-permute-start(bf16[512,1024]{1,0:T(8,128)(2,1)} %param.16), channel_id=1, source_target_pairs={{1,0},{0,1},{3,2},{2,3},{5,4},{4,5},{7,6},{6,7},{9,8},{8,9},{11,10... | collective-permute-start | bytes 3145736 | tf_op jit(solution)/shard_map/ppermute | solution.py:428
  11.7 90.0 %collective-permute-start.3 = (bf16[512,4096]{1,0:T(8,128)(2,1)}, bf16[512,4096]{1,0:T(8,128)(2,1)}, u32[]{:S(2)}, u32[]{:S(2)}) collective-permute-start(bf16[512,4096]{1,0:T(8,128)(2,1)} %param.17), channel_id=1, source_target_pairs={{1,0},{0,1},{3,2},{2,3},{5,4},{4,5},{7,6},{6,7},{9,8},{8,9},{11,10... | collective-permute-start | bytes 12582920 | tf_op jit(solution)/shard_map/ppermute | solution.py:428
  12.2 68.8 %collective-permute-start.4 = (bf16[2048,1024]{1,0:T(8,128)(2,1)}, bf16[2048,1024]{1,0:T(8,128)(2,1)}, u32[]{:S(2)}, u32[]{:S(2)}) collective-permute-start(bf16[2048,1024]{1,0:T(8,128)(2,1)} %param.18), channel_id=1, source_target_pairs={{1,0},{0,1},{3,2},{2,3},{5,4},{4,5},{7,6},{6,7},{9,8},{8,9},{11,10... | collective-permute-start | bytes 12582920 | tf_op jit(solution)/shard_map/ppermute | solution.py:428
  14.6 105.1 %collective-permute-start.6 = (bf16[128,1024]{1,0:T(8,128)(2,1)}, bf16[128,1024]{1,0:T(8,128)(2,1)}, u32[]{:S(2)}, u32[]{:S(2)}) collective-permute-start(bf16[128,1024]{1,0:T(8,128)(2,1)} %bitcast.156), channel_id=1, source_target_pairs={{1,0},{0,1},{3,2},{2,3},{5,4},{4,5},{7,6},{6,7},{9,8},{8,9},{11,10... | collective-permute-start | bytes 786440 | tf_op jit(solution)/shard_map/ppermute | solution.py:428
  26.1 38.2 %all-to-all-start = ((bf16[16,3,64,128]{3,2,1,0:T(8,128)(2,1)}), bf16[16,3,64,128]{3,2,1,0:T(8,128)(2,1)S(1)}, u32[]{:S(2)}, u32[]{:S(2)}) async-start(bf16[16,3,64,128]{3,2,1,0:T(8,128)(2,1)} %bitcast.138), calls=%async_computation | async-start | bytes 1572864 | tf_op jit(solution)/shard_map/all_to_all | solution.py:579
  75.5 20.4 %all-to-all-start.1 = ((bf16[16,64,128]{2,1,0:T(8,128)(2,1)}), bf16[16,64,128]{2,1,0:T(8,128)(2,1)S(1)}, u32[]{:S(2)}, u32[]{:S(2)}) async-start(bf16[16,64,128]{2,1,0:T(8,128)(2,1)} %get-tuple-element.37), calls=%async_computation.1 | async-start | bytes 524288 | tf_op jit(solution)/shard_map/all_to_all | solution.py:587
  80.6 342.1 %all-reduce.7.cloned.1.call-start = ((), (), s32[]{:S(2)}) async-start(), calls=%async_computation.5 | async-start | bytes 8388608 | tf_op jit(solution)/shard_map/psum | solution.py:612
  101.0 49.0 %collective-permute-start.7 = (bf16[128,512]{1,0:T(8,128)(2,1)}, bf16[128,512]{1,0:T(8,128)(2,1)S(1)}, u32[]{:S(2)}, u32[]{:S(2)}) collective-permute-start(bf16[128,512]{1,0:T(8,128)(2,1)} %get-tuple-element.103), channel_id=1, source_target_pairs={{1,0},{0,1},{3,2},{2,3},{5,4},{4,5},{7,6},{6,7},{9,8},{8,9},{11,10... | collective-permute-start | bytes 393224 | tf_op jit(solution)/shard_map/ppermute | solution.py:428
  115.5 29.6 %collective-permute-start.9 = (bf16[128,512]{0,1:T(8,128)(2,1)}, bf16[128,512]{0,1:T(8,128)(2,1)}, u32[]{:S(2)}, u32[]{:S(2)}) collective-permute-start(bf16[128,512]{0,1:T(8,128)(2,1)} %get-tuple-element.101), channel_id=1, source_target_pairs={{1,0},{0,1},{3,2},{2,3},{5,4},{4,5},{7,6},{6,7},{9,8},{8,9},{11,10... | collective-permute-start | bytes 393224 | tf_op jit(solution)/shard_map/ppermute | solution.py:428
  124.1 23.5 %collective-permute-start.8 = (bf16[128,4096]{1,0:T(8,128)(2,1)}, bf16[128,4096]{1,0:T(8,128)(2,1)}, u32[]{:S(2)}, u32[]{:S(2)}) collective-permute-start(bf16[128,4096]{1,0:T(8,128)(2,1)} %get-tuple-element.38), channel_id=1, source_target_pairs={{1,0},{0,1},{3,2},{2,3},{5,4},{4,5},{7,6},{6,7},{9,8},{8,9},{11,10... | collective-permute-start | bytes 3145736 | tf_op jit(solution)/shard_map/ppermute | solution.py:428
  153.1 67.8 %collective-permute-start.20 = (bf16[256,2560]{1,0:T(8,128)(2,1)}, bf16[256,2560]{1,0:T(8,128)(2,1)}, u32[]{:S(2)}, u32[]{:S(2)}) collective-permute-start(bf16[256,2560]{1,0:T(8,128)(2,1)} %convolution_convert_fusion), channel_id=1, source_target_pairs={{0,2},{2,0},{4,6},{6,4},{8,10},{10,8},{12,14},{14,12},{16,18},{18,... | collective-permute-start | bytes 3932168 | tf_op jit(solution)/shard_map/ppermute | solution.py:467
  160.4 32.7 %all-to-all-start.2 = ((bf16[16,64,128]{2,1,0:T(8,128)(2,1)}), bf16[16,64,128]{2,1,0:T(8,128)(2,1)S(1)}, u32[]{:S(2)}, u32[]{:S(2)}) async-start(bf16[16,64,128]{2,1,0:T(8,128)(2,1)} %multiply_convert_fusion), calls=%async_computation.2 | async-start | bytes 524288 | tf_op jit(solution)/shard_map/all_to_all | solution.py:689
  169.4 55.4 %collective-permute-start.22 = (bf16[256,2688]{1,0:T(8,128)(2,1)}, bf16[256,2688]{1,0:T(8,128)(2,1)}, u32[]{:S(2)}, u32[]{:S(2)}) collective-permute-start(bf16[256,2688]{1,0:T(8,128)(2,1)} %pad_maximum_fusion.4), channel_id=1, source_target_pairs={{0,4},{2,6},{4,0},{6,2},{8,12},{10,14},{12,8},{14,10},{16,20},{18,... | collective-permute-start | bytes 4128776 | tf_op jit(solution)/shard_map/ppermute | solution.py:467
  205.4 51.7 %all-to-all-start.3 = ((bf16[16,3,64,128]{3,2,1,0:T(8,128)(2,1)}), bf16[16,3,64,128]{3,2,1,0:T(8,128)(2,1)}, u32[]{:S(2)}, u32[]{:S(2)}) async-start(bf16[16,3,64,128]{3,2,1,0:T(8,128)(2,1)} %copy.39), calls=%async_computation.3 | async-start | bytes 1572864 | tf_op jit(solution)/shard_map/all_to_all | solution.py:750
  224.3 38.5 %collective-permute-start.21 = (bf16[128,2560]{1,0:T(8,128)(2,1)}, bf16[128,2560]{1,0:T(8,128)(2,1)}, u32[]{:S(2)}, u32[]{:S(2)}) collective-permute-start(bf16[128,2560]{1,0:T(8,128)(2,1)} %constant_dynamic-slice_fusion.8), channel_id=1, source_target_pairs={{0,4},{2,6},{4,0},{6,2},{8,12},{10,14},{12,8},{14,10},{16,20},{18,... | collective-permute-start | bytes 1966088 | tf_op jit(solution)/shard_map/ppermute | solution.py:467
  226.8 21.9 %collective-permute-start.13 = (bf16[208,512]{1,0:T(8,128)(2,1)S(1)}, bf16[208,512]{1,0:T(8,128)(2,1)S(1)}, u32[]{:S(2)}, u32[]{:S(2)}) collective-permute-start(bf16[208,512]{1,0:T(8,128)(2,1)S(1)} %pad_maximum_fusion.19), channel_id=1, source_target_pairs={{0,8},{2,10},{4,12},{6,14},{8,16},{10,18},{12,20},{14,22},{16,24},... | collective-permute-start | bytes 638984 | tf_op jit(solution)/shard_map/ppermute | solution.py:497
  228.3 24.5 %collective-permute-start.14 = (bf16[208,512]{1,0:T(8,128)(2,1)S(1)}, bf16[208,512]{1,0:T(8,128)(2,1)S(1)}, u32[]{:S(2)}, u32[]{:S(2)}) collective-permute-start(bf16[208,512]{1,0:T(8,128)(2,1)S(1)} %pad_maximum_fusion.19), channel_id=1, source_target_pairs={{0,16},{2,18},{4,20},{6,22},{8,24},{10,26},{12,28},{14,30},{16,0},... | collective-permute-start | bytes 638984 | tf_op jit(solution)/shard_map/ppermute | solution.py:497
  229.5 25.1 %collective-permute-start.15 = (bf16[208,512]{1,0:T(8,128)(2,1)S(1)}, bf16[208,512]{1,0:T(8,128)(2,1)S(1)}, u32[]{:S(2)}, u32[]{:S(2)}) collective-permute-start(bf16[208,512]{1,0:T(8,128)(2,1)S(1)} %pad_maximum_fusion.19), channel_id=1, source_target_pairs={{0,24},{2,26},{4,28},{6,30},{8,0},{10,2},{12,4},{14,6},{16,8},{18,... | collective-permute-start | bytes 638984 | tf_op jit(solution)/shard_map/ppermute | solution.py:497
  232.1 32.1 %collective-permute-start.23 = (bf16[128,2688]{1,0:T(8,128)(2,1)}, bf16[128,2688]{1,0:T(8,128)(2,1)}, u32[]{:S(2)}, u32[]{:S(2)}) collective-permute-start(bf16[128,2688]{1,0:T(8,128)(2,1)} %constant_dynamic-slice_fusion.7), channel_id=1, source_target_pairs={{0,2},{2,0},{4,6},{6,4},{8,10},{10,8},{12,14},{14,12},{16,18},{18,... | collective-permute-start | bytes 2064392 | tf_op jit(solution)/shard_map/ppermute | solution.py:467
  254.8 112.9 %collective-permute-start.18 = (bf16[832,256]{1,0:T(8,128)(2,1)S(1)}, bf16[832,256]{1,0:T(8,128)(2,1)}, u32[]{:S(2)}, u32[]{:S(2)}) collective-permute-start(bf16[832,256]{1,0:T(8,128)(2,1)S(1)} %get-tuple-element.93), channel_id=1, source_target_pairs={{0,4},{2,6},{4,0},{6,2},{8,12},{10,14},{12,8},{14,10},{16,20},{18,... | collective-permute-start | bytes 1277960 | tf_op jit(solution)/shard_map/ppermute | solution.py:467
  255.8 114.0 %collective-permute-start.16 = (bf16[832,256]{1,0:T(8,128)(2,1)S(1)}, bf16[832,256]{1,0:T(8,128)(2,1)S(1)}, u32[]{:S(2)}, u32[]{:S(2)}) collective-permute-start(bf16[832,256]{1,0:T(8,128)(2,1)S(1)} %get-tuple-element.94), channel_id=1, source_target_pairs={{0,2},{2,0},{4,6},{6,4},{8,10},{10,8},{12,14},{14,12},{16,18},{18,... | collective-permute-start | bytes 1277960 | tf_op jit(solution)/shard_map/ppermute | solution.py:467
  265.7 37.3 %collective-permute-start.25 = (bf16[32,5248]{1,0:T(8,128)(2,1)S(1)}, bf16[32,5248]{1,0:T(8,128)(2,1)S(1)}, u32[]{:S(2)}, u32[]{:S(2)}) collective-permute-start(bf16[32,5248]{1,0:T(8,128)(2,1)S(1)} %get-tuple-element.88), channel_id=1, source_target_pairs={{0,16},{2,18},{4,20},{6,22},{8,24},{10,26},{12,28},{14,30},{16,0},... | collective-permute-start | bytes 1007624 | tf_op jit(solution)/shard_map/ppermute | solution.py:497
  267.2 37.6 %collective-permute-start.26 = (bf16[32,5248]{1,0:T(8,128)(2,1)S(1)}, bf16[32,5248]{1,0:T(8,128)(2,1)S(1)}, u32[]{:S(2)}, u32[]{:S(2)}) collective-permute-start(bf16[32,5248]{1,0:T(8,128)(2,1)S(1)} %get-tuple-element.89), channel_id=1, source_target_pairs={{0,24},{2,26},{4,28},{6,30},{8,0},{10,2},{12,4},{14,6},{16,8},{18,... | collective-permute-start | bytes 1007624 | tf_op jit(solution)/shard_map/ppermute | solution.py:497
  305.1 51.7 %collective-permute-start.28 = (bf16[32,5248]{1,0:T(8,128)(2,1)S(1)}, bf16[32,5248]{1,0:T(8,128)(2,1)S(1)}, u32[]{:S(2)}, u32[]{:S(2)}) collective-permute-start(bf16[32,5248]{1,0:T(8,128)(2,1)S(1)} %add_convert_fusion.3), channel_id=1, source_target_pairs={{0,16},{2,18},{4,20},{6,22},{8,24},{10,26},{12,28},{14,30},{16,0},... | collective-permute-start | bytes 1007624 | tf_op jit(solution)/shard_map/ppermute | solution.py:497
  306.8 57.1 %collective-permute-start.29 = (bf16[32,5248]{1,0:T(8,128)(2,1)S(1)}, bf16[32,5248]{1,0:T(8,128)(2,1)S(1)}, u32[]{:S(2)}, u32[]{:S(2)}) collective-permute-start(bf16[32,5248]{1,0:T(8,128)(2,1)S(1)} %add_convert_fusion.3), channel_id=1, source_target_pairs={{0,24},{2,26},{4,28},{6,30},{8,0},{10,2},{12,4},{14,6},{16,8},{18,... | collective-permute-start | bytes 1007624 | tf_op jit(solution)/shard_map/ppermute | solution.py:497
  364.0 18.1 %collective-permute-start.30 = (bf16[128,2560]{1,0:T(8,128)(2,1)S(1)}, bf16[128,2560]{1,0:T(8,128)(2,1)S(1)}, u32[]{:S(2)}, u32[]{:S(2)}) collective-permute-start(bf16[128,2560]{1,0:T(8,128)(2,1)S(1)} %pad_maximum_fusion.14), channel_id=1, source_target_pairs={{0,4},{2,6},{4,0},{6,2},{8,12},{10,14},{12,8},{14,10},{16,20},{18,... | collective-permute-start | bytes 1966088 | tf_op jit(solution)/shard_map/ppermute | solution.py:467
  366.5 18.4 %collective-permute-start.32 = (bf16[128,2688]{1,0:T(8,128)(2,1)S(1)}, bf16[128,2688]{1,0:T(8,128)(2,1)S(1)}, u32[]{:S(2)}, u32[]{:S(2)}) collective-permute-start(bf16[128,2688]{1,0:T(8,128)(2,1)S(1)} %pad_maximum_fusion.11), channel_id=1, source_target_pairs={{0,2},{2,0},{4,6},{6,4},{8,10},{10,8},{12,14},{14,12},{16,18},{18,... | collective-permute-start | bytes 2064392 | tf_op jit(solution)/shard_map/ppermute | solution.py:467
  368.8 34.4 %collective-permute-start.19 = (bf16[1664,256]{1,0:T(8,128)(2,1)S(1)}, bf16[1664,256]{1,0:T(8,128)(2,1)S(1)}, u32[]{:S(2)}, u32[]{:S(2)}) collective-permute-start(bf16[1664,256]{1,0:T(8,128)(2,1)S(1)} %pad_maximum_fusion.9), channel_id=1, source_target_pairs={{0,2},{2,0},{4,6},{6,4},{8,10},{10,8},{12,14},{14,12},{16,18},{18,... | collective-permute-start | bytes 2555912 | tf_op jit(solution)/shard_map/ppermute | solution.py:467
  369.8 34.5 %collective-permute-start.17 = (bf16[1664,256]{1,0:T(8,128)(2,1)S(1)}, bf16[1664,256]{1,0:T(8,128)(2,1)S(1)}, u32[]{:S(2)}, u32[]{:S(2)}) collective-permute-start(bf16[1664,256]{1,0:T(8,128)(2,1)S(1)} %pad_maximum_fusion.8), channel_id=1, source_target_pairs={{0,4},{2,6},{4,0},{6,2},{8,12},{10,14},{12,8},{14,10},{16,20},{18,... | collective-permute-start | bytes 2555912 | tf_op jit(solution)/shard_map/ppermute | solution.py:467
  383.3 46.6 %collective-permute-start.31 = (bf16[256,2560]{1,0:T(8,128)(2,1)}, bf16[256,2560]{1,0:T(8,128)(2,1)}, u32[]{:S(2)}, u32[]{:S(2)}) collective-permute-start(bf16[256,2560]{1,0:T(8,128)(2,1)} %pad_maximum_fusion.6), channel_id=1, source_target_pairs={{0,2},{2,0},{4,6},{6,4},{8,10},{10,8},{12,14},{14,12},{16,18},{18,... | collective-permute-start | bytes 3932168 | tf_op jit(solution)/shard_map/ppermute | solution.py:467
  386.2 46.8 %collective-permute-start.33 = (bf16[256,2688]{1,0:T(8,128)(2,1)}, bf16[256,2688]{1,0:T(8,128)(2,1)}, u32[]{:S(2)}, u32[]{:S(2)}) collective-permute-start(bf16[256,2688]{1,0:T(8,128)(2,1)} %pad_maximum_fusion.5), channel_id=1, source_target_pairs={{0,4},{2,6},{4,0},{6,2},{8,12},{10,14},{12,8},{14,10},{16,20},{18,... | collective-permute-start | bytes 4128776 | tf_op jit(solution)/shard_map/ppermute | solution.py:467
  (52 other events, 433.1 us)
Sparse Core Ops, SparseCore 0:
  12.4 86.2 all-gather.1
  144.6 225.0 all-reduce.6

commit v3 on v1

--- a/solution.py
+++ b/solution.py
@@ -218,6 +218,29 @@
     unsort_tiles(load_q, n_q, give_q)
     unsort_tiles(load_k, n_k, give_k)
     unsort_tiles(load_v, n_k, give_v)
+
+
+def head_grad_kernel(x_ref, dq_ref, dk_ref, dv_ref, m_ref, c_ref):
+    low, f32 = jnp.bfloat16, jnp.float32
+
+    @pl.when(pl.program_id(0) == 0)
+    def _():
+        m_ref[...] = jnp.zeros(m_ref.shape, f32)
+        c_ref[...] = jnp.zeros(c_ref.shape, f32)
+
+    x = jnp.concatenate([x_ref[0], x_ref[1]], axis=0).astype(f32)
+    normed = normalize(x)[0].astype(low)
+    grads = jnp.concatenate(
+        [jnp.concatenate([ref[0], ref[1]], axis=1) for ref in (dq_ref, dk_ref, dv_ref)], axis=0
+    )
+    m_ref[...] += dot(grads, normed)
+    c_ref[...] += dot(jnp.ones((8, grads.shape[1]), low), grads, 1, 1)
+
+
+def takes(microseconds):
+    return pl.CostEstimate(
+        flops=0, transcendentals=0, bytes_accessed=int(microseconds * 3.2e6)
+    )
 
 
 def on_chip(n):
@@ -246,6 +269,7 @@
         ),
         scratch_shapes=[pltpu.VMEM((nk, TILE, HEAD_DIM), low)],
         compiler_params=pltpu.CompilerParams(vmem_limit_bytes=48 << 20),
+        cost_estimate=takes(10),
         name="attend",
     )(info, head_scale, q_tiles, kv_tiles)
 
@@ -274,8 +298,163 @@
             pltpu.VMEM((nk, TILE, HEAD_DIM), f32),
         ],
         compiler_params=pltpu.CompilerParams(vmem_limit_bytes=48 << 20),
+        cost_estimate=takes(10),
         name="attend_back",
     )(info, qs, ks, vs, att, log_total, grad_tiles)
+
+
+def stream_tiles(gathered, which):
+    _, _, rows, width = gathered.shape
+    return pl.BlockSpec((2, pl.Squeezed(), rows, width), lambda i: (i, which, 0, 0))
+
+
+def head_grad(gathered, dq, dk, dv):
+    width = gathered.shape[3]
+    f32 = jnp.float32
+    tiles = pl.BlockSpec((2, HEAD_DIM, 128), lambda i: (i, 0, 0))
+    return pl.pallas_call(
+        head_grad_kernel,
+        grid=(gathered.shape[0] // 2,),
+        in_specs=[stream_tiles(gathered, 0)] + [tiles] * 3,
+        out_specs=(
+            pl.BlockSpec((3 * HEAD_DIM, width), lambda i: (0, 0)),
+            pl.BlockSpec((8, 3 * HEAD_DIM), lambda i: (0, 0)),
+        ),
+        out_shape=(
+            jax.ShapeDtypeStruct((3 * HEAD_DIM, width), f32),
+            jax.ShapeDtypeStruct((8, 3 * HEAD_DIM), f32),
+        ),
+        cost_estimate=takes(8),
+        name="head_grad",
+    )(gathered, dq, dk, dv)
+
+
+def place_sums_kernel(
+    at_a_ref, at_b_ref, a_near_ref, a_far_ref, b_near_ref, b_far_ref, fc1_ref, out_ref
+):
+    f32 = jnp.float32
+    per, n, hidden_width = fc1_ref.shape
+    half = a_near_ref.shape[0]
+    cut_at = a_near_ref.shape[2]
+    rest = hidden_width - cut_at
+
+    def put_a(i, ref, at):
+        fc1_ref[i, :, :cut_at] = ref[at].astype(f32)
+
+    def put_b(i, ref, at):
+        fc1_ref[i, :, cut_at:] = ref[at, :, :rest].astype(f32)
+        out_ref[i] = ref[at, :, rest:].astype(f32)
+
+    for i in range(per):
+        r = pl.program_id(0) * per + i
+        for put, at, near, far in (
+            (put_a, at_a_ref[r], a_near_ref, a_far_ref),
+            (put_b, at_b_ref[r], b_near_ref, b_far_ref),
+        ):
+            pl.when(at < half)(partial(put, i, near, at))
+            pl.when(at >= half)(partial(put, i, far, at - half))
+
+
+def place_sums(at_a, at_b, sums_a, sums_b, hidden_width):
+    half, n, wide_a = sums_a[0].shape
+    wide_b = sums_b[0].shape[2]
+    blocks = 2 * half
+    per = 2
+    width = wide_a + wide_b - hidden_width
+    f32 = jnp.float32
+
+    def out_block(w):
+        return pl.BlockSpec((per, n, w), lambda r, at_a_ref, at_b_ref: (r, 0, 0))
+
+    return pl.pallas_call(
+        place_sums_kernel,
+        grid_spec=pltpu.PrefetchScalarGridSpec(
+            num_scalar_prefetch=2,
+            grid=(blocks // per,),
+            in_specs=on_chip(4),
+            out_specs=(out_block(hidden_width), out_block(width)),
+        ),
+        out_shape=(
+            jax.ShapeDtypeStruct((blocks, n, hidden_width), f32),
+            jax.ShapeDtypeStruct((blocks, n, width), f32),
+        ),
+        compiler_params=pltpu.CompilerParams(vmem_limit_bytes=48 << 20),
+        cost_estimate=takes(7),
+        name="place_sums",
+    )(at_a, at_b, *sums_a, *sums_b)
+
+
+def place_qkv_kernel(
+    at_l_ref, at_r_ref, left_ref, right_ref, weight_ref, gain_ref, bias_ref,
+    grad_ref, gain_sum_ref, bias_sum_ref, scale_ref, small_ref,
+):
+    f32 = jnp.float32
+    step = pl.program_id(0)
+    n_rows = 3 * HEAD_DIM
+    half = left_ref.shape[2]
+    pairs = grad_ref.shape[1] // 128
+    per = HEADS // 2 // pairs
+    which = step // per
+    row = lax.broadcasted_iota(jnp.int32, (16, 128), 0)
+    lane = lax.broadcasted_iota(jnp.int32, (1, 128), 1)
+
+    def extra_row(head, i):
+        rows = left_ref[at_l_ref[head], n_rows : n_rows + 16, :128].astype(f32)
+        return jnp.sum(jnp.where((row == i) | (row == i + 4), rows, 0.0), axis=0, keepdims=True)
+
+    @pl.when(step == 0)
+    def _():
+        gain_sum_ref[...] = jnp.zeros(gain_sum_ref.shape, f32)
+        bias_sum_ref[...] = jnp.zeros(bias_sum_ref.shape, f32)
+        for side, ref in enumerate((left_ref, right_ref)):
+            small_ref[:, side * half : side * half + half] = sum(
+                ref[head, n_rows + 16 :, :].astype(f32) for head in range(HEADS)
+            )
+        for head in range(HEADS):
+            scale_ref[head : head + 1, :] = extra_row(head, 3)
+
+    rows = pl.ds(pl.multiple_of(which * HEAD_DIM, HEAD_DIM), HEAD_DIM)
+    for pair in range(pairs):
+        first = 2 * (step % per * pairs + pair)
+        j = slice(pair * 128, pair * 128 + 128)
+        columns = jnp.where(lane < HEAD_DIM, extra_row(first, which), extra_row(first + 1, which))
+        for side, (ref, at_ref) in enumerate(((left_ref, at_l_ref), (right_ref, at_r_ref))):
+            sums = jnp.concatenate(
+                [ref[at_ref[first], rows, :], ref[at_ref[first + 1], rows, :]], axis=0
+            ).astype(f32).T
+            d = slice(side * half, side * half + half)
+            weight = weight_ref[d, j].astype(f32)
+            grad_ref[d, j] = sums * gain_ref[d, :] + bias_ref[d, :] * columns
+            gain_sum_ref[d, :] += weight * sums
+            bias_sum_ref[d, :] += weight * columns
+
+
+def place_qkv(at_l, at_r, left, right, weight, gain, bias):
+    wide, n_columns = weight.shape
+    f32 = jnp.float32
+    step = 512
+
+    def whole(shape):
+        return pl.BlockSpec(shape, lambda i, at_l_ref, at_r_ref: (0,) * len(shape))
+
+    column = pl.BlockSpec((wide, step), lambda i, at_l_ref, at_r_ref: (0, i))
+    outs = ((wide, 128), (wide, 128), (HEADS, 128), (16, wide))
+    return pl.pallas_call(
+        place_qkv_kernel,
+        grid_spec=pltpu.PrefetchScalarGridSpec(
+            num_scalar_prefetch=2,
+            grid=(n_columns // step,),
+            in_specs=[
+                whole(left.shape), whole(right.shape), column, whole((wide, 1)), whole((wide, 1)),
+            ],
+            out_specs=(column,) + tuple(whole(shape) for shape in outs),
+        ),
+        out_shape=(jax.ShapeDtypeStruct((wide, n_columns), f32),)
+        + tuple(jax.ShapeDtypeStruct(shape, f32) for shape in outs),
+        compiler_params=pltpu.CompilerParams(vmem_limit_bytes=48 << 20),
+        cost_estimate=takes(9),
+        name="place_qkv",
+    )(at_l, at_r, left, right, weight, gain[:, None], bias[:, None])
 
 
 def from_member(value, s, size):
@@ -315,6 +494,32 @@
     for s in range(1, size):
         pieces.append(from_member(part_of(value, size - s, me, size, 1), s, size))
     return jnp.concatenate(pieces, axis=0)
+
+
+def swapped(value, stride, groups):
+    return lax.ppermute(value, "ctx", [(i, i ^ stride) for i in range(groups)])
+
+
+def half_of(value, which, axis=0):
+    n = value.shape[axis] // 2
+    return lax.dynamic_slice_in_dim(value, which * n, n, axis)
+
+
+def bit_of(member, stride):
+    return (member // stride) % 2
+
+
+def from_line(value, k, plane, groups):
+    return lax.ppermute(value, "ctx", [(i, (i + k * plane) % groups) for i in range(groups)])
+
+
+def joined_places(lines_of, bits_of, order, member, line, lines, plane):
+    place = (line - lines_of) % lines
+    step = lines
+    for i in order:
+        place = place + (bits_of[i] ^ bit_of(member, 1 << i)) * step
+        step = 2 * step
+    return place.astype(jnp.int32)
 
 
 def local(
@@ -333,32 +538,43 @@
     head_groups = [[g * HEADS + i for i in range(HEADS)] for g in range(copies)]
     copy_groups = [[g * HEADS + i for g in range(copies)] for i in range(HEADS)]
     head = member % HEADS
+    lines = 1
+    while lines * lines < groups:
+        lines = 2 * lines
+    plane = groups // lines
+    line = member // plane
+    strides = [1 << i for i in range(plane.bit_length() - 1)]
     info = jnp.concatenate([(member // HEADS)[None].astype(jnp.int32), doc_lengths[0]])
 
-    qkv_parts = gather_parts(qkv_weight, size)
-    small = jnp.concatenate(
-        [norm_gain.reshape(-1), norm_bias.reshape(-1), mid_gain, mid_bias, head_scale]
-    )
-    smalls = gather_parts(small, size)
-    out_parts = gather_parts(out_weight, size)
-    fc1_parts = gather_parts(fc1_weight, size)
-    fc2_parts = gather_parts(fc2_weight, size)
-
-    n_norm = norm_gain.size
-    n_mid = mid_gain.size
-    n_head = head_scale.size
-    cut = [0, n_norm, 2 * n_norm, 2 * n_norm + n_mid, 2 * n_norm + 2 * n_mid, small.size]
-    fields = [[s[cut[i] : cut[i + 1]] for s in smalls] for i in range(5)]
-    gains = natural([f.reshape(3, -1) for f in fields[0]], me, 1).astype(f32)
-    biases = natural([f.reshape(3, -1) for f in fields[1]], me, 1).astype(f32)
-    mid_gains = natural(fields[2], me, 0).astype(f32)
-    mid_biases = natural(fields[3], me, 0).astype(f32)
-    head_scales = natural(fields[4], me, 0).astype(f32)
-    my_scale = lax.dynamic_slice_in_dim(head_scales, head, 1, 0)
+    gathered = lax.all_gather(
+        x_low[None],
+        "ctx", axis=0, axis_index_groups=None if copies == 1 else head_groups,
+    )
+    norm_vecs = jnp.concatenate([norm_gain, norm_bias], axis=0)
+    norm_vecs = natural(gather_parts(norm_vecs, size), me, 1).astype(f32)
+    norm_vecs, qkv_shard = lax.optimization_barrier((norm_vecs, qkv_weight))
+    gains, biases = norm_vecs[:3], norm_vecs[3:]
+    qkv_parts = gather_parts(qkv_shard, size)
 
     x_local = x_low.astype(f32)
     norm_one, inv_one = normalize(x_local)
     normed_one = (norm_one * gains[0] + biases[0]).astype(low)
+    normed_one, small, out_shard, fc1_shard, fc2_shard = lax.optimization_barrier(
+        (
+            normed_one, jnp.concatenate([mid_gain, mid_bias, head_scale]),
+            out_weight, fc1_weight, fc2_weight,
+        )
+    )
+    smalls = gather_parts(small, size)
+    out_parts = gather_parts(out_shard, size)
+    fc1_parts = gather_parts(fc1_shard, size)
+    fc2_parts = gather_parts(fc2_shard, size)
+    n_mid = mid_gain.size
+    cut = [0, n_mid, 2 * n_mid, small.size]
+    mid_gains, mid_biases, head_scales = (
+        natural([v[cut[i] : cut[i + 1]] for v in smalls], me, 0).astype(f32) for i in range(3)
+    )
+    my_scale = lax.dynamic_slice_in_dim(head_scales, head, 1, 0)
     project_t = sum(
         dot(qkv_parts[s], part_of(normed_one, s, me, size, 1), 0, 1) for s in range(size)
     ).astype(low)
@@ -389,29 +605,71 @@
 
     grad_ffn = cotangent[0]
     grad_top = grad_ffn.astype(f32)
-    fc2_grad = dot(all_tokens_own(mixed_in, me, size), all_tokens(grad_ffn, size), 0, 0).astype(low)
+    fc2_grad = dot(
+        all_tokens_own(mixed_in, me, size), all_tokens(grad_ffn, size), 0, 0
+    ).astype(low)
+    fc2_grad, norm_mid = lax.optimization_barrier((fc2_grad, norm_mid))
+    fc2_sum = lax.psum(fc2_grad, "ctx")
     grad_mixed = natural([dot(grad_ffn, part, 1, 1) for part in fc2_parts], me, 1)
     grad_active, mid_gain_grad, mid_bias_grad = norm_backward(
         grad_mixed, norm_mid, inv_mid, mid_gains
     )
     grad_hidden = gelu_back(grad_active)[0].astype(low)
-    fc1_grad = dot(
-        all_tokens_own(normed_two, me, size), all_tokens(grad_hidden, size), 0, 0
-    ).astype(low)
-    fc2_sum, fc1_sum = lax.psum((fc2_grad, fc1_grad), "ctx")
+    fc1_left = all_tokens_own(normed_two, me, size)
+    fc1_right = all_tokens(grad_hidden, size)
     grad_two = natural([dot(grad_hidden, part, 1, 1) for part in fc1_parts], me, 1)
     grad_mid_in, gain_two, bias_two = norm_backward(grad_two, norm_two, inv_two, gains[2])
     grad_middle = grad_top + grad_mid_in
     grad_branch_f, gain_att, bias_att = norm_backward(grad_middle, norm_att, inv_att, gains[1])
     grad_branch = grad_branch_f.astype(low)
-    out_grad = dot(
-        all_tokens_own(scaled_t.T, me, size), all_tokens(grad_branch, size), 0, 0
-    ).astype(low)
+    out_left = all_tokens_own(scaled_t.T, me, size)
+    out_right = all_tokens(grad_branch, size)
+
+    wide = norm_gain.shape[1]
+    squares = jnp.stack(
+        [jnp.sum(result * result), jnp.sum(attn_out * attn_out), jnp.sum(ffn_out * ffn_out)]
+    )
+    norms = jnp.stack([gain_att, gain_two, bias_att, bias_two])
+    mids = jnp.stack([mid_gain_grad, mid_bias_grad])
+    n_small = 4 + 2 * mid_gain.shape[0] // wide
+
+    def small_rows(s):
+        return jnp.concatenate(
+            [
+                part_of(norms, s, me, size, 1),
+                part_of(mids, s, me, size, 1).reshape(-1, wide),
+                jnp.pad(squares[None], ((0, 15 - n_small), (0, wide - 3))),
+            ],
+            axis=0,
+        )
+
+    own_rows = fc1_weight.shape[0]
+
+    cut_at = (hidden_width + width) // 2
+
+    def product_a(w):
+        return dot(half_of(fc1_left, w, 1), fc1_right[:, :cut_at], 0, 0)
+
+    def product_b(w):
+        return jnp.concatenate(
+            [
+                dot(half_of(fc1_left, w, 1), fc1_right[:, cut_at:], 0, 0),
+                dot(half_of(out_left, w, 1), out_right, 0, 0),
+            ],
+            axis=1,
+        )
+
+    sent_a = product_a(1 - bit_of(member, strides[0])).astype(low)
+    sent_b = product_b(1 - bit_of(member, strides[-1])).astype(low)
+
     grad_scaled_t = natural([dot(part, grad_branch, 1, 1) for part in out_parts], me, 0)
     grad_att = (
         grad_scaled_t.reshape(HEADS, HEAD_DIM, rows) * head_scales[:, None, None]
     ).astype(low)
     grad_tiles = lax.all_to_all(grad_att, "ctx", 0, 0, tiled=True, axis_index_groups=head_groups)
+    grad_tiles, sent_a, sent_b = lax.optimization_barrier((grad_tiles, sent_a, sent_b))
+    orders = (strides, strides[::-1])
+    got = [swapped(v, o[0], groups) for v, o in zip((sent_a, sent_b), orders)]
     dq, dk, dv, delta_sum = attend_back(
         info, qs, ks, vs, att, log_total, grad_tiles, low if copies == 1 else f32
     )
@@ -422,46 +680,139 @@
             ).astype(low)
             for d in (dk, dv)
         )
+
     grads_out = jnp.stack([dq, dk, dv], axis=1)
     grad_proj_t = lax.all_to_all(
         grads_out, "ctx", 0, 0, tiled=True, axis_index_groups=head_groups
     ).transpose(1, 0, 2, 3).reshape(3 * width, rows)
-    qkv_grad = dot(
-        all_tokens_own(normed_one, me, size), all_tokens(grad_proj_t.T, size), 0, 0
-    ).astype(low)
-    fc2_sum, fc1_sum, out_grad, qkv_grad = lax.optimization_barrier(
-        (fc2_sum, fc1_sum, out_grad, qkv_grad)
-    )
-    out_sum, qkv_sum = lax.psum((out_grad, qkv_grad), "ctx")
+    head_sums, column_sums = head_grad(gathered, dq, dk, dv)
+    my_scale_grad = jnp.sum(delta_sum) / my_scale[0]
+    extra = jnp.concatenate(
+        [column_sums[0].reshape(3, HEAD_DIM), jnp.full((1, HEAD_DIM), my_scale_grad)], axis=0
+    )
+    smalls_of = [small_rows(s) for s in range(size)]
+    if copies > 1:
+        head_sums, extra, smalls_of = (
+            lax.psum(d, "ctx", axis_index_groups=copy_groups)
+            for d in (head_sums, extra, smalls_of)
+        )
+    n_head_rows = head_sums.shape[0]
+    n_payload = n_head_rows + 32
+    extra = jnp.pad(jnp.concatenate([extra, extra], axis=1), ((0, 12), (0, wide - 2 * HEAD_DIM)))
+
+    def with_extra(sums, more, small_sums):
+        high = more.astype(low)
+        rest_of = (more - high.astype(f32)).astype(low)
+        both_parts = high + jnp.roll(rest_of, 4, axis=0)
+        return jnp.concatenate([sums.astype(low), both_parts, small_sums.astype(low)], axis=0)
+
+    own_sums = part_of(head_sums, 0, me, size, 1)
+    own_extra = extra
+    own_small = smalls_of[0]
+    for s in range(1, size):
+        more_rows = from_member(
+            with_extra(part_of(head_sums, size - s, me, size, 1), extra, smalls_of[size - s]),
+            s, size,
+        ).astype(f32)
+        own_sums = own_sums + more_rows[:n_head_rows]
+        own_small = own_small + more_rows[n_head_rows + 16 :]
+        more_rows = more_rows[n_head_rows : n_head_rows + 16]
+        own_extra = own_extra + jnp.pad(more_rows[:4] + more_rows[4:8], ((0, 12), (0, 0)))
+    payload = lax.optimization_barrier(with_extra(own_sums, own_extra, own_small))
+
+    got, payload = lax.optimization_barrier((got, payload))
+    sums = [
+        (product(bit_of(member, o[0])) + g.astype(f32)).astype(low)
+        for product, o, g in zip((product_a, product_b), orders, got)
+    ]
+    for step in range(1, len(strides)):
+        bits_now = [bit_of(member, o[step]) for o in orders]
+        got = [
+            swapped(half_of(v, 1 - bit), o[step], groups)
+            for v, bit, o in zip(sums, bits_now, orders)
+        ]
+        sums = [
+            (half_of(v, bit).astype(f32) + g.astype(f32)).astype(low)
+            for v, bit, g in zip(sums, bits_now, got)
+        ]
+    unit = jnp.concatenate(sums, axis=1)
+    one_chunk = own_rows // groups
+    sent = [
+        lax.dynamic_slice_in_dim(unit, (line + k) % lines * one_chunk, one_chunk, 0)
+        for k in range(lines)
+    ]
+    on_lines = [from_line(sent[k], k, plane, groups) for k in range(1, lines)]
+    by_permutes = copies == 1
+    unit = (sent[0].astype(f32) + sum(g.astype(f32) for g in on_lines)).astype(low)
+    got = [from_line(unit, k, plane, groups) for k in range(1, lines)]
+    on_line = [payload]
+    if by_permutes:
+        on_line += [from_line(payload, k, plane, groups) for k in range(1, lines)]
+    got, on_line = lax.optimization_barrier((got, on_line))
+    near = []
+    if by_permutes:
+        on_line = jnp.concatenate(on_line, axis=0)
+        near = [on_line[:, : wide // 2], on_line[:, wide // 2 :]]
+        near = [[v, swapped(v, o[0], groups)] for v, o in zip(near, orders)]
+    unit = jnp.concatenate([unit] + got, axis=0)
+    parts = [unit[:, :cut_at], unit[:, cut_at:]]
+    outward = orders[::-1]
+    for step in range(len(strides) - 1):
+        got = [swapped(v, o[step], groups) for v, o in zip(parts, outward)]
+        got, near = lax.optimization_barrier((got, near))
+        parts = [jnp.concatenate([v, g], axis=0) for v, g in zip(parts, got)]
+    if by_permutes:
+        near = [jnp.concatenate(v, axis=0) for v in near]
+        near = [[v, swapped(v, o[1], groups)] for v, o in zip(near, orders)]
+    far = [swapped(v, o[-1], groups) for v, o in zip(parts, outward)]
+
+    bits = range(len(strides))
+    heads = jnp.arange(HEADS)
+    if by_permutes:
+        left, right = (
+            jnp.concatenate(v, axis=0).reshape(HEADS, n_payload, wide // 2) for v in near
+        )
+        head_bits = [bit_of(heads, stride) for stride in strides]
+        at_l = joined_places(heads // plane, head_bits, bits, member, line, lines, plane)
+        at_r = joined_places(heads // plane, head_bits, bits[::-1], member, line, lines, plane)
+    else:
+        every = lax.all_gather(payload, "ctx", axis=0, axis_index_groups=head_groups)
+        left, right = every[:, :, : wide // 2], every[:, :, wide // 2 :]
+        at_l = at_r = heads.astype(jnp.int32)
+    qkv_sum, gain_parts, bias_parts, scales, small_sums = place_qkv(
+        at_l, at_r, left, right, qkv_weight, norm_gain[0].astype(f32), norm_bias[0].astype(f32)
+    )
+    gain_one, bias_one = jnp.sum(gain_parts, axis=1), jnp.sum(bias_parts, axis=1)
+    scale_sum = part_of(scales[:, 0], 0, me, size, 0)
     grad_one = natural([dot(grad_proj_t, part, 0, 1) for part in qkv_parts], me, 1)
-    grad_first, gain_one, bias_one = norm_backward(grad_one, norm_one, inv_one, gains[0])
+    grad_first = norm_backward(grad_one, norm_one, inv_one, gains[0])[0]
     input_grad = (grad_middle + grad_first).astype(low)[None]
 
-    my_scale_grad = jnp.sum(delta_sum) / my_scale[0]
-    scale_grad = jnp.where(jnp.arange(HEADS) == head, my_scale_grad, 0.0)
-    squares = jnp.stack(
-        [jnp.sum(result * result), jnp.sum(attn_out * attn_out), jnp.sum(ffn_out * ffn_out)]
-    )
-    packed = jnp.concatenate(
-        [gain_one, gain_att, gain_two, bias_one, bias_att, bias_two,
-         mid_gain_grad, mid_bias_grad, scale_grad, squares]
-    )
-    total = lax.psum(packed, ("ctx", "fsdp"))
-    gain_grad = part_of(total[: 3 * width].reshape(3, width), 0, me, size, 1)
-    bias_grad = part_of(total[3 * width : 6 * width].reshape(3, width), 0, me, size, 1)
-    at = 6 * width
-    mid_gain_sum = part_of(total[at : at + hidden_width], 0, me, size, 0)
-    at = at + hidden_width
-    mid_bias_sum = part_of(total[at : at + hidden_width], 0, me, size, 0)
-    at = at + hidden_width
-    scale_sum = part_of(total[at : at + HEADS], 0, me, size, 0)
-    rms_values = jnp.sqrt(total[at + HEADS :] / (rows * groups * size * width))
+    far, qkv_sum, input_grad = lax.optimization_barrier((far, qkv_sum, input_grad))
+    block = jnp.arange(groups)
+    block_bits = [block // lines // (1 << i) % 2 for i in bits]
+    at_a = joined_places(
+        block % lines, block_bits[::-1], bits[::-1], member, line, lines, plane
+    )
+    at_b = joined_places(block % lines, block_bits, bits, member, line, lines, plane)
+    ends = [
+        [d.reshape(groups // 2, one_chunk, -1) for d in pair] for pair in zip(parts, far)
+    ]
+    fc1_sum, out_sum = place_sums(at_a, at_b, ends[0], ends[1], hidden_width)
+    fc1_sum, fc2_sum = lax.optimization_barrier((fc1_sum, fc2_sum))
+    fc1_sum = fc1_sum.reshape(own_rows, hidden_width)
+    out_sum = out_sum.reshape(own_rows, width)
+    gain_grad = jnp.stack([gain_one, small_sums[0], small_sums[1]])
+    bias_grad = jnp.stack([bias_one, small_sums[2], small_sums[3]])
+    mid_sums = small_sums[4:n_small].reshape(2, -1)
+    mid_gain_sum, mid_bias_sum = mid_sums[0], mid_sums[1]
+    rms_values = jnp.sqrt(small_sums[n_small, :3] / (rows * groups * size * width))
     return (
         result.astype(low)[None],
         input_grad,
-        qkv_sum.astype(f32),
-        out_sum.astype(f32),
-        fc1_sum.astype(f32),
+        qkv_sum,
+        out_sum,
+        fc1_sum,
         fc2_sum.astype(f32),
         gain_grad,
         bias_grad,

time: 577 us -> 423 us (0.73)
  waiting for transfers between devices: 295 us -> 184 us
  blocking collectives: 109 us -> 0 us
  starting transfers between devices: 16.1 us -> 49.8 us
  Pallas kernels: 22.6 us -> 47.5 us
  matrix products: 55.6 us -> 61.9 us
    psum x2 -> x1, waiting for transfers between devices: 277 us -> 0.01 us  [local(): fc2_sum = lax.psum(fc2_grad, 'ctx')]
    ppermute x0 -> x21, waiting for transfers between devices: none -> 144 us  [the longest x12 82.7 us: swapped(): return lax.ppermute(value, 'ctx', [(i, i ^ stride) for i in range(groups)])]
    all_to_all x2 -> x0, blocking collectives: 64.2 us -> none  [the longest x1 41.8 us: local(): lax.all_to_all(grads_out, 'ctx', 0, 0, tiled=True, axis_index_groups=head...]
    psum x1 -> x0, blocking collectives: 44.9 us -> none  [local(): total = lax.psum(packed, ('ctx', 'fsdp'))]
    pallas_call x0 -> x3, Pallas kernels: none -> 24.9 us  [the longest x1 9.08 us: place_qkv(): pl.pallas_call(place_qkv_kernel, grid_spec=pltpu.PrefetchScalarGridSpec(n...]
    ppermute x0 -> x21, starting transfers between devices: none -> 23.4 us  [the longest x9 12.9 us: from_line(): lax.ppermute(value, 'ctx', [(i, (i + k * plane) % groups) for i in range(...]
    all_to_all x0 -> x2, starting transfers between devices: none -> 11.8 us  [the longest x1 6.07 us: local(): lax.all_to_all(grads_out, 'ctx', 0, 0, tiled=True, axis_index_groups=head...]
    all_to_all x1, waiting for transfers between devices: 0.66 us -> 11.1 us  [local(): lax.all_to_all(scaled_tiles, 'ctx', 0, 0, tiled=True, axis_index_groups=h...]
  transfers between devices with their start and end apart: 17 -> 40, of which waited for: 6 -> 16; matrix products, arithmetic and copies ran while one was open for 15% -> 25% of each run, Pallas kernels for 4% -> 11%
where the time goes in v3:
time: 423 us; the launch traced here: 416 us
  waiting for transfers between devices  184 us (43%)
  matrix products  61.9 us (15%)
  starting transfers between devices  49.8 us (12%)
  Pallas kernels  47.5 us (11%)
  other arithmetic  40.2 us (10%)
  between operations  17.2 us (4%)
  local copies, waits for them, and re-layouts  16 us (4%)
    ppermute x12, waiting for transfers between devices, swapped(): return lax.ppermute(value, 'ctx', [(i, i ^ stride) for i in range(groups)])  82.7 us
    dot_general x23, matrix products, dot(): lax.dot_general(a, b, (((ca,), (cb,)), ((), ())), preferred_element_type=...  61.9 us
    ppermute x9, waiting for transfers between devices, from_line(): lax.ppermute(value, 'ctx', [(i, (i + k * plane) % groups) for i in range(...  61.2 us
    all_to_all x1, waiting for transfers between devices, local(): lax.all_to_all(by_head, 'ctx', 0, 0, tiled=True, axis_index_groups=head_g...  15.1 us
    ppermute x9, starting transfers between devices, from_line(): lax.ppermute(value, 'ctx', [(i, (i + k * plane) % groups) for i in range(...  12.9 us
    pallas_call x1, Pallas kernels, attend(): pl.pallas_call(partial(attend_kernel, n_q=n_q, n_k=n_k, k_at=k_at), in_sp...  11.3 us
    pallas_call x1, Pallas kernels, attend_back(): pl.pallas_call(partial(attend_back_kernel, n_q=n_q, n_k=n_k), in_specs=in...  11.3 us
    all_to_all x1, waiting for transfers between devices, local(): lax.all_to_all(scaled_tiles, 'ctx', 0, 0, tiled=True, axis_index_groups=h...  11.1 us
  transfers between devices with their start and end apart: 40, of which 16 were waited for; matrix products, arithmetic and copies ran while one was open for 25% of the time, Pallas kernels for 11%

profile of v3, /device:TPU:12, one launch (start us, length us, event | category | flops | bytes accessed | tf_op | source)
XLA Modules:
  0.0 416.1 jit_solution(2238094818477073101)
XLA Ops:
  21.2 7.2 %all-to-all-start = ((bf16[16,3,64,128]{3,2,1,0:T(8,128)(2,1)}), bf16[16,3,64,128]{3,2,1,0:T(8,128)(2,1)S(1)}, u32[]{:S(2)}, u32[]{:S(2)}) async-start(bf16[16,3,64,128]{3,2,1,0:T(8,128)(2,1)} %bitcast.136), calls=%async_computation | async-start | bytes 1572864 | tf_op jit(solution)/shard_map/all_to_all | solution.py:582
  30.9 4.7 %convolution_bitcast_fusion.1 = f32[128,2048]{1,0:T(8,128)} fusion(bf16[2048,1024]{1,0:T(8,128)(2,1)} %param.18, bf16[1,128,1024]{2,1,0:T(8,128)(2,1)} %param.13), kind=kOutput, calls=%fused_computation.17 | convolution fusion | flops 536870912 | bytes 5505024 | tf_op jit(solution)/shard_map/dot_general | solution.py:19
  38.2 15.1 %all-to-all-done.q_ref.kv_ref = bf16[16,3,64,128]{3,2,1,0:T(8,128)(2,1)S(1)} async-done(((bf16[16,3,64,128]{3,2,1,0:T(8,128)(2,1)}), bf16[16,3,64,128]{3,2,1,0:T(8,128)(2,1)S(1)}, u32[]{:S(2)}, u32[]{:S(2)}) %all-to-all-start) | async-done | bytes 786464 | tf_op jit(solution)/shard_map/all_to_all | solution.py:582
  53.4 11.3 %attend.1 = (bf16[16,64,128]{2,1,0:T(8,128)(2,1)}, f32[8,64,256]{2,1,0:T(8,128)S(1)}, f32[8,1,256]{2,1,0:T(1,128)S(1)}, bf16[8,64,256]{2,1,0:T(8,128)(2,1)S(1)},...) custom-call(s32[9]{0:T(128)S(1)} %pad_add_fusion.1.info_ref, f32[1]{0:T(128)} %dynamic_slice.128.hs_ref, ...), custom_call_target="tpu_custom_call" | custom-call | bytes 32000000 | tf_op jit(solution)/shard_map/attend/pallas_call | solution.py:258
  64.7 4.7 %all-to-all-start.1 = ((bf16[16,64,128]{2,1,0:T(8,128)(2,1)}), bf16[16,64,128]{2,1,0:T(8,128)(2,1)S(1)}, u32[]{:S(2)}, u32[]{:S(2)}) async-start(bf16[16,64,128]{2,1,0:T(8,128)(2,1)} %get-tuple-element.69), calls=%async_computation.1 | async-start | bytes 524288 | tf_op jit(solution)/shard_map/all_to_all | solution.py:590
  69.5 11.1 %all-to-all-done.1 = bf16[16,64,128]{2,1,0:T(8,128)(2,1)S(1)} async-done(((bf16[16,64,128]{2,1,0:T(8,128)(2,1)}), bf16[16,64,128]{2,1,0:T(8,128)(2,1)S(1)}, u32[]{:S(2)}, u32[]{:S(2)}) %all-to-all-start.1) | async-done | bytes 262176 | tf_op jit(solution)/shard_map/all_to_all | solution.py:590
  86.4 3.8 fusion.120
  93.5 4.9 %convolution_bitcast_fusion = f32[128,2048]{1,0:T(8,128)} fusion(bf16[2048,1024]{1,0:T(8,128)(2,1)} %collective-permute-done.5, bf16[1,128,1024]{2,1,0:T(8,128)(2,1)} %param.13), kind=kOutput, calls=%fused_computation.16 | convolution fusion | flops 536870912 | bytes 5505024 | tf_op jit(solution)/shard_map/dot_general | solution.py:19
  101.3 4.3 %convolution_convert_fusion.1 = bf16[2048,1024]{1,0:T(8,128)(2,1)} fusion(bf16[128,2048]{1,0:T(8,128)(2,1)S(1)} %collective-permute-done.7, bf16[128,2048]{1,0:T(8,128)(2,1)S(1)} %get-tuple-element.153, bf16[128,1024]{1,0:T(8,128)(2,1)} %collective-permute-done.8, bf16[128,1024]{1,0:T(8,128)(2,1)} %bitcast.13), kind=kOutput, calls=%fused_computation.8 | convolution fusion | flops 1078984704 | bytes 5767168 | tf_op jit(solution)/shard_map/dot_general | solution.py:19
  105.6 3.9 multiply_reduce_fusion
  115.5 4.1 fusion.139
  119.7 4.5 %multiply_reduce_fusion.6 = (f32[]{:T(128)}, f32[]{:T(128)}, f32[128]{0:T(128)S(1)}, f32[128]{0:T(128)S(1)}, f32[1024]{0:T(1024)S(1)}, /*index=5*/f32[1024]{0:T(...) fusion(f32[128,1024]{1,0:T(8,128)S(1)} %get-tuple-element.145, f32[1024]{0:T(1024)S(1)} %bitcast.168, ...), kind=kOutput, calls=%fused_computation.111 | convolution fusion | flops 539358976 | bytes 7092236 | tf_op jit(solution)/shard_map/dot_general | solution.py:19
  134.0 5.7 %all-to-all-start.2 = ((bf16[16,64,128]{2,1,0:T(8,128)(2,1)}), bf16[16,64,128]{2,1,0:T(8,128)(2,1)S(1)}, u32[]{:S(2)}, u32[]{:S(2)}) async-start(bf16[16,64,128]{2,1,0:T(8,128)(2,1)} %multiply_convert_fusion), calls=%async_computation.2 | async-start | bytes 524288 | tf_op jit(solution)/shard_map/all_to_all | solution.py:669
  149.6 11.3 %attend_back.1 = (bf16[16,64,128]{2,1,0:T(8,128)(2,1)S(1)}, bf16[16,64,128]{2,1,0:T(8,128)(2,1)S(1)}, bf16[16,64,128]{2,1,0:T(8,128)(2,1)S(1)}, f32[1,256]{1,0:T(1,128)S(1)}) custom-call(s32[9]{0:T(128)S(1)} %pad_add_fusion.1.info_ref, bf16[8,64,256]{2,1,0:T(8,128)(2,1)S(1)} %get-tuple-element.76.qs_ref, bf16[8,64,256]{2,1,0:T(8,128)(2,1)S(1)} %get-tuple-element.77.ks_ref, ...), custom_call_target="tpu_custom_call" | custom-call | bytes 32000000 | tf_op jit(solution)/shard_map/attend_back/pallas_call | solution.py:282
  167.0 8.5 %head_grad.1 = (f32[192,1024]{1,0:T(8,128)}, f32[8,192]{1,0:T(8,128)}) custom-call(bf16[16,1,128,1024]{3,2,1,0:T(8,128)(2,1)} %bitcast.151, bf16[16,64,128]{2,1,0:T(8,128)(2,1)} %copy-done, bf16[16,64,128]{2,1,0:T(8,128)(2,1)} %copy-done.2, bf16[16,64,128]{2,1,0:T(8,128)(2,1)} %copy-done.4), custom_call_target="tpu_custom_call" | custom-call | bytes 25600000 | tf_op jit(solution)/shard_map/head_grad/pallas_call | solution.py:315
  178.9 6.1 %all-to-all-start.3 = ((bf16[16,3,64,128]{3,2,1,0:T(8,128)(2,1)}), bf16[16,3,64,128]{3,2,1,0:T(8,128)(2,1)}, u32[]{:S(2)}, u32[]{:S(2)}) async-start(bf16[16,3,64,128]{3,2,1,0:T(8,128)(2,1)} %copy.42), calls=%async_computation.3 | async-start | bytes 1572864 | tf_op jit(solution)/shard_map/all_to_all | solution.py:685
  187.0 10.6 %collective-permute-done.12 = bf16[256,2560]{1,0:T(8,128)(2,1)} collective-permute-done((bf16[256,2560]{1,0:T(8,128)(2,1)}, bf16[256,2560]{1,0:T(8,128)(2,1)}, u32[]{:S(2)}, u32[]{:S(2)}) %collective-permute-start.12) | collective-permute-done | bytes 1310752 | tf_op jit(solution)/shard_map/ppermute | solution.py:500
  197.6 7.8 %collective-permute-done.13 = bf16[256,2560]{1,0:T(8,128)(2,1)} collective-permute-done((bf16[256,2560]{1,0:T(8,128)(2,1)}, bf16[256,2560]{1,0:T(8,128)(2,1)}, u32[]{:S(2)}, u32[]{:S(2)}) %collective-permute-start.13) | collective-permute-done | bytes 1310752 | tf_op jit(solution)/shard_map/ppermute | solution.py:500
  215.8 9.2 %all-to-all-done.3 = bf16[16,3,64,128]{3,2,1,0:T(8,128)(2,1)} async-done(((bf16[16,3,64,128]{3,2,1,0:T(8,128)(2,1)}), bf16[16,3,64,128]{3,2,1,0:T(8,128)(2,1)}, u32[]{:S(2)}, u32[]{:S(2)}) %all-to-all-start.3) | async-done | bytes 786464 | tf_op jit(solution)/shard_map/all_to_all | solution.py:685
  226.2 3.2 fusion.142
  236.1 7.8 %collective-permute-done.17 = bf16[32,5120]{1,0:T(8,128)(2,1)S(1)} collective-permute-done((bf16[32,5120]{1,0:T(8,128)(2,1)S(1)}, bf16[32,5120]{1,0:T(8,128)(2,1)S(1)}, u32[]{:S(2)}, u32[]{:S(2)}) %collective-permute-start.17) | collective-permute-done | bytes 327712 | tf_op jit(solution)/shard_map/ppermute | solution.py:513
  245.1 22.9 %collective-permute-done.18 = bf16[32,5120]{1,0:T(8,128)(2,1)S(1)} collective-permute-done((bf16[32,5120]{1,0:T(8,128)(2,1)S(1)}, bf16[32,5120]{1,0:T(8,128)(2,1)S(1)}, u32[]{:S(2)}, u32[]{:S(2)}) %collective-permute-start.18) | collective-permute-done | bytes 327712 | tf_op jit(solution)/shard_map/ppermute | solution.py:513
  268.2 3.4 collective-permute-start.21
  274.0 7.4 %collective-permute-done.20 = bf16[32,5120]{1,0:T(8,128)(2,1)S(1)} collective-permute-done((bf16[32,5120]{1,0:T(8,128)(2,1)S(1)}, bf16[32,5120]{1,0:T(8,128)(2,1)S(1)}, u32[]{:S(2)}, u32[]{:S(2)}) %collective-permute-start.20) | collective-permute-done | bytes 327712 | tf_op jit(solution)/shard_map/ppermute | solution.py:513
  281.4 19.5 %collective-permute-done.21 = bf16[32,5120]{1,0:T(8,128)(2,1)S(1)} collective-permute-done((bf16[32,5120]{1,0:T(8,128)(2,1)S(1)}, bf16[32,5120]{1,0:T(8,128)(2,1)S(1)}, u32[]{:S(2)}, u32[]{:S(2)}) %collective-permute-start.21) | collective-permute-done | bytes 327712 | tf_op jit(solution)/shard_map/ppermute | solution.py:513
  300.9 3.7 collective-permute-done.22
  311.0 26.8 %collective-permute-done.28 = bf16[896,256]{1,0:T(8,128)(2,1)S(1)} collective-permute-done((bf16[896,256]{1,0:T(8,128)(2,1)S(1)}, bf16[896,256]{1,0:T(8,128)(2,1)S(1)}, u32[]{:S(2)}, u32[]{:S(2)}) %collective-permute-start.28) | collective-permute-done | bytes 458784 | tf_op jit(solution)/shard_map/ppermute | solution.py:500
  342.5 24.8 %collective-permute-done.33 = bf16[1792,256]{1,0:T(8,128)(2,1)S(1)} collective-permute-done((bf16[1792,256]{1,0:T(8,128)(2,1)S(1)}, bf16[1792,256]{1,0:T(8,128)(2,1)S(1)}, u32[]{:S(2)}, u32[]{:S(2)}) %collective-permute-start.33) | collective-permute-done | bytes 917536 | tf_op jit(solution)/shard_map/ppermute | solution.py:500
  367.5 9.1 %place_qkv.1 = (f32[512,3072]{1,0:T(8,128)}, f32[512,128]{1,0:T(8,128)S(1)}, f32[512,128]{1,0:T(8,128)S(1)}, f32[16,128]{1,0:T(8,128)S(1)}, f32[16,512]{1,0:T(8,128)S(1)}) custom-call(s32[16]{0:T(128)S(1)} %get-tuple-element.181.at_l_ref, s32[16]{0:T(128)S(1)} %get-tuple-element.180.at_r_ref, bf16[16,224,256]{2,1,0:T(8,128)(2,1)S(1)} %bitcast.141, ...), custom_call_target="tpu_custom_call" | custom-call | bytes 28800000 | tf_op jit(solution)/shard_map/place_qkv/pallas_call | solution.py:442
  382.1 11.7 %collective-permute-done.31 = bf16[256,2560]{1,0:T(8,128)(2,1)} collective-permute-done((bf16[256,2560]{1,0:T(8,128)(2,1)S(1)}, bf16[256,2560]{1,0:T(8,128)(2,1)}, u32[]{:S(2)}, u32[]{:S(2)}) %collective-permute-start.31) | collective-permute-done | bytes 1310752 | tf_op jit(solution)/shard_map/ppermute | solution.py:500
  394.8 7.3 %place_sums.1 = (f32[16,32,4096]{2,1,0:T(8,128)}, f32[16,32,1024]{2,1,0:T(8,128)}) custom-call(s32[16]{0:T(128)S(1)} %get-tuple-element.179.at_a_ref, s32[16]{0:T(128)S(1)} %get-tuple-element.178.at_b_ref, bf16[8,32,2560]{2,1,0:T(8,128)(2,1)S(1)} %bitcast.143, bf16[8,32,2560]{2,1,0:T(8,128)(2,1)} %bitcast.43.a_far_ref, bf16[8,32,2560]{2,1,0:T(8,128)(2,1)S(1)} %bitcast.142, ...), custom_call_target="tpu_custom_call" | custom-call | bytes 22400000 | tf_op jit(solution)/shard_map/place_sums/pallas_call | solution.py:369
  402.2 6.6 %convert_element_type.214 = f32[2048,1024]{1,0:T(8,128)} convert(bf16[2048,1024]{1,0:T(8,128)(2,1)} %all-reduce.6.cloned.1.call-done) | non-fusion elementwise | flops 2097152 | bytes 12582912 | tf_op jit(solution)/shard_map/convert_element_type | solution.py:816
  (258 shorter events, 105.9 us)
Async XLA Ops:
  21.2 32.1 %all-to-all-start = ((bf16[16,3,64,128]{3,2,1,0:T(8,128)(2,1)}), bf16[16,3,64,128]{3,2,1,0:T(8,128)(2,1)S(1)}, u32[]{:S(2)}, u32[]{:S(2)}) async-start(bf16[16,3,64,128]{3,2,1,0:T(8,128)(2,1)} %bitcast.136), calls=%async_computation | async-start | bytes 1572864 | tf_op jit(solution)/shard_map/all_to_all | solution.py:582
  28.4 138.6 %all-gather.3.cloned.1.call-start = ((), (), s32[]{:S(2)}) async-start(), calls=%async_computation.5 | async-start | bytes 4456448 | tf_op jit(solution)/shard_map/all_gather | solution.py:549
  29.1 72.1 %collective-permute-start.8 = (bf16[128,1024]{1,0:T(8,128)(2,1)}, bf16[128,1024]{1,0:T(8,128)(2,1)}, u32[]{:S(2)}, u32[]{:S(2)}) collective-permute-start(bf16[128,1024]{1,0:T(8,128)(2,1)} %bitcast.13), channel_id=1, source_target_pairs={{1,0},{0,1},{3,2},{2,3},{5,4},{4,5},{7,6},{6,7},{9,8},{8,9},{11,10... | collective-permute-start | bytes 786440 | tf_op jit(solution)/shard_map/ppermute | solution.py:461
  29.9 56.5 %collective-permute-start.4 = (bf16[512,4096]{1,0:T(8,128)(2,1)}, bf16[512,4096]{1,0:T(8,128)(2,1)}, u32[]{:S(2)}, u32[]{:S(2)}) collective-permute-start(bf16[512,4096]{1,0:T(8,128)(2,1)} %param.17), channel_id=1, source_target_pairs={{1,0},{0,1},{3,2},{2,3},{5,4},{4,5},{7,6},{6,7},{9,8},{8,9},{11,10... | collective-permute-start | bytes 12582920 | tf_op jit(solution)/shard_map/ppermute | solution.py:461
  30.6 62.9 %collective-permute-start.5 = (bf16[2048,1024]{1,0:T(8,128)(2,1)}, bf16[2048,1024]{1,0:T(8,128)(2,1)}, u32[]{:S(2)}, u32[]{:S(2)}) collective-permute-start(bf16[2048,1024]{1,0:T(8,128)(2,1)} %param.18), channel_id=1, source_target_pairs={{1,0},{0,1},{3,2},{2,3},{5,4},{4,5},{7,6},{6,7},{9,8},{8,9},{11,10... | collective-permute-start | bytes 12582920 | tf_op jit(solution)/shard_map/ppermute | solution.py:461
  35.6 46.6 %collective-permute-start.3 = (bf16[512,1024]{1,0:T(8,128)(2,1)}, bf16[512,1024]{1,0:T(8,128)(2,1)}, u32[]{:S(2)}, u32[]{:S(2)}) collective-permute-start(bf16[512,1024]{1,0:T(8,128)(2,1)} %param.16), channel_id=1, source_target_pairs={{1,0},{0,1},{3,2},{2,3},{5,4},{4,5},{7,6},{6,7},{9,8},{8,9},{11,10... | collective-permute-start | bytes 3145736 | tf_op jit(solution)/shard_map/ppermute | solution.py:461
  64.7 15.9 %all-to-all-start.1 = ((bf16[16,64,128]{2,1,0:T(8,128)(2,1)}), bf16[16,64,128]{2,1,0:T(8,128)(2,1)S(1)}, u32[]{:S(2)}, u32[]{:S(2)}) async-start(bf16[16,64,128]{2,1,0:T(8,128)(2,1)} %get-tuple-element.69), calls=%async_computation.1 | async-start | bytes 524288 | tf_op jit(solution)/shard_map/all_to_all | solution.py:590
  98.5 45.5 %collective-permute-start.6 = (bf16[128,512]{1,0:T(8,128)(2,1)}, bf16[128,512]{1,0:T(8,128)(2,1)}, u32[]{:S(2)}, u32[]{:S(2)}) collective-permute-start(bf16[128,512]{1,0:T(8,128)(2,1)} %get-tuple-element.158), channel_id=1, source_target_pairs={{1,0},{0,1},{3,2},{2,3},{5,4},{4,5},{7,6},{6,7},{9,8},{8,9},{11,10... | collective-permute-start | bytes 393224 | tf_op jit(solution)/shard_map/ppermute | solution.py:461
  99.5 41.0 %collective-permute-start.10 = (bf16[128,512]{0,1:T(8,128)(2,1)}, bf16[128,512]{0,1:T(8,128)(2,1)}, u32[]{:S(2)}, u32[]{:S(2)}) collective-permute-start(bf16[128,512]{0,1:T(8,128)(2,1)} %get-tuple-element.156), channel_id=1, source_target_pairs={{1,0},{0,1},{3,2},{2,3},{5,4},{4,5},{7,6},{6,7},{9,8},{8,9},{11,10... | collective-permute-start | bytes 393224 | tf_op jit(solution)/shard_map/ppermute | solution.py:461
  112.4 31.5 %collective-permute-start.9 = (bf16[128,4096]{1,0:T(8,128)(2,1)}, bf16[128,4096]{1,0:T(8,128)(2,1)}, u32[]{:S(2)}, u32[]{:S(2)}) collective-permute-start(bf16[128,4096]{1,0:T(8,128)(2,1)} %fusion.9), channel_id=1, source_target_pairs={{1,0},{0,1},{3,2},{2,3},{5,4},{4,5},{7,6},{6,7},{9,8},{8,9},{11,10... | collective-permute-start | bytes 3145736 | tf_op jit(solution)/shard_map/ppermute | solution.py:461
  134.0 15.6 %all-to-all-start.2 = ((bf16[16,64,128]{2,1,0:T(8,128)(2,1)}), bf16[16,64,128]{2,1,0:T(8,128)(2,1)S(1)}, u32[]{:S(2)}, u32[]{:S(2)}) async-start(bf16[16,64,128]{2,1,0:T(8,128)(2,1)} %multiply_convert_fusion), calls=%async_computation.2 | async-start | bytes 524288 | tf_op jit(solution)/shard_map/all_to_all | solution.py:669
  139.7 262.5 %all-reduce.6.cloned.1.call-start = ((), (), s32[]{:S(2)}) async-start(), calls=%async_computation.4 | async-start | bytes 8388608 | tf_op jit(solution)/shard_map/psum | solution.py:612
  163.6 34.0 %collective-permute-start.12 = (bf16[256,2560]{1,0:T(8,128)(2,1)}, bf16[256,2560]{1,0:T(8,128)(2,1)}, u32[]{:S(2)}, u32[]{:S(2)}) collective-permute-start(bf16[256,2560]{1,0:T(8,128)(2,1)} %convolution_convert_fusion), channel_id=1, source_target_pairs={{0,2},{2,0},{4,6},{6,4},{8,10},{10,8},{12,14},{14,12},{16,18},{18,... | collective-permute-start | bytes 3932168 | tf_op jit(solution)/shard_map/ppermute | solution.py:500
  165.1 40.3 %collective-permute-start.13 = (bf16[256,2560]{1,0:T(8,128)(2,1)}, bf16[256,2560]{1,0:T(8,128)(2,1)}, u32[]{:S(2)}, u32[]{:S(2)}) collective-permute-start(bf16[256,2560]{1,0:T(8,128)(2,1)} %pad_maximum_fusion.2), channel_id=1, source_target_pairs={{0,4},{2,6},{4,0},{6,2},{8,12},{10,14},{12,8},{14,10},{16,20},{18,... | collective-permute-start | bytes 3932168 | tf_op jit(solution)/shard_map/ppermute | solution.py:500
  178.9 46.1 %all-to-all-start.3 = ((bf16[16,3,64,128]{3,2,1,0:T(8,128)(2,1)}), bf16[16,3,64,128]{3,2,1,0:T(8,128)(2,1)}, u32[]{:S(2)}, u32[]{:S(2)}) async-start(bf16[16,3,64,128]{3,2,1,0:T(8,128)(2,1)} %copy.42), calls=%async_computation.3 | async-start | bytes 1572864 | tf_op jit(solution)/shard_map/all_to_all | solution.py:685
  205.4 66.3 %collective-permute-start.23 = (bf16[224,512]{1,0:T(8,128)(2,1)S(1)}, bf16[224,512]{1,0:T(8,128)(2,1)S(1)}, u32[]{:S(2)}, u32[]{:S(2)}) collective-permute-start(bf16[224,512]{1,0:T(8,128)(2,1)S(1)} %pad_maximum_fusion.13), channel_id=1, source_target_pairs={{0,8},{2,10},{4,12},{6,14},{8,16},{10,18},{12,20},{14,22},{16,24},... | collective-permute-start | bytes 688136 | tf_op jit(solution)/shard_map/ppermute | solution.py:513
  207.4 66.6 %collective-permute-start.24 = (bf16[224,512]{1,0:T(8,128)(2,1)S(1)}, bf16[224,512]{1,0:T(8,128)(2,1)}, u32[]{:S(2)}, u32[]{:S(2)}) collective-permute-start(bf16[224,512]{1,0:T(8,128)(2,1)S(1)} %pad_maximum_fusion.13), channel_id=1, source_target_pairs={{0,16},{2,18},{4,20},{6,22},{8,24},{10,26},{12,28},{14,30},{16,0},... | collective-permute-start | bytes 688136 | tf_op jit(solution)/shard_map/ppermute | solution.py:513
  212.1 17.3 %collective-permute-start.16 = (bf16[128,2560]{1,0:T(8,128)(2,1)}, bf16[128,2560]{1,0:T(8,128)(2,1)S(1)}, u32[]{:S(2)}, u32[]{:S(2)}) collective-permute-start(bf16[128,2560]{1,0:T(8,128)(2,1)} %constant_dynamic-slice_fusion.1), channel_id=1, source_target_pairs={{0,2},{2,0},{4,6},{6,4},{8,10},{10,8},{12,14},{14,12},{16,18},{18,... | collective-permute-start | bytes 1966088 | tf_op jit(solution)/shard_map/ppermute | solution.py:500
  215.4 14.1 %collective-permute-start.15 = (bf16[128,2560]{1,0:T(8,128)(2,1)}, bf16[128,2560]{1,0:T(8,128)(2,1)}, u32[]{:S(2)}, u32[]{:S(2)}) collective-permute-start(bf16[128,2560]{1,0:T(8,128)(2,1)} %constant_dynamic-slice_fusion.2), channel_id=1, source_target_pairs={{0,4},{2,6},{4,0},{6,2},{8,12},{10,14},{12,8},{14,10},{16,20},{18,... | collective-permute-start | bytes 1966088 | tf_op jit(solution)/shard_map/ppermute | solution.py:500
  231.0 37.0 %collective-permute-start.18 = (bf16[32,5120]{1,0:T(8,128)(2,1)S(1)}, bf16[32,5120]{1,0:T(8,128)(2,1)S(1)}, u32[]{:S(2)}, u32[]{:S(2)}) collective-permute-start(bf16[32,5120]{1,0:T(8,128)(2,1)S(1)} %get-tuple-element.149), channel_id=1, source_target_pairs={{0,16},{2,18},{4,20},{6,22},{8,24},{10,26},{12,28},{14,30},{16,0},... | collective-permute-start | bytes 983048 | tf_op jit(solution)/shard_map/ppermute | solution.py:513
  231.6 36.4 %collective-permute-start.19 = (bf16[32,5120]{1,0:T(8,128)(2,1)S(1)}, bf16[32,5120]{1,0:T(8,128)(2,1)S(1)}, u32[]{:S(2)}, u32[]{:S(2)}) collective-permute-start(bf16[32,5120]{1,0:T(8,128)(2,1)S(1)} %get-tuple-element.150), channel_id=1, source_target_pairs={{0,24},{2,26},{4,28},{6,30},{8,0},{10,2},{12,4},{14,6},{16,8},{18,... | collective-permute-start | bytes 983048 | tf_op jit(solution)/shard_map/ppermute | solution.py:513
  243.9 30.2 %collective-permute-start.25 = (bf16[224,512]{1,0:T(8,128)(2,1)S(1)}, bf16[224,512]{1,0:T(8,128)(2,1)S(1)}, u32[]{:S(2)}, u32[]{:S(2)}) collective-permute-start(bf16[224,512]{1,0:T(8,128)(2,1)S(1)} %pad_maximum_fusion.13), channel_id=1, source_target_pairs={{0,24},{2,26},{4,28},{6,30},{8,0},{10,2},{12,4},{14,6},{16,8},{18,... | collective-permute-start | bytes 688136 | tf_op jit(solution)/shard_map/ppermute | solution.py:513
  268.2 32.6 %collective-permute-start.21 = (bf16[32,5120]{1,0:T(8,128)(2,1)S(1)}, bf16[32,5120]{1,0:T(8,128)(2,1)S(1)}, u32[]{:S(2)}, u32[]{:S(2)}) collective-permute-start(bf16[32,5120]{1,0:T(8,128)(2,1)S(1)} %add_convert_fusion.3), channel_id=1, source_target_pairs={{0,16},{2,18},{4,20},{6,22},{8,24},{10,26},{12,28},{14,30},{16,0},... | collective-permute-start | bytes 983048 | tf_op jit(solution)/shard_map/ppermute | solution.py:513
  271.7 32.9 %collective-permute-start.22 = (bf16[32,5120]{1,0:T(8,128)(2,1)S(1)}, bf16[32,5120]{1,0:T(8,128)(2,1)S(1)}, u32[]{:S(2)}, u32[]{:S(2)}) collective-permute-start(bf16[32,5120]{1,0:T(8,128)(2,1)S(1)} %add_convert_fusion.3), channel_id=1, source_target_pairs={{0,24},{2,26},{4,28},{6,30},{8,0},{10,2},{12,4},{14,6},{16,8},{18,... | collective-permute-start | bytes 983048 | tf_op jit(solution)/shard_map/ppermute | solution.py:513
  304.8 33.1 %collective-permute-start.26 = (bf16[128,2560]{1,0:T(8,128)(2,1)S(1)}, bf16[128,2560]{1,0:T(8,128)(2,1)S(1)}, u32[]{:S(2)}, u32[]{:S(2)}) collective-permute-start(bf16[128,2560]{1,0:T(8,128)(2,1)S(1)} %get-tuple-element.147), channel_id=1, source_target_pairs={{0,4},{2,6},{4,0},{6,2},{8,12},{10,14},{12,8},{14,10},{16,20},{18,... | collective-permute-start | bytes 1966088 | tf_op jit(solution)/shard_map/ppermute | solution.py:500
  305.2 32.6 %collective-permute-start.27 = (bf16[128,2560]{1,0:T(8,128)(2,1)S(1)}, bf16[128,2560]{1,0:T(8,128)(2,1)S(1)}, u32[]{:S(2)}, u32[]{:S(2)}) collective-permute-start(bf16[128,2560]{1,0:T(8,128)(2,1)S(1)} %get-tuple-element.146), channel_id=1, source_target_pairs={{0,2},{2,0},{4,6},{6,4},{8,10},{10,8},{12,14},{14,12},{16,18},{18,... | collective-permute-start | bytes 1966088 | tf_op jit(solution)/shard_map/ppermute | solution.py:500
  307.1 30.7 %collective-permute-start.28 = (bf16[896,256]{1,0:T(8,128)(2,1)S(1)}, bf16[896,256]{1,0:T(8,128)(2,1)S(1)}, u32[]{:S(2)}, u32[]{:S(2)}) collective-permute-start(bf16[896,256]{1,0:T(8,128)(2,1)S(1)} %get-tuple-element.100), channel_id=1, source_target_pairs={{0,2},{2,0},{4,6},{6,4},{8,10},{10,8},{12,14},{14,12},{16,18},{18,... | collective-permute-start | bytes 1376264 | tf_op jit(solution)/shard_map/ppermute | solution.py:500
  308.4 29.5 %collective-permute-start.29 = (bf16[896,256]{1,0:T(8,128)(2,1)S(1)}, bf16[896,256]{1,0:T(8,128)(2,1)S(1)}, u32[]{:S(2)}, u32[]{:S(2)}) collective-permute-start(bf16[896,256]{1,0:T(8,128)(2,1)S(1)} %get-tuple-element.102), channel_id=1, source_target_pairs={{0,4},{2,6},{4,0},{6,2},{8,12},{10,14},{12,8},{14,10},{16,20},{18,... | collective-permute-start | bytes 1376264 | tf_op jit(solution)/shard_map/ppermute | solution.py:500
  337.9 29.3 %collective-permute-start.33 = (bf16[1792,256]{1,0:T(8,128)(2,1)S(1)}, bf16[1792,256]{1,0:T(8,128)(2,1)S(1)}, u32[]{:S(2)}, u32[]{:S(2)}) collective-permute-start(bf16[1792,256]{1,0:T(8,128)(2,1)S(1)} %pad_maximum_fusion.7), channel_id=1, source_target_pairs={{0,2},{2,0},{4,6},{6,4},{8,10},{10,8},{12,14},{14,12},{16,18},{18,... | collective-permute-start | bytes 2752520 | tf_op jit(solution)/shard_map/ppermute | solution.py:500
  338.5 28.9 %collective-permute-start.32 = (bf16[1792,256]{1,0:T(8,128)(2,1)S(1)}, bf16[1792,256]{1,0:T(8,128)(2,1)S(1)}, u32[]{:S(2)}, u32[]{:S(2)}) collective-permute-start(bf16[1792,256]{1,0:T(8,128)(2,1)S(1)} %pad_maximum_fusion.6), channel_id=1, source_target_pairs={{0,4},{2,6},{4,0},{6,2},{8,12},{10,14},{12,8},{14,10},{16,20},{18,... | collective-permute-start | bytes 2752520 | tf_op jit(solution)/shard_map/ppermute | solution.py:500
  339.7 54.1 %collective-permute-start.31 = (bf16[256,2560]{1,0:T(8,128)(2,1)S(1)}, bf16[256,2560]{1,0:T(8,128)(2,1)}, u32[]{:S(2)}, u32[]{:S(2)}) collective-permute-start(bf16[256,2560]{1,0:T(8,128)(2,1)S(1)} %pad_maximum_fusion.5), channel_id=1, source_target_pairs={{0,4},{2,6},{4,0},{6,2},{8,12},{10,14},{12,8},{14,10},{16,20},{18,... | collective-permute-start | bytes 3932168 | tf_op jit(solution)/shard_map/ppermute | solution.py:500
  340.8 54.0 %collective-permute-start.30 = (bf16[256,2560]{1,0:T(8,128)(2,1)S(1)}, bf16[256,2560]{1,0:T(8,128)(2,1)}, u32[]{:S(2)}, u32[]{:S(2)}) collective-permute-start(bf16[256,2560]{1,0:T(8,128)(2,1)S(1)} %pad_maximum_fusion.4), channel_id=1, source_target_pairs={{0,2},{2,0},{4,6},{6,4},{8,10},{10,8},{12,14},{14,12},{16,18},{18,... | collective-permute-start | bytes 3932168 | tf_op jit(solution)/shard_map/ppermute | solution.py:500
  (39 other events, 229.4 us)
Sparse Core Ops, SparseCore 0:
  32.0 81.0 all-gather.2
  146.7 225.8 all-reduce.5

commit v4 on v3

--- a/solution.py
+++ b/solution.py
@@ -788,6 +788,9 @@
     grad_first = norm_backward(grad_one, norm_one, inv_one, gains[0])[0]
     input_grad = (grad_middle + grad_first).astype(low)[None]
 
+    fc2_sum, qkv_sum = lax.optimization_barrier((fc2_sum, qkv_sum))
+    fc2_sum = fc2_sum.astype(f32)
+    far, fc2_sum = lax.optimization_barrier((far, fc2_sum))
     far, qkv_sum, input_grad = lax.optimization_barrier((far, qkv_sum, input_grad))
     block = jnp.arange(groups)
     block_bits = [block // lines // (1 << i) % 2 for i in bits]
@@ -799,7 +802,6 @@
         [d.reshape(groups // 2, one_chunk, -1) for d in pair] for pair in zip(parts, far)
     ]
     fc1_sum, out_sum = place_sums(at_a, at_b, ends[0], ends[1], hidden_width)
-    fc1_sum, fc2_sum = lax.optimization_barrier((fc1_sum, fc2_sum))
     fc1_sum = fc1_sum.reshape(own_rows, hidden_width)
     out_sum = out_sum.reshape(own_rows, width)
     gain_grad = jnp.stack([gain_one, small_sums[0], small_sums[1]])
@@ -813,7 +815,7 @@
         qkv_sum,
         out_sum,
         fc1_sum,
-        fc2_sum.astype(f32),
+        fc2_sum,
         gain_grad,
         bias_grad,
         mid_gain_sum,

time: 423 us -> 416 us (0.983)
  waiting for transfers between devices: 184 us -> 175 us
    ppermute x12, waiting for transfers between devices: 82.7 us -> 75.5 us  [swapped(): return lax.ppermute(value, 'ctx', [(i, i ^ stride) for i in range(groups)])]
  transfers between devices with their start and end apart: 40 -> 40, of which waited for: 16 -> 16; matrix products, arithmetic and copies ran while one was open for 25% -> 27% of each run, Pallas kernels for 11% -> 10%
where the time goes in v4:
time: 416 us; the launch traced here: 409 us
  waiting for transfers between devices  175 us (42%)
  matrix products  61.8 us (15%)
  starting transfers between devices  50.9 us (12%)
  Pallas kernels  48.3 us (12%)
  other arithmetic  40.2 us (10%)
  between operations  17.2 us (4%)
  local copies, waits for them, and re-layouts  16 us (4%)
    ppermute x12, waiting for transfers between devices, swapped(): return lax.ppermute(value, 'ctx', [(i, i ^ stride) for i in range(groups)])  75.5 us
    dot_general x23, matrix products, dot(): lax.dot_general(a, b, (((ca,), (cb,)), ((), ())), preferred_element_type=...  61.8 us
    ppermute x9, waiting for transfers between devices, from_line(): lax.ppermute(value, 'ctx', [(i, (i + k * plane) % groups) for i in range(...  60.7 us
    all_to_all x1, waiting for transfers between devices, local(): lax.all_to_all(by_head, 'ctx', 0, 0, tiled=True, axis_index_groups=head_g...  15.1 us
    ppermute x9, starting transfers between devices, from_line(): lax.ppermute(value, 'ctx', [(i, (i + k * plane) % groups) for i in range(...  13.7 us
    pallas_call x1, Pallas kernels, attend(): pl.pallas_call(partial(attend_kernel, n_q=n_q, n_k=n_k, k_at=k_at), in_sp...  11.7 us
    pallas_call x1, Pallas kernels, attend_back(): pl.pallas_call(partial(attend_back_kernel, n_q=n_q, n_k=n_k), in_specs=in...  11.7 us
    ppermute x12, starting transfers between devices, swapped(): return lax.ppermute(value, 'ctx', [(i, i ^ stride) for i in range(groups)])  10.8 us
  transfers between devices with their start and end apart: 40, of which 16 were waited for; matrix products, arithmetic and copies ran while one was open for 27% of the time, Pallas kernels for 10%

profile of v4, /device:TPU:12, one launch (start us, length us, event | category | flops | bytes accessed | tf_op | source)
XLA Modules:
  0.0 409.3 jit_solution(16109944048290071940)
XLA Ops:
  21.2 7.2 %all-to-all-start = ((bf16[16,3,64,128]{3,2,1,0:T(8,128)(2,1)}), bf16[16,3,64,128]{3,2,1,0:T(8,128)(2,1)S(1)}, u32[]{:S(2)}, u32[]{:S(2)}) async-start(bf16[16,3,64,128]{3,2,1,0:T(8,128)(2,1)} %bitcast.136), calls=%async_computation | async-start | bytes 1572864 | tf_op jit(solution)/shard_map/all_to_all | solution.py:582
  30.9 4.7 %convolution_bitcast_fusion.1 = f32[128,2048]{1,0:T(8,128)} fusion(bf16[2048,1024]{1,0:T(8,128)(2,1)} %param.18, bf16[1,128,1024]{2,1,0:T(8,128)(2,1)} %param.13), kind=kOutput, calls=%fused_computation.17 | convolution fusion | flops 536870912 | bytes 5505024 | tf_op jit(solution)/shard_map/dot_general | solution.py:19
  38.2 15.1 %all-to-all-done.q_ref.kv_ref = bf16[16,3,64,128]{3,2,1,0:T(8,128)(2,1)S(1)} async-done(((bf16[16,3,64,128]{3,2,1,0:T(8,128)(2,1)}), bf16[16,3,64,128]{3,2,1,0:T(8,128)(2,1)S(1)}, u32[]{:S(2)}, u32[]{:S(2)}) %all-to-all-start) | async-done | bytes 786464 | tf_op jit(solution)/shard_map/all_to_all | solution.py:582
  53.4 11.7 %attend.1 = (bf16[16,64,128]{2,1,0:T(8,128)(2,1)}, f32[8,64,256]{2,1,0:T(8,128)S(1)}, f32[8,1,256]{2,1,0:T(1,128)S(1)}, bf16[8,64,256]{2,1,0:T(8,128)(2,1)S(1)},...) custom-call(s32[9]{0:T(128)S(1)} %pad_add_fusion.1.info_ref, f32[1]{0:T(128)} %dynamic_slice.128.hs_ref, ...), custom_call_target="tpu_custom_call" | custom-call | bytes 32000000 | tf_op jit(solution)/shard_map/attend/pallas_call | solution.py:258
  65.1 4.7 %all-to-all-start.1 = ((bf16[16,64,128]{2,1,0:T(8,128)(2,1)}), bf16[16,64,128]{2,1,0:T(8,128)(2,1)S(1)}, u32[]{:S(2)}, u32[]{:S(2)}) async-start(bf16[16,64,128]{2,1,0:T(8,128)(2,1)} %get-tuple-element.72), calls=%async_computation.1 | async-start | bytes 524288 | tf_op jit(solution)/shard_map/all_to_all | solution.py:590
  69.9 10.6 %all-to-all-done.1 = bf16[16,64,128]{2,1,0:T(8,128)(2,1)S(1)} async-done(((bf16[16,64,128]{2,1,0:T(8,128)(2,1)}), bf16[16,64,128]{2,1,0:T(8,128)(2,1)S(1)}, u32[]{:S(2)}, u32[]{:S(2)}) %all-to-all-start.1) | async-done | bytes 262176 | tf_op jit(solution)/shard_map/all_to_all | solution.py:590
  86.4 3.8 fusion.120
  93.5 4.9 %convolution_bitcast_fusion = f32[128,2048]{1,0:T(8,128)} fusion(bf16[2048,1024]{1,0:T(8,128)(2,1)} %collective-permute-done.5, bf16[1,128,1024]{2,1,0:T(8,128)(2,1)} %param.13), kind=kOutput, calls=%fused_computation.16 | convolution fusion | flops 536870912 | bytes 5505024 | tf_op jit(solution)/shard_map/dot_general | solution.py:19
  101.2 4.3 %convolution_convert_fusion.1 = bf16[2048,1024]{1,0:T(8,128)(2,1)} fusion(bf16[128,2048]{1,0:T(8,128)(2,1)S(1)} %collective-permute-done.7, bf16[128,2048]{1,0:T(8,128)(2,1)S(1)} %get-tuple-element.159, bf16[128,1024]{1,0:T(8,128)(2,1)} %collective-permute-done.8, bf16[128,1024]{1,0:T(8,128)(2,1)} %bitcast.13), kind=kOutput, calls=%fused_computation.8 | convolution fusion | flops 1078984704 | bytes 5767168 | tf_op jit(solution)/shard_map/dot_general | solution.py:19
  105.6 3.9 multiply_reduce_fusion
  115.5 4.1 %fusion.139 = f32[128,512]{1,0:T(8,128)S(1)} fusion(bf16[128,4096]{1,0:T(8,128)(2,1)} %fusion.9, bf16[512,4096]{1,0:T(8,128)(2,1)} %collective-permute-done.4), kind=kOutput, calls=%fused_computation.328 | convolution fusion | flops 536870912 | bytes 5505024 | tf_op jit(solution)/shard_map/dot_general | solution.py:19
  119.7 4.5 %multiply_reduce_fusion.6 = (f32[]{:T(128)}, f32[]{:T(128)}, f32[128]{0:T(128)S(1)}, f32[128]{0:T(128)S(1)}, f32[1024]{0:T(1024)S(1)}, /*index=5*/f32[1024]{0:T(...) fusion(f32[128,1024]{1,0:T(8,128)S(1)} %get-tuple-element.151, f32[1024]{0:T(1024)S(1)} %bitcast.168, ...), kind=kOutput, calls=%fused_computation.111 | convolution fusion | flops 539358976 | bytes 7092236 | tf_op jit(solution)/shard_map/dot_general | solution.py:19
  134.0 5.7 %all-to-all-start.2 = ((bf16[16,64,128]{2,1,0:T(8,128)(2,1)}), bf16[16,64,128]{2,1,0:T(8,128)(2,1)S(1)}, u32[]{:S(2)}, u32[]{:S(2)}) async-start(bf16[16,64,128]{2,1,0:T(8,128)(2,1)} %multiply_convert_fusion), calls=%async_computation.2 | async-start | bytes 524288 | tf_op jit(solution)/shard_map/all_to_all | solution.py:669
  149.5 11.7 %attend_back.1 = (bf16[16,64,128]{2,1,0:T(8,128)(2,1)S(1)}, bf16[16,64,128]{2,1,0:T(8,128)(2,1)S(1)}, bf16[16,64,128]{2,1,0:T(8,128)(2,1)S(1)}, f32[1,256]{1,0:T(1,128)S(1)}) custom-call(s32[9]{0:T(128)S(1)} %pad_add_fusion.1.info_ref, bf16[8,64,256]{2,1,0:T(8,128)(2,1)S(1)} %get-tuple-element.79.qs_ref, bf16[8,64,256]{2,1,0:T(8,128)(2,1)S(1)} %get-tuple-element.80.ks_ref, ...), custom_call_target="tpu_custom_call" | custom-call | bytes 32000000 | tf_op jit(solution)/shard_map/attend_back/pallas_call | solution.py:282
  167.4 8.5 %head_grad.1 = (f32[192,1024]{1,0:T(8,128)}, f32[8,192]{1,0:T(8,128)}) custom-call(bf16[16,1,128,1024]{3,2,1,0:T(8,128)(2,1)} %bitcast.151, bf16[16,64,128]{2,1,0:T(8,128)(2,1)} %copy-done, bf16[16,64,128]{2,1,0:T(8,128)(2,1)} %copy-done.2, bf16[16,64,128]{2,1,0:T(8,128)(2,1)} %copy-done.4), custom_call_target="tpu_custom_call" | custom-call | bytes 25600000 | tf_op jit(solution)/shard_map/head_grad/pallas_call | solution.py:315
  179.2 6.0 %all-to-all-start.3 = ((bf16[16,3,64,128]{3,2,1,0:T(8,128)(2,1)}), bf16[16,3,64,128]{3,2,1,0:T(8,128)(2,1)}, u32[]{:S(2)}, u32[]{:S(2)}) async-start(bf16[16,3,64,128]{3,2,1,0:T(8,128)(2,1)} %copy.42), calls=%async_computation.3 | async-start | bytes 1572864 | tf_op jit(solution)/shard_map/all_to_all | solution.py:685
  187.3 10.3 %collective-permute-done.12 = bf16[256,2560]{1,0:T(8,128)(2,1)} collective-permute-done((bf16[256,2560]{1,0:T(8,128)(2,1)}, bf16[256,2560]{1,0:T(8,128)(2,1)}, u32[]{:S(2)}, u32[]{:S(2)}) %collective-permute-start.12) | collective-permute-done | bytes 1310752 | tf_op jit(solution)/shard_map/ppermute | solution.py:500
  197.6 8.3 %collective-permute-done.13 = bf16[256,2560]{1,0:T(8,128)(2,1)} collective-permute-done((bf16[256,2560]{1,0:T(8,128)(2,1)}, bf16[256,2560]{1,0:T(8,128)(2,1)}, u32[]{:S(2)}, u32[]{:S(2)}) %collective-permute-start.13) | collective-permute-done | bytes 1310752 | tf_op jit(solution)/shard_map/ppermute | solution.py:500
  216.2 8.8 %all-to-all-done.3 = bf16[16,3,64,128]{3,2,1,0:T(8,128)(2,1)} async-done(((bf16[16,3,64,128]{3,2,1,0:T(8,128)(2,1)}), bf16[16,3,64,128]{3,2,1,0:T(8,128)(2,1)}, u32[]{:S(2)}, u32[]{:S(2)}) %all-to-all-start.3) | async-done | bytes 786464 | tf_op jit(solution)/shard_map/all_to_all | solution.py:685
  226.2 3.2 fusion.142
  236.1 7.6 %collective-permute-done.17 = bf16[32,5120]{1,0:T(8,128)(2,1)S(1)} collective-permute-done((bf16[32,5120]{1,0:T(8,128)(2,1)S(1)}, bf16[32,5120]{1,0:T(8,128)(2,1)S(1)}, u32[]{:S(2)}, u32[]{:S(2)}) %collective-permute-start.17) | collective-permute-done | bytes 327712 | tf_op jit(solution)/shard_map/ppermute | solution.py:513
  245.8 22.5 %collective-permute-done.18 = bf16[32,5120]{1,0:T(8,128)(2,1)S(1)} collective-permute-done((bf16[32,5120]{1,0:T(8,128)(2,1)S(1)}, bf16[32,5120]{1,0:T(8,128)(2,1)S(1)}, u32[]{:S(2)}, u32[]{:S(2)}) %collective-permute-start.18) | collective-permute-done | bytes 327712 | tf_op jit(solution)/shard_map/ppermute | solution.py:513
  268.5 3.4 collective-permute-start.21
  274.3 7.3 %collective-permute-done.20 = bf16[32,5120]{1,0:T(8,128)(2,1)S(1)} collective-permute-done((bf16[32,5120]{1,0:T(8,128)(2,1)S(1)}, bf16[32,5120]{1,0:T(8,128)(2,1)S(1)}, u32[]{:S(2)}, u32[]{:S(2)}) %collective-permute-start.20) | collective-permute-done | bytes 327712 | tf_op jit(solution)/shard_map/ppermute | solution.py:513
  281.5 19.7 %collective-permute-done.21 = bf16[32,5120]{1,0:T(8,128)(2,1)S(1)} collective-permute-done((bf16[32,5120]{1,0:T(8,128)(2,1)S(1)}, bf16[32,5120]{1,0:T(8,128)(2,1)S(1)}, u32[]{:S(2)}, u32[]{:S(2)}) %collective-permute-start.21) | collective-permute-done | bytes 327712 | tf_op jit(solution)/shard_map/ppermute | solution.py:513
  301.2 3.7 collective-permute-done.22
  311.6 25.7 %collective-permute-done.28 = bf16[896,256]{1,0:T(8,128)(2,1)S(1)} collective-permute-done((bf16[896,256]{1,0:T(8,128)(2,1)S(1)}, bf16[896,256]{1,0:T(8,128)(2,1)S(1)}, u32[]{:S(2)}, u32[]{:S(2)}) %collective-permute-start.28) | collective-permute-done | bytes 458784 | tf_op jit(solution)/shard_map/ppermute | solution.py:500
  342.0 24.8 %collective-permute-done.33 = bf16[1792,256]{1,0:T(8,128)(2,1)S(1)} collective-permute-done((bf16[1792,256]{1,0:T(8,128)(2,1)S(1)}, bf16[1792,256]{1,0:T(8,128)(2,1)S(1)}, u32[]{:S(2)}, u32[]{:S(2)}) %collective-permute-start.33) | collective-permute-done | bytes 917536 | tf_op jit(solution)/shard_map/ppermute | solution.py:500
  367.1 9.1 %place_qkv.1 = (f32[512,3072]{1,0:T(8,128)}, f32[512,128]{1,0:T(8,128)S(1)}, f32[512,128]{1,0:T(8,128)S(1)}, f32[16,128]{1,0:T(8,128)S(1)}, f32[16,512]{1,0:T(8,128)S(1)}) custom-call(s32[16]{0:T(128)S(1)} %get-tuple-element.187.at_l_ref, s32[16]{0:T(128)S(1)} %get-tuple-element.186.at_r_ref, bf16[16,224,256]{2,1,0:T(8,128)(2,1)S(1)} %bitcast.141, ...), custom_call_target="tpu_custom_call" | custom-call | bytes 28800000 | tf_op jit(solution)/shard_map/place_qkv/pallas_call | solution.py:442
  378.1 6.6 %convert_element_type.213 = f32[2048,1024]{1,0:T(8,128)} convert(bf16[2048,1024]{1,0:T(8,128)(2,1)} %all-reduce.6.cloned.1.call-done) | non-fusion elementwise | flops 2097152 | bytes 12582912 | tf_op jit(solution)/shard_map/convert_element_type | solution.py:792
  388.3 5.3 %collective-permute-done.31 = bf16[256,2560]{1,0:T(8,128)(2,1)} collective-permute-done((bf16[256,2560]{1,0:T(8,128)(2,1)S(1)}, bf16[256,2560]{1,0:T(8,128)(2,1)}, u32[]{:S(2)}, u32[]{:S(2)}) %collective-permute-start.31) | collective-permute-done | bytes 1310752 | tf_op jit(solution)/shard_map/ppermute | solution.py:500
  394.7 7.3 %place_sums.1 = (f32[16,32,4096]{2,1,0:T(8,128)}, f32[16,32,1024]{2,1,0:T(8,128)}) custom-call(s32[16]{0:T(128)S(1)} %get-tuple-element.185.at_a_ref, s32[16]{0:T(128)S(1)} %get-tuple-element.184.at_b_ref, bf16[8,32,2560]{2,1,0:T(8,128)(2,1)S(1)} %bitcast.143, bf16[8,32,2560]{2,1,0:T(8,128)(2,1)} %bitcast.43.a_far_ref, bf16[8,32,2560]{2,1,0:T(8,128)(2,1)S(1)} %bitcast.142, ...), custom_call_target="tpu_custom_call" | custom-call | bytes 22400000 | tf_op jit(solution)/shard_map/place_sums/pallas_call | solution.py:369
  (258 shorter events, 107.0 us)
Async XLA Ops:
  21.2 32.1 %all-to-all-start = ((bf16[16,3,64,128]{3,2,1,0:T(8,128)(2,1)}), bf16[16,3,64,128]{3,2,1,0:T(8,128)(2,1)S(1)}, u32[]{:S(2)}, u32[]{:S(2)}) async-start(bf16[16,3,64,128]{3,2,1,0:T(8,128)(2,1)} %bitcast.136), calls=%async_computation | async-start | bytes 1572864 | tf_op jit(solution)/shard_map/all_to_all | solution.py:582
  28.4 138.9 %all-gather.3.cloned.1.call-start = ((), (), s32[]{:S(2)}) async-start(), calls=%async_computation.5 | async-start | bytes 4456448 | tf_op jit(solution)/shard_map/all_gather | solution.py:549
  29.1 72.1 %collective-permute-start.8 = (bf16[128,1024]{1,0:T(8,128)(2,1)}, bf16[128,1024]{1,0:T(8,128)(2,1)}, u32[]{:S(2)}, u32[]{:S(2)}) collective-permute-start(bf16[128,1024]{1,0:T(8,128)(2,1)} %bitcast.13), channel_id=1, source_target_pairs={{1,0},{0,1},{3,2},{2,3},{5,4},{4,5},{7,6},{6,7},{9,8},{8,9},{11,10... | collective-permute-start | bytes 786440 | tf_op jit(solution)/shard_map/ppermute | solution.py:461
  29.9 56.4 %collective-permute-start.4 = (bf16[512,4096]{1,0:T(8,128)(2,1)}, bf16[512,4096]{1,0:T(8,128)(2,1)}, u32[]{:S(2)}, u32[]{:S(2)}) collective-permute-start(bf16[512,4096]{1,0:T(8,128)(2,1)} %param.17), channel_id=1, source_target_pairs={{1,0},{0,1},{3,2},{2,3},{5,4},{4,5},{7,6},{6,7},{9,8},{8,9},{11,10... | collective-permute-start | bytes 12582920 | tf_op jit(solution)/shard_map/ppermute | solution.py:461
  30.6 62.9 %collective-permute-start.5 = (bf16[2048,1024]{1,0:T(8,128)(2,1)}, bf16[2048,1024]{1,0:T(8,128)(2,1)}, u32[]{:S(2)}, u32[]{:S(2)}) collective-permute-start(bf16[2048,1024]{1,0:T(8,128)(2,1)} %param.18), channel_id=1, source_target_pairs={{1,0},{0,1},{3,2},{2,3},{5,4},{4,5},{7,6},{6,7},{9,8},{8,9},{11,10... | collective-permute-start | bytes 12582920 | tf_op jit(solution)/shard_map/ppermute | solution.py:461
  35.6 46.6 %collective-permute-start.3 = (bf16[512,1024]{1,0:T(8,128)(2,1)}, bf16[512,1024]{1,0:T(8,128)(2,1)}, u32[]{:S(2)}, u32[]{:S(2)}) collective-permute-start(bf16[512,1024]{1,0:T(8,128)(2,1)} %param.16), channel_id=1, source_target_pairs={{1,0},{0,1},{3,2},{2,3},{5,4},{4,5},{7,6},{6,7},{9,8},{8,9},{11,10... | collective-permute-start | bytes 3145736 | tf_op jit(solution)/shard_map/ppermute | solution.py:461
  65.1 15.5 %all-to-all-start.1 = ((bf16[16,64,128]{2,1,0:T(8,128)(2,1)}), bf16[16,64,128]{2,1,0:T(8,128)(2,1)S(1)}, u32[]{:S(2)}, u32[]{:S(2)}) async-start(bf16[16,64,128]{2,1,0:T(8,128)(2,1)} %get-tuple-element.72), calls=%async_computation.1 | async-start | bytes 524288 | tf_op jit(solution)/shard_map/all_to_all | solution.py:590
  98.4 45.5 %collective-permute-start.6 = (bf16[128,512]{1,0:T(8,128)(2,1)}, bf16[128,512]{1,0:T(8,128)(2,1)}, u32[]{:S(2)}, u32[]{:S(2)}) collective-permute-start(bf16[128,512]{1,0:T(8,128)(2,1)} %get-tuple-element.164), channel_id=1, source_target_pairs={{1,0},{0,1},{3,2},{2,3},{5,4},{4,5},{7,6},{6,7},{9,8},{8,9},{11,10... | collective-permute-start | bytes 393224 | tf_op jit(solution)/shard_map/ppermute | solution.py:461
  99.4 41.0 %collective-permute-start.10 = (bf16[128,512]{0,1:T(8,128)(2,1)}, bf16[128,512]{0,1:T(8,128)(2,1)}, u32[]{:S(2)}, u32[]{:S(2)}) collective-permute-start(bf16[128,512]{0,1:T(8,128)(2,1)} %get-tuple-element.162), channel_id=1, source_target_pairs={{1,0},{0,1},{3,2},{2,3},{5,4},{4,5},{7,6},{6,7},{9,8},{8,9},{11,10... | collective-permute-start | bytes 393224 | tf_op jit(solution)/shard_map/ppermute | solution.py:461
  112.4 31.5 %collective-permute-start.9 = (bf16[128,4096]{1,0:T(8,128)(2,1)}, bf16[128,4096]{1,0:T(8,128)(2,1)}, u32[]{:S(2)}, u32[]{:S(2)}) collective-permute-start(bf16[128,4096]{1,0:T(8,128)(2,1)} %fusion.9), channel_id=1, source_target_pairs={{1,0},{0,1},{3,2},{2,3},{5,4},{4,5},{7,6},{6,7},{9,8},{8,9},{11,10... | collective-permute-start | bytes 3145736 | tf_op jit(solution)/shard_map/ppermute | solution.py:461
  126.6 13.9 %collective-permute-start.11 = (bf16[128,1024]{1,0:T(8,128)(2,1)S(1)}, bf16[128,1024]{1,0:T(8,128)(2,1)S(1)}, u32[]{:S(2)}, u32[]{:S(2)}) collective-permute-start(bf16[128,1024]{1,0:T(8,128)(2,1)S(1)} %multiply_convert_fusion.1), channel_id=1, source_target_pairs={{1,0},{0,1},{3,2},{2,3},{5,4},{4,5},{7,6},{6,7},{9,8},{8,9},{11,10... | collective-permute-start | bytes 786440 | tf_op jit(solution)/shard_map/ppermute | solution.py:461
  134.0 15.6 %all-to-all-start.2 = ((bf16[16,64,128]{2,1,0:T(8,128)(2,1)}), bf16[16,64,128]{2,1,0:T(8,128)(2,1)S(1)}, u32[]{:S(2)}, u32[]{:S(2)}) async-start(bf16[16,64,128]{2,1,0:T(8,128)(2,1)} %multiply_convert_fusion), calls=%async_computation.2 | async-start | bytes 524288 | tf_op jit(solution)/shard_map/all_to_all | solution.py:669
  139.6 238.5 %all-reduce.6.cloned.1.call-start = ((), (), s32[]{:S(2)}) async-start(), calls=%async_computation.4 | async-start | bytes 8388608 | tf_op jit(solution)/shard_map/psum | solution.py:612
  164.0 33.6 %collective-permute-start.12 = (bf16[256,2560]{1,0:T(8,128)(2,1)}, bf16[256,2560]{1,0:T(8,128)(2,1)}, u32[]{:S(2)}, u32[]{:S(2)}) collective-permute-start(bf16[256,2560]{1,0:T(8,128)(2,1)} %convolution_convert_fusion), channel_id=1, source_target_pairs={{0,2},{2,0},{4,6},{6,4},{8,10},{10,8},{12,14},{14,12},{16,18},{18,... | collective-permute-start | bytes 3932168 | tf_op jit(solution)/shard_map/ppermute | solution.py:500
  165.5 40.4 %collective-permute-start.13 = (bf16[256,2560]{1,0:T(8,128)(2,1)}, bf16[256,2560]{1,0:T(8,128)(2,1)}, u32[]{:S(2)}, u32[]{:S(2)}) collective-permute-start(bf16[256,2560]{1,0:T(8,128)(2,1)} %pad_maximum_fusion.2), channel_id=1, source_target_pairs={{0,4},{2,6},{4,0},{6,2},{8,12},{10,14},{12,8},{14,10},{16,20},{18,... | collective-permute-start | bytes 3932168 | tf_op jit(solution)/shard_map/ppermute | solution.py:500
  179.2 45.7 %all-to-all-start.3 = ((bf16[16,3,64,128]{3,2,1,0:T(8,128)(2,1)}), bf16[16,3,64,128]{3,2,1,0:T(8,128)(2,1)}, u32[]{:S(2)}, u32[]{:S(2)}) async-start(bf16[16,3,64,128]{3,2,1,0:T(8,128)(2,1)} %copy.42), calls=%async_computation.3 | async-start | bytes 1572864 | tf_op jit(solution)/shard_map/all_to_all | solution.py:685
  205.9 66.1 %collective-permute-start.23 = (bf16[224,512]{1,0:T(8,128)(2,1)S(1)}, bf16[224,512]{1,0:T(8,128)(2,1)S(1)}, u32[]{:S(2)}, u32[]{:S(2)}) collective-permute-start(bf16[224,512]{1,0:T(8,128)(2,1)S(1)} %pad_maximum_fusion.13), channel_id=1, source_target_pairs={{0,8},{2,10},{4,12},{6,14},{8,16},{10,18},{12,20},{14,22},{16,24},... | collective-permute-start | bytes 688136 | tf_op jit(solution)/shard_map/ppermute | solution.py:513
  208.4 65.9 %collective-permute-start.24 = (bf16[224,512]{1,0:T(8,128)(2,1)S(1)}, bf16[224,512]{1,0:T(8,128)(2,1)}, u32[]{:S(2)}, u32[]{:S(2)}) collective-permute-start(bf16[224,512]{1,0:T(8,128)(2,1)S(1)} %pad_maximum_fusion.13), channel_id=1, source_target_pairs={{0,16},{2,18},{4,20},{6,22},{8,24},{10,26},{12,28},{14,30},{16,0},... | collective-permute-start | bytes 688136 | tf_op jit(solution)/shard_map/ppermute | solution.py:513
  212.6 16.8 %collective-permute-start.16 = (bf16[128,2560]{1,0:T(8,128)(2,1)}, bf16[128,2560]{1,0:T(8,128)(2,1)S(1)}, u32[]{:S(2)}, u32[]{:S(2)}) collective-permute-start(bf16[128,2560]{1,0:T(8,128)(2,1)} %constant_dynamic-slice_fusion.1), channel_id=1, source_target_pairs={{0,2},{2,0},{4,6},{6,4},{8,10},{10,8},{12,14},{14,12},{16,18},{18,... | collective-permute-start | bytes 1966088 | tf_op jit(solution)/shard_map/ppermute | solution.py:500
  231.0 37.3 %collective-permute-start.18 = (bf16[32,5120]{1,0:T(8,128)(2,1)S(1)}, bf16[32,5120]{1,0:T(8,128)(2,1)S(1)}, u32[]{:S(2)}, u32[]{:S(2)}) collective-permute-start(bf16[32,5120]{1,0:T(8,128)(2,1)S(1)} %get-tuple-element.155), channel_id=1, source_target_pairs={{0,16},{2,18},{4,20},{6,22},{8,24},{10,26},{12,28},{14,30},{16,0},... | collective-permute-start | bytes 983048 | tf_op jit(solution)/shard_map/ppermute | solution.py:513
  232.0 36.2 %collective-permute-start.19 = (bf16[32,5120]{1,0:T(8,128)(2,1)S(1)}, bf16[32,5120]{1,0:T(8,128)(2,1)S(1)}, u32[]{:S(2)}, u32[]{:S(2)}) collective-permute-start(bf16[32,5120]{1,0:T(8,128)(2,1)S(1)} %get-tuple-element.156), channel_id=1, source_target_pairs={{0,24},{2,26},{4,28},{6,30},{8,0},{10,2},{12,4},{14,6},{16,8},{18,... | collective-permute-start | bytes 983048 | tf_op jit(solution)/shard_map/ppermute | solution.py:513
  243.6 30.6 %collective-permute-start.25 = (bf16[224,512]{1,0:T(8,128)(2,1)S(1)}, bf16[224,512]{1,0:T(8,128)(2,1)S(1)}, u32[]{:S(2)}, u32[]{:S(2)}) collective-permute-start(bf16[224,512]{1,0:T(8,128)(2,1)S(1)} %pad_maximum_fusion.13), channel_id=1, source_target_pairs={{0,24},{2,26},{4,28},{6,30},{8,0},{10,2},{12,4},{14,6},{16,8},{18,... | collective-permute-start | bytes 688136 | tf_op jit(solution)/shard_map/ppermute | solution.py:513
  268.5 32.7 %collective-permute-start.21 = (bf16[32,5120]{1,0:T(8,128)(2,1)S(1)}, bf16[32,5120]{1,0:T(8,128)(2,1)S(1)}, u32[]{:S(2)}, u32[]{:S(2)}) collective-permute-start(bf16[32,5120]{1,0:T(8,128)(2,1)S(1)} %add_convert_fusion.3), channel_id=1, source_target_pairs={{0,16},{2,18},{4,20},{6,22},{8,24},{10,26},{12,28},{14,30},{16,0},... | collective-permute-start | bytes 983048 | tf_op jit(solution)/shard_map/ppermute | solution.py:513
  272.0 33.0 %collective-permute-start.22 = (bf16[32,5120]{1,0:T(8,128)(2,1)S(1)}, bf16[32,5120]{1,0:T(8,128)(2,1)S(1)}, u32[]{:S(2)}, u32[]{:S(2)}) collective-permute-start(bf16[32,5120]{1,0:T(8,128)(2,1)S(1)} %add_convert_fusion.3), channel_id=1, source_target_pairs={{0,24},{2,26},{4,28},{6,30},{8,0},{10,2},{12,4},{14,6},{16,8},{18,... | collective-permute-start | bytes 983048 | tf_op jit(solution)/shard_map/ppermute | solution.py:513
  305.2 32.2 %collective-permute-start.26 = (bf16[128,2560]{1,0:T(8,128)(2,1)S(1)}, bf16[128,2560]{1,0:T(8,128)(2,1)S(1)}, u32[]{:S(2)}, u32[]{:S(2)}) collective-permute-start(bf16[128,2560]{1,0:T(8,128)(2,1)S(1)} %get-tuple-element.153), channel_id=1, source_target_pairs={{0,4},{2,6},{4,0},{6,2},{8,12},{10,14},{12,8},{14,10},{16,20},{18,... | collective-permute-start | bytes 1966088 | tf_op jit(solution)/shard_map/ppermute | solution.py:500
  305.2 32.1 %collective-permute-start.27 = (bf16[128,2560]{1,0:T(8,128)(2,1)S(1)}, bf16[128,2560]{1,0:T(8,128)(2,1)S(1)}, u32[]{:S(2)}, u32[]{:S(2)}) collective-permute-start(bf16[128,2560]{1,0:T(8,128)(2,1)S(1)} %get-tuple-element.152), channel_id=1, source_target_pairs={{0,2},{2,0},{4,6},{6,4},{8,10},{10,8},{12,14},{14,12},{16,18},{18,... | collective-permute-start | bytes 1966088 | tf_op jit(solution)/shard_map/ppermute | solution.py:500
  308.6 28.8 %collective-permute-start.28 = (bf16[896,256]{1,0:T(8,128)(2,1)S(1)}, bf16[896,256]{1,0:T(8,128)(2,1)S(1)}, u32[]{:S(2)}, u32[]{:S(2)}) collective-permute-start(bf16[896,256]{1,0:T(8,128)(2,1)S(1)} %get-tuple-element.104), channel_id=1, source_target_pairs={{0,2},{2,0},{4,6},{6,4},{8,10},{10,8},{12,14},{14,12},{16,18},{18,... | collective-permute-start | bytes 1376264 | tf_op jit(solution)/shard_map/ppermute | solution.py:500
  308.7 28.7 %collective-permute-start.29 = (bf16[896,256]{1,0:T(8,128)(2,1)S(1)}, bf16[896,256]{1,0:T(8,128)(2,1)S(1)}, u32[]{:S(2)}, u32[]{:S(2)}) collective-permute-start(bf16[896,256]{1,0:T(8,128)(2,1)S(1)} %get-tuple-element.106), channel_id=1, source_target_pairs={{0,4},{2,6},{4,0},{6,2},{8,12},{10,14},{12,8},{14,10},{16,20},{18,... | collective-permute-start | bytes 1376264 | tf_op jit(solution)/shard_map/ppermute | solution.py:500
  337.4 29.4 %collective-permute-start.33 = (bf16[1792,256]{1,0:T(8,128)(2,1)S(1)}, bf16[1792,256]{1,0:T(8,128)(2,1)S(1)}, u32[]{:S(2)}, u32[]{:S(2)}) collective-permute-start(bf16[1792,256]{1,0:T(8,128)(2,1)S(1)} %pad_maximum_fusion.7), channel_id=1, source_target_pairs={{0,2},{2,0},{4,6},{6,4},{8,10},{10,8},{12,14},{14,12},{16,18},{18,... | collective-permute-start | bytes 2752520 | tf_op jit(solution)/shard_map/ppermute | solution.py:500
  338.2 28.7 %collective-permute-start.32 = (bf16[1792,256]{1,0:T(8,128)(2,1)S(1)}, bf16[1792,256]{1,0:T(8,128)(2,1)S(1)}, u32[]{:S(2)}, u32[]{:S(2)}) collective-permute-start(bf16[1792,256]{1,0:T(8,128)(2,1)S(1)} %pad_maximum_fusion.6), channel_id=1, source_target_pairs={{0,4},{2,6},{4,0},{6,2},{8,12},{10,14},{12,8},{14,10},{16,20},{18,... | collective-permute-start | bytes 2752520 | tf_op jit(solution)/shard_map/ppermute | solution.py:500
  339.4 54.2 %collective-permute-start.31 = (bf16[256,2560]{1,0:T(8,128)(2,1)S(1)}, bf16[256,2560]{1,0:T(8,128)(2,1)}, u32[]{:S(2)}, u32[]{:S(2)}) collective-permute-start(bf16[256,2560]{1,0:T(8,128)(2,1)S(1)} %pad_maximum_fusion.5), channel_id=1, source_target_pairs={{0,4},{2,6},{4,0},{6,2},{8,12},{10,14},{12,8},{14,10},{16,20},{18,... | collective-permute-start | bytes 3932168 | tf_op jit(solution)/shard_map/ppermute | solution.py:500
  340.6 54.1 %collective-permute-start.30 = (bf16[256,2560]{1,0:T(8,128)(2,1)S(1)}, bf16[256,2560]{1,0:T(8,128)(2,1)}, u32[]{:S(2)}, u32[]{:S(2)}) collective-permute-start(bf16[256,2560]{1,0:T(8,128)(2,1)S(1)} %pad_maximum_fusion.4), channel_id=1, source_target_pairs={{0,2},{2,0},{4,6},{6,4},{8,10},{10,8},{12,14},{14,12},{16,18},{18,... | collective-permute-start | bytes 3932168 | tf_op jit(solution)/shard_map/ppermute | solution.py:500
  (39 other events, 229.3 us)
Sparse Core Ops, SparseCore 0:
  32.0 81.0 all-gather.2
  146.7 225.3 all-reduce.5
